TPU v7x, 32 devices: a whole 2x2x4 slice. The times are simulated.
32 devices in a mesh: ctx: 16 (over z, y, x), head: 2 (over core).
Axes of the slice: x: 2, y: 2, z: 4, core: 2. Of those that a mesh axis runs over, the one named last changes fastest.
Arguments:
- tokens: bfloat16 [4096, 3072], P('ctx'), may hold values from -6 to 6
- w_query: bfloat16 [3072, 4096], P('ctx', 'head'), may hold values from -0.109375 to 0.109375
- w_key: bfloat16 [3072, 4096], P('ctx', 'head'), may hold values from -0.109375 to 0.109375
- w_value: bfloat16 [3072, 4096], P('ctx', 'head'), may hold values from -0.109375 to 0.109375
- log_decay: float32 [32, 4096], P('head', 'ctx'), may hold values from -1 to 0
- norm_gain: float32 [4096], P('head'), may hold values from 0.25 to 1.75
- w_out: bfloat16 [4096, 3072], P('head', 'ctx'), may hold values from -0.09375 to 0.09375
Outputs:
- layer_out: bfloat16 [4096, 3072], P('ctx', 'head')
All inputs are finite; a program needn't handle non-finite values.
Results may differ from a plain program's by a relative error of at most 0.014.
Values may be sent and summed in bfloat16 or wider, within the bound.
No kernel may reach another device: no remote copies, remote signals or barrier semaphores. Data moves between devices by JAX's collectives and lax.ppermute only.
A program may use at most 128 MiB of HBM per device.

v0:
```python
import functools
import math

import jax
import jax.numpy as jnp
from jax import lax
from jax.experimental import pallas as pl
from jax.experimental.pallas import tpu as pltpu
from jax.sharding import PartitionSpec as P


F32 = jnp.float32
BF16 = jnp.bfloat16


def silu(x):
    return x / (1.0 + jnp.exp(-x))


def block_state(k, v, cum_t, heads, head_dim):
    rows = k.shape[0]
    out = []
    for i in range(heads):
        cols = slice(i * head_dim, (i + 1) * head_dim)
        cum = cum_t[:, i : i + 1]
        last = cum_t[rows - 1 : rows, i : i + 1]
        decayed = (k[:, cols].astype(F32) * jnp.exp(last - cum)).astype(BF16)
        out.append(
            lax.dot_general(
                decayed, v[:, cols], (((0,), (0,)), ((), ())), preferred_element_type=F32
            )
        )
    return out


def state_body(where, k_ref, v_ref, cum_t_ref, out_ref, *, heads, head_dim):
    for i, s in enumerate(block_state(k_ref[0], v_ref[0], cum_t_ref[0], heads, head_dim)):
        out_ref[0, i] = s


def block_states(block_at, k, v, cum_t, heads, head_dim):
    count, rows, width = k.shape
    here = lambda i, w: (i, 0, 0)
    return pl.pallas_call(
        functools.partial(state_body, heads=heads, head_dim=head_dim),
        grid_spec=pltpu.PrefetchScalarGridSpec(
            num_scalar_prefetch=1,
            grid=(count,),
            in_specs=[
                pl.BlockSpec((1, rows, width), here),
                pl.BlockSpec((1, rows, width), here),
                pl.BlockSpec((1, rows, heads), lambda i, w: (w[i], 0, 0)),
            ],
            out_specs=pl.BlockSpec(
                (1, heads, head_dim, head_dim), lambda i, w: (i, 0, 0, 0)
            ),
        ),
        out_shape=jax.ShapeDtypeStruct((count, heads, head_dim, head_dim), F32),
        name="block_states",
    )(block_at, k, v, cum_t)


def halves(step, refs):
    pair, got, pair_other, got_other = refs
    own = lambda: jnp.where(step < 2, pair[0], got[0])
    other = lambda: jnp.where(step % 2 == 0, pair_other[0], got_other[0])
    return own, other


def family_specs(rows, share):
    return [
        pl.BlockSpec((1, rows, share), lambda i, w: (jnp.minimum(i, 1), 0, 0)),
        pl.BlockSpec((1, rows, share), lambda i, w: (jnp.maximum(i - 2, 0), 0, 0)),
        pl.BlockSpec((1, rows, share), lambda i, w: (i // 2, 0, 0)),
        pl.BlockSpec((1, rows, share), lambda i, w: (i // 2, 0, 0)),
    ]


def product(tokens, weight_ref, first, second):
    cut = weight_ref.shape[1]
    return jnp.dot(
        tokens[:, :cut], weight_ref[first], preferred_element_type=F32
    ) + jnp.dot(tokens[:, cut:], weight_ref[second], preferred_element_type=F32)


def keys_values_body(
    where, pair, got, pair_other, got_other, wk_ref, wv_ref, cum_t_ref, k_ref, v_ref, state_ref,
    *, heads, head_dim,
):
    own, other = (x() for x in halves(pl.program_id(0), (pair, got, pair_other, got_other)))
    mine, swap = where[4], where[5]
    at = lambda side, i: 2 * side + (i ^ swap)
    full = lambda w: product(own, w, at(mine, 0), at(mine, 1)) + product(
        other, w, at(1 - mine, 0), at(1 - mine, 1)
    )
    k = silu(full(wk_ref)).astype(BF16)
    v = full(wv_ref).astype(BF16)
    k_ref[0] = k
    v_ref[0] = v
    for i, s in enumerate(block_state(k, v, cum_t_ref[0], heads, head_dim)):
        state_ref[0, i] = s


def keys_values(table, family, wk, wv, cum_t, heads, head_dim):
    _, rows, share = family[0].shape
    width = wk.shape[2]
    whole = lambda i, w: (0, 0, 0)
    here = lambda i, w: (i, 0, 0)
    return pl.pallas_call(
        functools.partial(keys_values_body, heads=heads, head_dim=head_dim),
        grid_spec=pltpu.PrefetchScalarGridSpec(
            num_scalar_prefetch=1,
            grid=(4,),
            in_specs=family_specs(rows, share)
            + [
                pl.BlockSpec(wk.shape, whole),
                pl.BlockSpec(wv.shape, whole),
                pl.BlockSpec((1, rows, heads), lambda i, w: (w[i], 0, 0)),
            ],
            out_specs=[
                pl.BlockSpec((1, rows, width), here),
                pl.BlockSpec((1, rows, width), here),
                pl.BlockSpec((1, heads, head_dim, head_dim), lambda i, w: (i, 0, 0, 0)),
            ],
        ),
        out_shape=[
            jax.ShapeDtypeStruct((4, rows, width), BF16),
            jax.ShapeDtypeStruct((4, rows, width), BF16),
            jax.ShapeDtypeStruct((4, heads, head_dim, head_dim), F32),
        ],
    )(table, *family, wk, wv, cum_t)


def query_body(where, *refs, late):
    tokens, (w_ref, *rest) = refs[:8], refs[8:]
    step = pl.program_id(0)
    mine, swap = where[0], where[1]
    use_own = (mine == 1) if late else (mine == 0)
    for f in range(2):
        own, other = halves(step % 4, tokens[4 * f : 4 * f + 4])

        @pl.when(step // 4 == f)
        def _():
            for flag, side in ((use_own, own), (jnp.logical_not(use_own), other)):

                @pl.when(flag)
                def _():
                    part = product(side(), w_ref, swap, 1 ^ swap)
                    if late:
                        rest[1][0] = silu(rest[0][0] + part).astype(BF16)
                    else:
                        rest[0][0] = part


def query_part(table, near, far, weight, early):
    _, rows, share = near[0].shape
    width = weight.shape[2]
    late = early is not None
    here = lambda i, w: (i, 0, 0)

    def moved(spec, f):
        inner = spec.index_map
        return pl.BlockSpec(
            spec.block_shape,
            (lambda i, w: inner(jnp.minimum(i, 3), w)) if f == 0 else (
                lambda i, w: inner(jnp.maximum(i - 4, 0), w)
            ),
        )

    specs = [moved(s, f) for f in range(2) for s in family_specs(rows, share)]
    specs.append(pl.BlockSpec(weight.shape, lambda i, w: (0, 0, 0)))
    args = [*near, *far, weight]
    if late:
        specs.append(pl.BlockSpec((1, rows, width), here))
        args.append(early)
    return pl.pallas_call(
        functools.partial(query_body, late=late),
        grid_spec=pltpu.PrefetchScalarGridSpec(
            num_scalar_prefetch=1,
            grid=(8,),
            in_specs=specs,
            out_specs=pl.BlockSpec((1, rows, width), here),
        ),
        out_shape=jax.ShapeDtypeStruct((8, rows, width), BF16 if late else F32),
    )(table, *args)


def mix_body(
    pos, q_ref, k_ref, v_ref, cum_ref, cum_t_ref, state_ref, group_ref, gain_ref, out_ref, carry_ref,
    *, heads, head_dim,
):
    @pl.when(pl.program_id(0) == 0)
    def _():
        carry_ref[...] = group_ref[...]

    rows = q_ref.shape[1]
    causal = lax.broadcasted_iota(jnp.int32, (rows, rows), 0) >= lax.broadcasted_iota(
        jnp.int32, (rows, rows), 1
    )
    for i in range(heads):
        cols = slice(i * head_dim, (i + 1) * head_dim)
        q, k, v = q_ref[0, :, cols], k_ref[0, :, cols], v_ref[0, :, cols]
        cum = cum_t_ref[0, :, i : i + 1]
        last = cum_t_ref[0, rows - 1 : rows, i : i + 1]
        diff = cum - cum_ref[0, i : i + 1, :]
        decay = jnp.where(causal, jnp.exp(jnp.where(causal, diff, 0.0)), 0.0)
        scores = lax.dot_general(q, k, (((1,), (1,)), ((), ())), preferred_element_type=F32)
        weights = (scores * decay).astype(BF16)
        intra = jnp.dot(weights, v, preferred_element_type=F32)
        state = carry_ref[i]
        carry_ref[i] = jnp.exp(last) * state + state_ref[0, i]
        high = state.astype(BF16)
        low = (state - high.astype(F32)).astype(BF16)
        inter = jnp.dot(q, high, preferred_element_type=F32) + jnp.dot(
            q, low, preferred_element_type=F32
        )
        mixed = intra + jnp.exp(cum) * inter
        scale = lax.rsqrt(jnp.mean(mixed * mixed, axis=-1, keepdims=True) + 1e-06)
        out_ref[0, :, cols] = (mixed * scale * gain_ref[:, cols]).astype(BF16)


def mix(pos, q, k, v, cum, cum_t, states, group, gain, heads, head_dim):
    count, rows, width = k.shape
    at = lambda b, p: (p[b], 0, 0)
    plain = lambda b, p: (b, 0, 0)
    return pl.pallas_call(
        functools.partial(mix_body, heads=heads, head_dim=head_dim),
        grid_spec=pltpu.PrefetchScalarGridSpec(
            num_scalar_prefetch=1,
            grid=(count,),
            in_specs=[
                pl.BlockSpec((1, rows, width), at),
                pl.BlockSpec((1, rows, width), at),
                pl.BlockSpec((1, rows, width), at),
                pl.BlockSpec((1, heads, rows), plain),
                pl.BlockSpec((1, rows, heads), plain),
                pl.BlockSpec((1, heads, head_dim, head_dim), lambda b, p: (p[b], 0, 0, 0)),
                pl.BlockSpec((heads, head_dim, head_dim), lambda b, p: (0, 0, 0)),
                pl.BlockSpec((1, width), lambda b, p: (0, 0)),
            ],
            out_specs=pl.BlockSpec((1, rows, width), lambda b, p: (p[count + b], 0, 0)),
            scratch_shapes=[pltpu.VMEM((heads, head_dim, head_dim), F32)],
        ),
        out_shape=jax.ShapeDtypeStruct((count, rows, width), BF16),
        name="mix",
    )(pos, q, k, v, cum, cum_t, states, group, gain)


def per_device(tokens, w_query, w_key, w_value, log_decay, norm_gain, w_out, *, n, nh):
    rows, model = tokens.shape
    heads_here = log_decay.shape[0]
    head_dim = w_query.shape[1] // heads_here
    g = math.gcd(heads_here, max(n // 2, 1))
    ng = n // g
    heads = heads_here // g
    width = heads * head_dim
    c = lax.axis_index("ctx")
    h = lax.axis_index("head")
    member = c % g
    group = c // g
    bits = [1 << i for i in range(g.bit_length() - 1)][::-1]
    cube = len(bits) == 3 and ng == 2 and nh == 2
    orders = (bits[:1] + bits[1:][::-1], bits)
    plane = g // 2 if cube else g
    part = (member % plane) * (g // plane) + member // plane

    def exchange(value, where):
        pairs = []
        for a in range(n):
            for b in range(nh):
                to = where(a, b)
                if to is not None:
                    pairs.append((a * nh + b, to[0] * nh + to[1]))
        return lax.ppermute(value, ("ctx", "head"), pairs)

    def spread(value, split, concat, size):
        groups = [[a * size + b for b in range(size)] for a in range(n // size)]
        return lax.all_to_all(
            value, "ctx", split, concat, axis_index_groups=groups, tiled=True
        )

    def over_groups(piece):
        pieces = [piece]
        step = 1
        while step < ng:
            pieces += [exchange(p, lambda a, b: (a ^ (step * g), b)) for p in pieces]
            step *= 2
        return pieces

    def over_planes(piece):
        odd = (c // plane) % 2 == 1
        same = jnp.where(odd, piece[1], piece[0])
        cross = jnp.where(odd, piece[0], piece[1])
        move = lambda x, r: exchange(x, lambda a, b: (a ^ (r * plane), b))
        return [same, move(cross, 1), move(same, 2), move(cross, 3)]

    def true_order(pieces, index):
        if len(pieces) == 1:
            return pieces
        half = len(pieces) // 2
        low, high = true_order(pieces[:half], index), true_order(pieces[half:], index)
        upper = (index & half) != 0
        return [jnp.where(upper, b, a) for a, b in zip(low, high)] + [
            jnp.where(upper, a, b) for a, b in zip(low, high)
        ]

    levels = g // plane
    cumul = jnp.cumsum(log_decay, axis=1).reshape(plane, levels, heads * rows)
    cumul = cumul.transpose(1, 0, 2).reshape(g, heads * rows)
    cumul = spread(cumul, 0, 0, g).reshape(g, heads, rows)
    cum_t = cumul.transpose(0, 2, 1)
    last = cumul[:, :, -1]

    apart = jnp.arange(g, dtype=jnp.int32) ^ member.astype(jnp.int32)

    def place(order):
        out = jnp.zeros_like(apart)
        for i, bit in enumerate(order[::-1]):
            out = out + jnp.where((apart & bit) != 0, 1 << i, 0)
        return out

    def masks(order):
        spots = jnp.arange(g, dtype=jnp.int32)
        out = jnp.zeros_like(spots)
        for i, bit in enumerate(order[::-1]):
            out = out + jnp.where((spots & (1 << i)) != 0, bit, 0)
        return out

    share = model // nh
    own = lax.dynamic_slice_in_dim(tokens, h * share, share, axis=1)[None]
    step_to = lambda stage: (lambda a, b: (a ^ orders[b & 1][stage], b))
    if cube:
        axes = bits
        received = [[bits[0]] + o[1:][::-1] for o in orders]
        odd = (h & 1) == 1
        pos = jnp.where(odd, place(received[1]), place(received[0]))
        block_at = jnp.where(odd, masks(received[1]), masks(received[0])) ^ member
        pos = jnp.concatenate([pos, place(axes)])
        families = []
        for one in (own, exchange(own, step_to(0))):
            two = exchange(one, step_to(1))
            pair = jnp.concatenate([one, two])
            families.append([pair, exchange(pair, step_to(2))])
        families = [f + [exchange(x, lambda a, b: (a, b ^ 1)) for x in f] for f in families]

        def rows_of(weight):
            moved = spread(weight, 1, 0, plane)
            return over_planes([moved[:, :width], moved[:, width:]])

        stack = lambda pieces: jnp.stack(pieces)
        wk, wv, wq = rows_of(w_key), rows_of(w_value), rows_of(w_query)
        turn = jnp.stack([h ^ group, (c // plane) % 2]).astype(jnp.int32)
        wk, wv = stack(wk), stack(wv)
        parts = [
            keys_values(
                jnp.concatenate([block_at[4 * i : 4 * i + 4], turn]), family, wk, wv, cum_t,
                heads, head_dim,
            )
            for i, family in enumerate(families)
        ]
        keys, values, states = (jnp.concatenate(x) for x in zip(*parts))
        early = query_part(turn, *families, stack(wq[:2]), None)
        queries = query_part(turn, *families, stack(wq[2:]), early)
    else:
        axes = orders[0][::-1]
        pos = place(axes)
        block_at = masks(axes) ^ member
        pos = jnp.concatenate([pos, pos])
        for stage in range(len(bits)):
            got = exchange(own, lambda a, b: (a ^ orders[0][stage], b))
            own = jnp.concatenate([own, got], axis=0)
        shares = [own]
        step = 1
        while step < nh:
            shares += [exchange(s, lambda a, b: (a, b ^ step)) for s in shares]
            step *= 2
        full = jnp.concatenate(true_order(shares, h), axis=-1).reshape(g * rows, model)

        def project(weight, act):
            pieces = over_groups(spread(weight, 1, 0, g))
            whole = jnp.concatenate(true_order(pieces, group), axis=0)
            out = act(jnp.dot(full, whole, preferred_element_type=F32)).astype(BF16)
            return out.reshape(g, rows, width)

        keys, values = project(w_key, silu), project(w_value, lambda raw: raw)
        queries = project(w_query, silu)
        states = block_states(block_at, keys, values, cum_t, heads, head_dim)

    through = jnp.cumsum(last, axis=0)
    left = jnp.exp(through[-1] - through)[block_at]
    total = jnp.sum(left[:, :, None, None] * states, axis=0)
    keep = jnp.exp(through[-1])
    later = lambda by: (lambda a, b: (a + by * g, b) if a + by * g < n else None)
    entering = exchange(total, later(1))
    step = 1
    if ng > 2:
        keep = exchange(keep, later(1))
    while step < ng - 1:
        entering = entering + keep[:, None, None] * exchange(entering, later(step))
        keep = keep * exchange(keep, later(step))
        step *= 2

    gain = lax.dynamic_slice_in_dim(norm_gain, part * width, width)[None]
    normed = mix(
        pos, queries, keys, values, cumul, cum_t, states, entering, gain, heads, head_dim
    ).reshape(g * rows, width)
    sides = [normed] + [exchange(normed, lambda a, b: (a, b ^ p)) for p in range(1, nh)]

    out_cols = model // nh
    if cube:
        by_plane = spread(w_out.reshape(plane, levels, width, -1), 0, 0, plane)
        local = by_plane.transpose(1, 2, 0, 3).reshape(levels, width, -1)
        pieces = over_planes(local)
        mine = []
        for p in range(nh):
            side = h ^ p ^ group
            first = jnp.where(side == 0, pieces[0], pieces[2])
            second = jnp.where(side == 0, pieces[1], pieces[3])
            swap = (c // plane) % 2 == 1
            mine.append(
                jnp.concatenate(
                    [jnp.where(swap, second, first), jnp.where(swap, first, second)], axis=1
                )
            )
    else:
        local = spread(w_out.reshape(g, width, -1), 0, 0, g)
        local = local.transpose(1, 0, 2).reshape(width, -1)
        whole = jnp.concatenate(true_order(over_groups(local), group), axis=1)
        whole = whole.reshape(width, nh, out_cols).transpose(1, 0, 2)
        mine = [lax.dynamic_index_in_dim(whole, h ^ p, 0, False) for p in range(nh)]
    right = mine[:1] + [exchange(m, lambda a, b: (a, b ^ (p + 1))) for p, m in enumerate(mine[1:])]
    partial = sum(
        jnp.dot(t, w, preferred_element_type=F32) for t, w in zip(sides, right)
    ).astype(BF16)

    chunks = max(len(bits), 1)
    span = out_cols // chunks
    summed = []
    for j in range(chunks):
        piece = partial[:, j * span : (j + 1) * span].reshape((2,) * len(bits) + (rows, -1))
        left_bits = list(axes)
        for bit in bits[j:] + bits[:j]:
            axis = left_bits.index(bit)
            left_bits.pop(axis)
            kept = lax.index_in_dim(piece, 0, axis, False)
            sent = lax.index_in_dim(piece, 1, axis, False)
            got = exchange(sent, lambda a, b: (a ^ bit, b))
            piece = (kept.astype(F32) + got.astype(F32)).astype(BF16)
        summed.append(piece)
    return jnp.concatenate(summed, axis=1)


def solution(mesh):
    placed = (
        P("ctx", None),
        P("ctx", "head"),
        P("ctx", "head"),
        P("ctx", "head"),
        P("head", "ctx"),
        P("head"),
        P("head", "ctx"),
    )
    body = functools.partial(per_device, n=mesh.shape["ctx"], nh=mesh.shape["head"])

    return jax.shard_map(
        body, mesh=mesh, in_specs=placed, out_specs=P("ctx", "head"), check_vma=False
    )
```

profile of v0, /device:TPU:0, one launch (start us, length us, event | category | flops | bytes accessed | tf_op | source)
XLA Modules:
  0.0 296.0 jit_solution(13975750249001087713)
XLA Ops:
  0.0 1.4 copy-done
  1.5 3.1 %collective-permute-start.4 = (bf16[1,256,1536]{2,1,0:T(8,128)(2,1)S(1)}, bf16[1,256,1536]{2,1,0:T(8,128)(2,1)}, u32[]{:S(2)}, u32[]{:S(2)}) collective-permute-start(bf16[1,256,1536]{2,1,0:T(8,128)(2,1)S(1)} %dynamic-slice_bitcast_fusion), channel_id=1, source_target_pairs={{0,8},{1,9},{2,10},{3,11},{4,12},{5,13},{6,14},{7,15},{8,0},{9,1},... | collective-permute-start | bytes 2359304 | tf_op jit(solution)/shard_map/ppermute | solution.py:274
  4.6 1.5 collective-permute-start
  7.0 4.2 %all-to-all-start = ((bf16[192,4,512]{2,0,1:T(8,128)(2,1)}), bf16[192,4,512]{2,0,1:T(8,128)(2,1)}, u32[]{:S(2)}, u32[]{:S(2)}) async-start(bf16[192,4,512]{2,0,1:T(8,128)(2,1)} %bitcast.129), calls=%async_computation | async-start | bytes 1572864 | tf_op jit(solution)/shard_map/all_to_all | solution.py:278
  12.0 10.2 %collective-permute-done.4 = bf16[1,256,1536]{2,1,0:T(8,128)(2,1)} collective-permute-done((bf16[1,256,1536]{2,1,0:T(8,128)(2,1)S(1)}, bf16[1,256,1536]{2,1,0:T(8,128)(2,1)}, u32[]{:S(2)}, u32[]{:S(2)}) %collective-permute-start.4) | collective-permute-done | bytes 786464 | tf_op jit(solution)/shard_map/ppermute | solution.py:274
  22.2 1.7 collective-permute-start.5
  24.5 1.3 pad_maximum_fusion.refs_0_.pair
  25.8 1.6 collective-permute-start.1
  28.6 13.1 %collective-permute-done.5 = bf16[1,256,1536]{2,1,0:T(8,128)(2,1)} collective-permute-done((bf16[1,256,1536]{2,1,0:T(8,128)(2,1)}, bf16[1,256,1536]{2,1,0:T(8,128)(2,1)}, u32[]{:S(2)}, u32[]{:S(2)}) %collective-permute-start.5) | collective-permute-done | bytes 786464 | tf_op jit(solution)/shard_map/ppermute | solution.py:274
  41.7 1.2 constant_dynamic-update-slice_fusion.refs_4_.pair
  42.9 2.8 collective-permute-start.6
  46.3 2.1 copy.82
  48.4 4.2 %all-to-all-start.1 = ((bf16[192,4,512]{2,0,1:T(8,128)(2,1)}), bf16[192,4,512]{2,0,1:T(8,128)(2,1)}, u32[]{:S(2)}, u32[]{:S(2)}) async-start(bf16[192,4,512]{2,0,1:T(8,128)(2,1)} %bitcast.141), calls=%async_computation.1 | async-start | bytes 1572864 | tf_op jit(solution)/shard_map/all_to_all | solution.py:278
  53.2 2.1 broadcast_select_fusion.15
  55.3 3.7 %collective-permute-start.10 = (bf16[768,256]{1,0:T(8,128)(2,1)}, bf16[768,256]{1,0:T(8,128)(2,1)}, u32[]{:S(2)}, u32[]{:S(2)}) collective-permute-start(bf16[768,256]{1,0:T(8,128)(2,1)} %get-tuple-element.34), channel_id=1, source_target_pairs={{0,24},{1,25},{2,26},{3,27},{4,28},{5,29},{6,30},{7,31},{8,16},{9,... | collective-permute-start | bytes 1179656 | tf_op jit(solution)/shard_map/ppermute | solution.py:274
  59.5 2.1 copy.81
  62.9 11.0 %all-to-all-done.1 = bf16[192,4,512]{2,0,1:T(8,128)(2,1)} async-done(((bf16[192,4,512]{2,0,1:T(8,128)(2,1)}), bf16[192,4,512]{2,0,1:T(8,128)(2,1)}, u32[]{:S(2)}, u32[]{:S(2)}) %all-to-all-start.1) | async-done | bytes 786464 | tf_op jit(solution)/shard_map/all_to_all | solution.py:278
  73.9 4.2 %all-to-all-start.2 = ((bf16[192,4,512]{2,0,1:T(8,128)(2,1)}), bf16[192,4,512]{2,0,1:T(8,128)(2,1)}, u32[]{:S(2)}, u32[]{:S(2)}) async-start(bf16[192,4,512]{2,0,1:T(8,128)(2,1)} %bitcast.140), calls=%async_computation.2 | async-start | bytes 1572864 | tf_op jit(solution)/shard_map/all_to_all | solution.py:278
  78.1 1.9 broadcast_select_fusion.13
  80.0 3.1 %collective-permute-start.14 = (bf16[768,256]{1,0:T(8,128)(2,1)}, bf16[768,256]{1,0:T(8,128)(2,1)}, u32[]{:S(2)}, u32[]{:S(2)}) collective-permute-start(bf16[768,256]{1,0:T(8,128)(2,1)} %get-tuple-element.32), channel_id=1, source_target_pairs={{0,24},{1,25},{2,26},{3,27},{4,28},{5,29},{6,30},{7,31},{8,16},{9,... | collective-permute-start | bytes 1179656 | tf_op jit(solution)/shard_map/ppermute | solution.py:274
  83.7 15.9 %collective-permute-done.9 = bf16[768,256]{1,0:T(8,128)(2,1)} collective-permute-done((bf16[768,256]{1,0:T(8,128)(2,1)}, bf16[768,256]{1,0:T(8,128)(2,1)}, u32[]{:S(2)}, u32[]{:S(2)}) %collective-permute-start.9) | collective-permute-done | bytes 393248 | tf_op jit(solution)/shard_map/ppermute | solution.py:274
  99.6 1.7 collective-permute-start.13
  103.9 1.3 all_to_all.66
  105.3 3.2 %reshape.148 = bf16[4,2,256,192]{2,1,0,3:T(2,128)(2,1)} reshape(bf16[2048,192]{0,1:T(8,128)(2,1)} %param.13) | data formatting | bytes 1572864 | tf_op jit(solution)/shard_map/reshape | solution.py:411
  108.5 2.6 copy.57
  111.7 4.1 %all-to-all-start.3 = ((f32[8,1,512]{2,1,0:T(1,128)}), f32[8,1,512]{2,1,0:T(1,128)S(1)}, u32[]{:S(2)}, u32[]{:S(2)}) async-start(f32[8,1,512]{2,1,0:T(1,128)} %all_to_all.66), calls=%async_computation.3 | async-start | bytes 32768 | tf_op jit(solution)/shard_map/all_to_all | solution.py:278
  116.3 2.0 broadcast_select_fusion.11
  118.4 3.6 %all-to-all-done.3 = f32[8,1,512]{2,1,0:T(1,128)S(1)} async-done(((f32[8,1,512]{2,1,0:T(1,128)}), f32[8,1,512]{2,1,0:T(1,128)S(1)}, u32[]{:S(2)}, u32[]{:S(2)}) %all-to-all-start.3) | async-done | bytes 16416 | tf_op jit(solution)/shard_map/all_to_all | solution.py:278
  122.0 4.2 %all-to-all-start.4 = ((bf16[4,2,256,192]{2,1,3,0:T(2,128)(2,1)}), bf16[4,2,256,192]{2,1,3,0:T(2,128)(2,1)}, u32[]{:S(2)}, u32[]{:S(2)}) async-start(bf16[4,2,256,192]{2,1,3,0:T(2,128)(2,1)} %copy.57), calls=%async_computation.4 | async-start | bytes 1572864 | tf_op jit(solution)/shard_map/all_to_all | solution.py:278
  126.2 2.5 collective-permute-start.17
  129.2 1.2 pad_add_fusion.pos
  130.4 1.3 dynamic_slice.7
  131.8 1.2 pad_clamp_fusion
  134.3 1.4 copy.54
  136.4 1.3 copy.55
  137.7 1.3 copy.56
  139.1 1.3 reduce_window_sum.28
  141.0 3.9 %collective-permute-start.16 = (bf16[768,256]{1,0:T(8,128)(2,1)}, bf16[768,256]{1,0:T(8,128)(2,1)}, u32[]{:S(2)}, u32[]{:S(2)}) collective-permute-start(bf16[768,256]{1,0:T(8,128)(2,1)} %get-tuple-element.29), channel_id=1, source_target_pairs={{0,16},{1,17},{2,18},{3,19},{4,20},{5,21},{6,22},{7,23},{8,24},{9,... | collective-permute-start | bytes 1179656 | tf_op jit(solution)/shard_map/ppermute | solution.py:274
  146.3 1.3 copy.84
  148.6 13.2 %collective-permute-done.16 = bf16[768,256]{1,0:T(8,128)(2,1)} collective-permute-done((bf16[768,256]{1,0:T(8,128)(2,1)}, bf16[768,256]{1,0:T(8,128)(2,1)}, u32[]{:S(2)}, u32[]{:S(2)}) %collective-permute-start.16) | collective-permute-done | bytes 393248 | tf_op jit(solution)/shard_map/ppermute | solution.py:274
  161.8 2.1 pad_maximum_fusion.5.refs_8_
  163.8 2.1 pad_maximum_fusion.6.refs_8_
  165.9 2.6 pad_maximum_fusion.1.wk_ref
  168.6 2.4 collective-permute-done.15
  172.2 2.5 pad_maximum_fusion.2.wv_ref
  174.7 3.1 %collective-permute-start.20 = (bf16[256,768]{0,1:T(8,128)(2,1)}, bf16[256,768]{0,1:T(8,128)(2,1)}, u32[]{:S(2)}, u32[]{:S(2)}) collective-permute-start(bf16[256,768]{0,1:T(8,128)(2,1)} %bitcast.32), channel_id=1, source_target_pairs={{0,24},{1,25},{2,26},{3,27},{4,28},{5,29},{6,30},{7,31},{8,16},{9,... | collective-permute-start | bytes 1179656 | tf_op jit(solution)/shard_map/ppermute | solution.py:274
  178.1 9.5 %shard_map.75 = (bf16[4,256,256]{2,1,0:T(8,128)(2,1)}, bf16[4,256,256]{2,1,0:T(8,128)(2,1)}, f32[4,2,128,128]{3,2,1,0:T(8,128)}) custom-call(s32[6]{0:T(128)} %add_add_fusion.where, bf16[2,256,1536]{2,1,0:T(8,128)(2,1)} %copy-done.2, bf16[2,256,1536]{2,1,0:T(8,128)(2,1)} %collective-permute-done.1.refs_1_.got, ...), custom_call_target="tpu_custom_call" | custom-call | tf_op jit(solution)/shard_map/pallas_call | solution.py:109
  188.7 9.5 %shard_map.76 = (bf16[4,256,256]{2,1,0:T(8,128)(2,1)}, bf16[4,256,256]{2,1,0:T(8,128)(2,1)}, f32[4,2,128,128]{3,2,1,0:T(8,128)}) custom-call(s32[6]{0:T(128)} %add_add_fusion.1.where, bf16[2,256,1536]{2,1,0:T(8,128)(2,1)} %copy-done.3, bf16[2,256,1536]{2,1,0:T(8,128)(2,1)} %collective-permute-done.6.refs_5_.got, ...), custom_call_target="tpu_custom_call" | custom-call | tf_op jit(solution)/shard_map/pallas_call | solution.py:109
  200.2 5.1 %collective-permute-start.18 = (f32[2,128,128]{2,1,0:T(8,128)}, f32[2,128,128]{2,1,0:T(8,128)}, u32[]{:S(2)}, u32[]{:S(2)}) collective-permute-start(f32[2,128,128]{2,1,0:T(8,128)} %multiply_reduce_fusion), channel_id=1, source_target_pairs={{0,16},{1,17},{2,18},{3,19},{4,20},{5,21},{6,22},{7,23},{8,24},{9,... | collective-permute-start | bytes 393224 | tf_op jit(solution)/shard_map/ppermute | solution.py:274
  205.3 10.7 %shard_map.73.refs_9_ = f32[8,256,256]{2,1,0:T(8,128)} custom-call(s32[2]{0:T(128)} %pad_add_fusion.1.where, bf16[2,256,1536]{2,1,0:T(8,128)(2,1)} %copy-done.2, bf16[2,256,1536]{2,1,0:T(8,128)(2,1)} %collective-permute-done.1.refs_1_.got, bf16[2,256,1536]{2,1,0:T(8,128)(2,1)} %collective-permute-done.2.refs_2_.pair_other, ...), custom_call_target="tpu_custom_call" | custom-call | tf_op jit(solution)/shard_map/pallas_call | solution.py:176
  216.1 11.0 %shard_map.74.q_ref = bf16[8,256,256]{2,1,0:T(8,128)(2,1)} custom-call(s32[2]{0:T(128)} %pad_add_fusion.1.where, bf16[2,256,1536]{2,1,0:T(8,128)(2,1)} %copy-done.2, bf16[2,256,1536]{2,1,0:T(8,128)(2,1)} %collective-permute-done.1.refs_1_.got, bf16[2,256,1536]{2,1,0:T(8,128)(2,1)} %collective-permute-done.2.refs_2_.pair_other, ...), custom_call_target="tpu_custom_call" | custom-call | tf_op jit(solution)/shard_map/pallas_call | solution.py:176
  227.1 1.5 pad_maximum_fusion.3
  228.6 8.9 %mix.1 = bf16[8,256,256]{2,1,0:T(8,128)(2,1)} custom-call(s32[16]{0:T(128)} %pad_add_fusion.pos, bf16[8,256,256]{2,1,0:T(8,128)(2,1)} %shard_map.74.q_ref, bf16[8,256,256]{2,1,0:T(8,128)(2,1)} %get-tuple-element.37.k_ref, bf16[8,256,256]{2,1,0:T(8,128)(2,1)} %get-tuple-element.38.v_ref, f32[8,2,256]{2,1,0:T(2,128)} %copy-done.14, f32[8,256,2]{2,1,0:T(8,128)} %bitcast.133, ...), custom_call_target="tpu_custom_call" | custom-call | tf_op jit(solution)/shard_map/mix/pallas_call | solution.py:226
  238.3 1.5 broadcast_select_fusion.9
  240.4 1.9 collective-permute-done.23
  242.3 1.8 fusion.34
  244.2 1.8 add_convert_fusion
  247.7 1.6 collective-permute-start.27
  250.3 21.6 %collective-permute-done.30 = bf16[2,2,256,512]{3,2,1,0:T(8,128)(2,1)S(1)} collective-permute-done((bf16[2,2,256,512]{3,2,1,0:T(8,128)(2,1)S(1)}, bf16[2,2,256,512]{3,2,1,0:T(8,128)(2,1)S(1)}, u32[]{:S(2)}, u32[]{:S(2)}) %collective-permute-start.30) | collective-permute-done | bytes 1048608 | tf_op jit(solution)/shard_map/ppermute | solution.py:274
  274.9 1.6 collective-permute-start.25
  276.5 9.2 %collective-permute-done.31 = bf16[2,256,512]{2,1,0:T(8,128)(2,1)S(1)} collective-permute-done((bf16[2,256,512]{2,1,0:T(8,128)(2,1)S(1)}, bf16[2,256,512]{2,1,0:T(8,128)(2,1)S(1)}, u32[]{:S(2)}, u32[]{:S(2)}) %collective-permute-start.31) | collective-permute-done | bytes 524320 | tf_op jit(solution)/shard_map/ppermute | solution.py:274
  288.6 1.2 collective-permute-start.26
  289.8 3.6 %collective-permute-done.32 = bf16[256,512]{1,0:T(8,128)(2,1)S(1)} collective-permute-done((bf16[256,512]{1,0:T(8,128)(2,1)S(1)}, bf16[256,512]{1,0:T(8,128)(2,1)S(1)}, u32[]{:S(2)}, u32[]{:S(2)}) %collective-permute-start.32) | collective-permute-done | bytes 262176 | tf_op jit(solution)/shard_map/ppermute | solution.py:274
  293.8 1.2 collective-permute-done.26
  (131 shorter events, 32.5 us)
Async XLA Ops:
  0.0 1.4 copy-start
  0.0 6.1 %copy-start.7 = (bf16[192,2048]{1,0:T(8,128)(2,1)S(1)}, bf16[192,2048]{1,0:T(8,128)(2,1)}, u32[]{:S(2)}) copy-start(bf16[192,2048]{1,0:T(8,128)(2,1)} %param.8) | copy-start | bytes 2359300
  1.5 20.8 %collective-permute-start.4 = (bf16[1,256,1536]{2,1,0:T(8,128)(2,1)S(1)}, bf16[1,256,1536]{2,1,0:T(8,128)(2,1)}, u32[]{:S(2)}, u32[]{:S(2)}) collective-permute-start(bf16[1,256,1536]{2,1,0:T(8,128)(2,1)S(1)} %dynamic-slice_bitcast_fusion), channel_id=1, source_target_pairs={{0,8},{1,9},{2,10},{3,11},{4,12},{5,13},{6,14},{7,15},{8,0},{9,1},... | collective-permute-start | bytes 2359304 | tf_op jit(solution)/shard_map/ppermute | solution.py:274
  4.6 20.0 %collective-permute-start = (bf16[1,256,1536]{2,1,0:T(8,128)(2,1)S(1)}, bf16[1,256,1536]{2,1,0:T(8,128)(2,1)}, u32[]{:S(2)}, u32[]{:S(2)}) collective-permute-start(bf16[1,256,1536]{2,1,0:T(8,128)(2,1)S(1)} %dynamic-slice_bitcast_fusion), channel_id=1, source_target_pairs={{0,2},{1,5},{2,0},{3,7},{4,6},{5,1},{6,4},{7,3},{8,10},{9,13},{10,... | collective-permute-start | bytes 2359304 | tf_op jit(solution)/shard_map/ppermute | solution.py:274
  6.1 5.2 %copy-start.15 = (f32[16,256]{1,0:T(8,128)S(1)}, f32[16,256]{1,0:T(8,128)}, u32[]{:S(2)}) copy-start(f32[16,256]{1,0:T(8,128)} %param.11) | copy-start | bytes 49156
  7.0 41.4 %all-to-all-start = ((bf16[192,4,512]{2,0,1:T(8,128)(2,1)}), bf16[192,4,512]{2,0,1:T(8,128)(2,1)}, u32[]{:S(2)}, u32[]{:S(2)}) async-start(bf16[192,4,512]{2,0,1:T(8,128)(2,1)} %bitcast.129), calls=%async_computation | async-start | bytes 1572864 | tf_op jit(solution)/shard_map/all_to_all | solution.py:278
  22.2 19.5 %collective-permute-start.5 = (bf16[1,256,1536]{2,1,0:T(8,128)(2,1)}, bf16[1,256,1536]{2,1,0:T(8,128)(2,1)}, u32[]{:S(2)}, u32[]{:S(2)}) collective-permute-start(bf16[1,256,1536]{2,1,0:T(8,128)(2,1)} %collective-permute-done.4), channel_id=1, source_target_pairs={{0,2},{1,5},{2,0},{3,7},{4,6},{5,1},{6,4},{7,3},{8,10},{9,13},{10,... | collective-permute-start | bytes 2359304 | tf_op jit(solution)/shard_map/ppermute | solution.py:274
  25.8 89.9 %copy-start.2 = (bf16[2,256,1536]{2,1,0:T(8,128)(2,1)}, bf16[2,256,1536]{2,1,0:T(8,128)(2,1)S(1)}, u32[]{:S(2)}) copy-start(bf16[2,256,1536]{2,1,0:T(8,128)(2,1)S(1)} %pad_maximum_fusion.refs_0_.pair) | copy-start | bytes 4718596
  25.8 90.0 %collective-permute-start.1 = (bf16[2,256,1536]{2,1,0:T(8,128)(2,1)S(1)}, bf16[2,256,1536]{2,1,0:T(8,128)(2,1)}, u32[]{:S(2)}, u32[]{:S(2)}) collective-permute-start(bf16[2,256,1536]{2,1,0:T(8,128)(2,1)S(1)} %pad_maximum_fusion.refs_0_.pair), channel_id=1, source_target_pairs={{0,4},{1,3},{2,6},{3,1},{4,0},{5,7},{6,2},{7,5},{8,12},{9,11},{10,... | collective-permute-start | bytes 4718600 | tf_op jit(solution)/shard_map/ppermute | solution.py:274
  42.9 85.7 %copy-start.3 = (bf16[2,256,1536]{2,1,0:T(8,128)(2,1)}, bf16[2,256,1536]{2,1,0:T(8,128)(2,1)S(1)}, u32[]{:S(2)}) copy-start(bf16[2,256,1536]{2,1,0:T(8,128)(2,1)S(1)} %constant_dynamic-update-slice_fusion.refs_4_.pair) | copy-start | bytes 4718596
  42.9 85.7 %collective-permute-start.6 = (bf16[2,256,1536]{2,1,0:T(8,128)(2,1)S(1)}, bf16[2,256,1536]{2,1,0:T(8,128)(2,1)}, u32[]{:S(2)}, u32[]{:S(2)}) collective-permute-start(bf16[2,256,1536]{2,1,0:T(8,128)(2,1)S(1)} %constant_dynamic-update-slice_fusion.refs_4_.pair), channel_id=1, source_target_pairs={{0,4},{1,3},{2,6},{3,1},{4,0},{5,7},{6,2},{7,5},{8,12},{9,11},{10,... | collective-permute-start | bytes 4718600 | tf_op jit(solution)/shard_map/ppermute | solution.py:274
  48.4 25.5 %all-to-all-start.1 = ((bf16[192,4,512]{2,0,1:T(8,128)(2,1)}), bf16[192,4,512]{2,0,1:T(8,128)(2,1)}, u32[]{:S(2)}, u32[]{:S(2)}) async-start(bf16[192,4,512]{2,0,1:T(8,128)(2,1)} %bitcast.141), calls=%async_computation.1 | async-start | bytes 1572864 | tf_op jit(solution)/shard_map/all_to_all | solution.py:278
  55.3 24.8 %collective-permute-start.10 = (bf16[768,256]{1,0:T(8,128)(2,1)}, bf16[768,256]{1,0:T(8,128)(2,1)}, u32[]{:S(2)}, u32[]{:S(2)}) collective-permute-start(bf16[768,256]{1,0:T(8,128)(2,1)} %get-tuple-element.34), channel_id=1, source_target_pairs={{0,24},{1,25},{2,26},{3,27},{4,28},{5,29},{6,30},{7,31},{8,16},{9,... | collective-permute-start | bytes 1179656 | tf_op jit(solution)/shard_map/ppermute | solution.py:274
  62.2 37.3 %collective-permute-start.11 = (bf16[768,256]{1,0:T(8,128)(2,1)}, bf16[768,256]{1,0:T(8,128)(2,1)}, u32[]{:S(2)}, u32[]{:S(2)}) collective-permute-start(bf16[768,256]{1,0:T(8,128)(2,1)} %get-tuple-element.34), channel_id=1, source_target_pairs={{0,8},{1,9},{2,10},{3,11},{4,12},{5,13},{6,14},{7,15},{8,0},{9,1},... | collective-permute-start | bytes 1179656 | tf_op jit(solution)/shard_map/ppermute | solution.py:274
  62.2 37.3 %collective-permute-start.9 = (bf16[768,256]{1,0:T(8,128)(2,1)}, bf16[768,256]{1,0:T(8,128)(2,1)}, u32[]{:S(2)}, u32[]{:S(2)}) collective-permute-start(bf16[768,256]{1,0:T(8,128)(2,1)} %get-tuple-element.33), channel_id=1, source_target_pairs={{0,16},{1,17},{2,18},{3,19},{4,20},{5,21},{6,22},{7,23},{8,24},{9,... | collective-permute-start | bytes 1179656 | tf_op jit(solution)/shard_map/ppermute | solution.py:274
  73.9 37.7 %all-to-all-start.2 = ((bf16[192,4,512]{2,0,1:T(8,128)(2,1)}), bf16[192,4,512]{2,0,1:T(8,128)(2,1)}, u32[]{:S(2)}, u32[]{:S(2)}) async-start(bf16[192,4,512]{2,0,1:T(8,128)(2,1)} %bitcast.140), calls=%async_computation.2 | async-start | bytes 1572864 | tf_op jit(solution)/shard_map/all_to_all | solution.py:278
  78.1 5.0 %copy-start.16 = (s32[8]{0:T(128)S(1)}, s32[8]{0:T(128)}, u32[]{:S(2)}) copy-start(s32[8]{0:T(128)} %fusion.20) | copy-start | bytes 100
  80.0 35.7 %collective-permute-start.14 = (bf16[768,256]{1,0:T(8,128)(2,1)}, bf16[768,256]{1,0:T(8,128)(2,1)}, u32[]{:S(2)}, u32[]{:S(2)}) collective-permute-start(bf16[768,256]{1,0:T(8,128)(2,1)} %get-tuple-element.32), channel_id=1, source_target_pairs={{0,24},{1,25},{2,26},{3,27},{4,28},{5,29},{6,30},{7,31},{8,16},{9,... | collective-permute-start | bytes 1179656 | tf_op jit(solution)/shard_map/ppermute | solution.py:274
  99.5 29.1 %collective-permute-start.12 = (bf16[768,256]{1,0:T(8,128)(2,1)}, bf16[768,256]{1,0:T(8,128)(2,1)}, u32[]{:S(2)}, u32[]{:S(2)}) collective-permute-start(bf16[768,256]{1,0:T(8,128)(2,1)} %get-tuple-element.32), channel_id=1, source_target_pairs={{0,8},{1,9},{2,10},{3,11},{4,12},{5,13},{6,14},{7,15},{8,0},{9,1},... | collective-permute-start | bytes 1179656 | tf_op jit(solution)/shard_map/ppermute | solution.py:274
  99.6 26.6 %collective-permute-start.13 = (bf16[768,256]{1,0:T(8,128)(2,1)S(1)}, bf16[768,256]{1,0:T(8,128)(2,1)}, u32[]{:S(2)}, u32[]{:S(2)}) collective-permute-start(bf16[768,256]{1,0:T(8,128)(2,1)S(1)} %get-tuple-element.31), channel_id=1, source_target_pairs={{0,16},{1,17},{2,18},{3,19},{4,20},{5,21},{6,22},{7,23},{8,24},{9,... | collective-permute-start | bytes 1179656 | tf_op jit(solution)/shard_map/ppermute | solution.py:274
  105.3 5.8 %copy-start.17 = (s32[4]{0:T(128)S(1)}, s32[4]{0:T(128)}, u32[]{:S(2)}) copy-start(s32[4]{0:T(128)} %get-tuple-element.35) | copy-start | bytes 52
  111.7 10.3 %all-to-all-start.3 = ((f32[8,1,512]{2,1,0:T(1,128)}), f32[8,1,512]{2,1,0:T(1,128)S(1)}, u32[]{:S(2)}, u32[]{:S(2)}) async-start(f32[8,1,512]{2,1,0:T(1,128)} %all_to_all.66), calls=%async_computation.3 | async-start | bytes 32768 | tf_op jit(solution)/shard_map/all_to_all | solution.py:278
  115.7 58.9 %collective-permute-start.2 = (bf16[2,256,1536]{2,1,0:T(8,128)(2,1)S(1)}, bf16[2,256,1536]{2,1,0:T(8,128)(2,1)}, u32[]{:S(2)}, u32[]{:S(2)}) collective-permute-start(bf16[2,256,1536]{2,1,0:T(8,128)(2,1)S(1)} %pad_maximum_fusion.refs_0_.pair), channel_id=1, source_target_pairs={{0,1},{1,0},{2,3},{3,2},{4,5},{5,4},{6,7},{7,6},{8,9},{9,8},{10,11... | collective-permute-start | bytes 4718600 | tf_op jit(solution)/shard_map/ppermute | solution.py:274
  115.8 61.9 %collective-permute-start.3 = (bf16[2,256,1536]{2,1,0:T(8,128)(2,1)}, bf16[2,256,1536]{2,1,0:T(8,128)(2,1)}, u32[]{:S(2)}, u32[]{:S(2)}) collective-permute-start(bf16[2,256,1536]{2,1,0:T(8,128)(2,1)} %collective-permute-done.1.refs_1_.got), channel_id=1, source_target_pairs={{0,1},{1,0},{2,3},{3,2},{4,5},{5,4},{6,7},{7,6},{8,9},{9,8},{10,11... | collective-permute-start | bytes 4718600 | tf_op jit(solution)/shard_map/ppermute | solution.py:274
  122.0 24.3 %all-to-all-start.4 = ((bf16[4,2,256,192]{2,1,3,0:T(2,128)(2,1)}), bf16[4,2,256,192]{2,1,3,0:T(2,128)(2,1)}, u32[]{:S(2)}, u32[]{:S(2)}) async-start(bf16[4,2,256,192]{2,1,3,0:T(2,128)(2,1)} %copy.57), calls=%async_computation.4 | async-start | bytes 1572864 | tf_op jit(solution)/shard_map/all_to_all | solution.py:278
  126.2 14.9 %collective-permute-start.17 = (bf16[768,256]{1,0:T(8,128)(2,1)}, bf16[768,256]{1,0:T(8,128)(2,1)}, u32[]{:S(2)}, u32[]{:S(2)}) collective-permute-start(bf16[768,256]{1,0:T(8,128)(2,1)} %get-tuple-element.30), channel_id=1, source_target_pairs={{0,24},{1,25},{2,26},{3,27},{4,28},{5,29},{6,30},{7,31},{8,16},{9,... | collective-permute-start | bytes 1179656 | tf_op jit(solution)/shard_map/ppermute | solution.py:274
  128.7 60.0 %collective-permute-start.7 = (bf16[2,256,1536]{2,1,0:T(8,128)(2,1)S(1)}, bf16[2,256,1536]{2,1,0:T(8,128)(2,1)}, u32[]{:S(2)}, u32[]{:S(2)}) collective-permute-start(bf16[2,256,1536]{2,1,0:T(8,128)(2,1)S(1)} %constant_dynamic-update-slice_fusion.refs_4_.pair), channel_id=1, source_target_pairs={{0,1},{1,0},{2,3},{3,2},{4,5},{5,4},{6,7},{7,6},{8,9},{9,8},{10,11... | collective-permute-start | bytes 4718600 | tf_op jit(solution)/shard_map/ppermute | solution.py:274
  128.7 60.0 %collective-permute-start.8 = (bf16[2,256,1536]{2,1,0:T(8,128)(2,1)}, bf16[2,256,1536]{2,1,0:T(8,128)(2,1)}, u32[]{:S(2)}, u32[]{:S(2)}) collective-permute-start(bf16[2,256,1536]{2,1,0:T(8,128)(2,1)} %collective-permute-done.6.refs_5_.got), channel_id=1, source_target_pairs={{0,1},{1,0},{2,3},{3,2},{4,5},{5,4},{6,7},{7,6},{8,9},{9,8},{10,11... | collective-permute-start | bytes 4718600 | tf_op jit(solution)/shard_map/ppermute | solution.py:274
  134.3 6.7 %copy-start.14 = (f32[8,2,256]{2,1,0:T(2,128)}, f32[8,2,256]{2,1,0:T(2,128)S(1)}, u32[]{:S(2)}) copy-start(f32[8,2,256]{2,1,0:T(2,128)S(1)} %reshape.146.cum_ref) | copy-start | bytes 49156
  141.0 20.7 %collective-permute-start.16 = (bf16[768,256]{1,0:T(8,128)(2,1)}, bf16[768,256]{1,0:T(8,128)(2,1)}, u32[]{:S(2)}, u32[]{:S(2)}) collective-permute-start(bf16[768,256]{1,0:T(8,128)(2,1)} %get-tuple-element.29), channel_id=1, source_target_pairs={{0,16},{1,17},{2,18},{3,19},{4,20},{5,21},{6,22},{7,23},{8,24},{9,... | collective-permute-start | bytes 1179656 | tf_op jit(solution)/shard_map/ppermute | solution.py:274
  146.3 15.5 %copy-start.13 = (bf16[768,256]{1,0:T(8,128)(2,1)S(1)}, bf16[768,256]{1,0:T(8,128)(2,1)}, u32[]{:S(2)}) copy-start(bf16[768,256]{1,0:T(8,128)(2,1)} %get-tuple-element.30) | copy-start | bytes 1179652
  161.8 9.3 %collective-permute-start.15 = (bf16[768,256]{1,0:T(8,128)(2,1)S(1)}, bf16[768,256]{1,0:T(8,128)(2,1)S(1)}, u32[]{:S(2)}, u32[]{:S(2)}) collective-permute-start(bf16[768,256]{1,0:T(8,128)(2,1)S(1)} %copy-done.13), channel_id=1, source_target_pairs={{0,8},{1,9},{2,10},{3,11},{4,12},{5,13},{6,14},{7,15},{8,0},{9,1},... | collective-permute-start | bytes 1179656 | tf_op jit(solution)/shard_map/ppermute | solution.py:274
  165.9 6.2 %copy-start.6 = (bf16[768,256]{1,0:T(8,128)(2,1)S(1)}, bf16[768,256]{1,0:T(8,128)(2,1)}, u32[]{:S(2)}) copy-start(bf16[768,256]{1,0:T(8,128)(2,1)} %get-tuple-element.29) | copy-start | bytes 1179652
  171.0 66.5 %collective-permute-start.19 = (bf16[256,768]{0,1:T(8,128)(2,1)}, bf16[256,768]{0,1:T(8,128)(2,1)S(1)}, u32[]{:S(2)}, u32[]{:S(2)}) collective-permute-start(bf16[256,768]{0,1:T(8,128)(2,1)} %bitcast.32), channel_id=1, source_target_pairs={{0,8},{1,9},{2,10},{3,11},{4,12},{5,13},{6,14},{7,15},{8,0},{9,1},... | collective-permute-start | bytes 1179656 | tf_op jit(solution)/shard_map/ppermute | solution.py:274
  174.7 62.9 %collective-permute-start.20 = (bf16[256,768]{0,1:T(8,128)(2,1)}, bf16[256,768]{0,1:T(8,128)(2,1)}, u32[]{:S(2)}, u32[]{:S(2)}) collective-permute-start(bf16[256,768]{0,1:T(8,128)(2,1)} %bitcast.32), channel_id=1, source_target_pairs={{0,24},{1,25},{2,26},{3,27},{4,28},{5,29},{6,30},{7,31},{8,16},{9,... | collective-permute-start | bytes 1179656 | tf_op jit(solution)/shard_map/ppermute | solution.py:274
  177.8 60.5 %collective-permute-start.21 = (bf16[256,768]{0,1:T(8,128)(2,1)}, bf16[256,768]{0,1:T(8,128)(2,1)}, u32[]{:S(2)}, u32[]{:S(2)}) collective-permute-start(bf16[256,768]{0,1:T(8,128)(2,1)} %bitcast.33), channel_id=1, source_target_pairs={{0,16},{1,17},{2,18},{3,19},{4,20},{5,21},{6,22},{7,23},{8,24},{9,... | collective-permute-start | bytes 1179656 | tf_op jit(solution)/shard_map/ppermute | solution.py:274
  199.2 16.8 %copy-start.4 = (f32[8,2,128,128]{3,2,1,0:T(8,128)}, f32[8,2,128,128]{3,2,1,0:T(8,128)S(1)}, u32[]{:S(2)}) copy-start(f32[8,2,128,128]{3,2,1,0:T(8,128)S(1)} %constant_dynamic-update-slice_fusion.2.state_ref) | copy-start | bytes 3145732
  200.2 28.4 %collective-permute-start.18 = (f32[2,128,128]{2,1,0:T(8,128)}, f32[2,128,128]{2,1,0:T(8,128)}, u32[]{:S(2)}, u32[]{:S(2)}) collective-permute-start(f32[2,128,128]{2,1,0:T(8,128)} %multiply_reduce_fusion), channel_id=1, source_target_pairs={{0,16},{1,17},{2,18},{3,19},{4,20},{5,21},{6,22},{7,23},{8,24},{9,... | collective-permute-start | bytes 393224 | tf_op jit(solution)/shard_map/ppermute | solution.py:274
  216.0 11.0 %copy-start.8 = (bf16[4,256,256]{2,1,0:T(8,128)(2,1)S(1)}, bf16[4,256,256]{2,1,0:T(8,128)(2,1)}, u32[]{:S(2)}) copy-start(bf16[4,256,256]{2,1,0:T(8,128)(2,1)} %get-tuple-element.11) | copy-start | bytes 1572868
  216.0 11.0 %copy-start.9 = (bf16[4,256,256]{2,1,0:T(8,128)(2,1)S(1)}, bf16[4,256,256]{2,1,0:T(8,128)(2,1)}, u32[]{:S(2)}) copy-start(bf16[4,256,256]{2,1,0:T(8,128)(2,1)} %get-tuple-element.13) | copy-start | bytes 1572868
  216.0 11.0 %copy-start.10 = (bf16[4,256,256]{2,1,0:T(8,128)(2,1)S(1)}, bf16[4,256,256]{2,1,0:T(8,128)(2,1)}, u32[]{:S(2)}) copy-start(bf16[4,256,256]{2,1,0:T(8,128)(2,1)} %get-tuple-element.12) | copy-start | bytes 1572868
  216.0 11.0 %copy-start.11 = (bf16[4,256,256]{2,1,0:T(8,128)(2,1)S(1)}, bf16[4,256,256]{2,1,0:T(8,128)(2,1)}, u32[]{:S(2)}) copy-start(bf16[4,256,256]{2,1,0:T(8,128)(2,1)} %get-tuple-element.14) | copy-start | bytes 1572868
  237.5 4.8 %collective-permute-start.22 = (bf16[2048,256]{1,0:T(8,128)(2,1)}, bf16[2048,256]{1,0:T(8,128)(2,1)S(1)}, u32[]{:S(2)}, u32[]{:S(2)}) collective-permute-start(bf16[2048,256]{1,0:T(8,128)(2,1)} %bitcast.137), channel_id=1, source_target_pairs={{0,1},{1,0},{2,3},{3,2},{4,5},{5,4},{6,7},{7,6},{8,9},{9,8},{10,11... | collective-permute-start | bytes 3145736 | tf_op jit(solution)/shard_map/ppermute | solution.py:274
  237.5 0.7 copy-start.12
  239.8 4.3 %copy-start.5 = (bf16[8,256,256]{2,1,0:T(8,128)(2,1)S(1)}, bf16[8,256,256]{2,1,0:T(8,128)(2,1)}, u32[]{:S(2)}) copy-start(bf16[8,256,256]{2,1,0:T(8,128)(2,1)} %mix.1) | copy-start | bytes 3145732
  239.8 2.5 collective-permute-start.23
  246.4 25.5 %collective-permute-start.30 = (bf16[2,2,256,512]{3,2,1,0:T(8,128)(2,1)S(1)}, bf16[2,2,256,512]{3,2,1,0:T(8,128)(2,1)S(1)}, u32[]{:S(2)}, u32[]{:S(2)}) collective-permute-start(bf16[2,2,256,512]{3,2,1,0:T(8,128)(2,1)S(1)} %slice_bitcast_fusion), channel_id=1, source_target_pairs={{0,2},{1,3},{2,0},{3,1},{4,6},{5,7},{6,4},{7,5},{8,10},{9,11},{10,... | collective-permute-start | bytes 3145736 | tf_op jit(solution)/shard_map/ppermute | solution.py:274
  247.7 25.5 %collective-permute-start.27 = (bf16[2,2,256,512]{3,2,0,1:T(8,128)(2,1)S(1)}, bf16[2,2,256,512]{3,2,0,1:T(8,128)(2,1)S(1)}, u32[]{:S(2)}, u32[]{:S(2)}) collective-permute-start(bf16[2,2,256,512]{3,2,0,1:T(8,128)(2,1)S(1)} %bitcast.145), channel_id=1, source_target_pairs={{0,4},{1,5},{2,6},{3,7},{4,0},{5,1},{6,2},{7,3},{8,12},{9,13},{10,... | collective-permute-start | bytes 3145736 | tf_op jit(solution)/shard_map/ppermute | solution.py:274
  249.4 25.2 %collective-permute-start.24 = (bf16[2,2,256,512]{3,2,1,0:T(8,128)(2,1)S(1)}, bf16[2,2,256,512]{3,2,1,0:T(8,128)(2,1)S(1)}, u32[]{:S(2)}, u32[]{:S(2)}) collective-permute-start(bf16[2,2,256,512]{3,2,1,0:T(8,128)(2,1)S(1)} %bitcast.146), channel_id=1, source_target_pairs={{0,8},{1,9},{2,10},{3,11},{4,12},{5,13},{6,14},{7,15},{8,0},{9,1},... | collective-permute-start | bytes 3145736 | tf_op jit(solution)/shard_map/ppermute | solution.py:274
  272.2 13.4 %collective-permute-start.31 = (bf16[2,256,512]{2,1,0:T(8,128)(2,1)S(1)}, bf16[2,256,512]{2,1,0:T(8,128)(2,1)S(1)}, u32[]{:S(2)}, u32[]{:S(2)}) collective-permute-start(bf16[2,256,512]{2,1,0:T(8,128)(2,1)S(1)} %slice_bitcast_fusion.2), channel_id=1, source_target_pairs={{0,8},{1,9},{2,10},{3,11},{4,12},{5,13},{6,14},{7,15},{8,0},{9,1},... | collective-permute-start | bytes 1572872 | tf_op jit(solution)/shard_map/ppermute | solution.py:274
  273.5 13.3 %collective-permute-start.28 = (bf16[2,256,512]{2,1,0:T(8,128)(2,1)S(1)}, bf16[2,256,512]{2,1,0:T(8,128)(2,1)S(1)}, u32[]{:S(2)}, u32[]{:S(2)}) collective-permute-start(bf16[2,256,512]{2,1,0:T(8,128)(2,1)S(1)} %slice_bitcast_fusion.4), channel_id=1, source_target_pairs={{0,2},{1,3},{2,0},{3,1},{4,6},{5,7},{6,4},{7,5},{8,10},{9,11},{10,... | collective-permute-start | bytes 1572872 | tf_op jit(solution)/shard_map/ppermute | solution.py:274
  274.9 13.5 %collective-permute-start.25 = (bf16[2,256,512]{2,1,0:T(8,128)(2,1)S(1)}, bf16[2,256,512]{2,1,0:T(8,128)(2,1)S(1)}, u32[]{:S(2)}, u32[]{:S(2)}) collective-permute-start(bf16[2,256,512]{2,1,0:T(8,128)(2,1)S(1)} %slice_bitcast_fusion.6), channel_id=1, source_target_pairs={{0,4},{1,5},{2,6},{3,7},{4,0},{5,1},{6,2},{7,3},{8,12},{9,13},{10,... | collective-permute-start | bytes 1572872 | tf_op jit(solution)/shard_map/ppermute | solution.py:274
  285.8 7.6 %collective-permute-start.32 = (bf16[256,512]{1,0:T(8,128)(2,1)S(1)}, bf16[256,512]{1,0:T(8,128)(2,1)S(1)}, u32[]{:S(2)}, u32[]{:S(2)}) collective-permute-start(bf16[256,512]{1,0:T(8,128)(2,1)S(1)} %slice_bitcast_fusion.8), channel_id=1, source_target_pairs={{0,4},{1,5},{2,6},{3,7},{4,0},{5,1},{6,2},{7,3},{8,12},{9,13},{10,... | collective-permute-start | bytes 786440 | tf_op jit(solution)/shard_map/ppermute | solution.py:274
  287.0 6.7 %collective-permute-start.29 = (bf16[256,512]{1,0:T(8,128)(2,1)S(1)}, bf16[256,512]{1,0:T(8,128)(2,1)S(1)}, u32[]{:S(2)}, u32[]{:S(2)}) collective-permute-start(bf16[256,512]{1,0:T(8,128)(2,1)S(1)} %slice_bitcast_fusion.10), channel_id=1, source_target_pairs={{0,8},{1,9},{2,10},{3,11},{4,12},{5,13},{6,14},{7,15},{8,0},{9,1},... | collective-permute-start | bytes 786440 | tf_op jit(solution)/shard_map/ppermute | solution.py:274
  288.6 6.4 %collective-permute-start.26 = (bf16[256,512]{1,0:T(8,128)(2,1)S(1)}, bf16[256,512]{1,0:T(8,128)(2,1)S(1)}, u32[]{:S(2)}, u32[]{:S(2)}) collective-permute-start(bf16[256,512]{1,0:T(8,128)(2,1)S(1)} %slice_bitcast_fusion.12), channel_id=1, source_target_pairs={{0,2},{1,3},{2,0},{3,1},{4,6},{5,7},{6,4},{7,5},{8,10},{9,11},{10,... | collective-permute-start | bytes 786440 | tf_op jit(solution)/shard_map/ppermute | solution.py:274
  293.4 2.6 copy-start.1
where the time goes:
time: 298 us; the launch traced here: 296 us
  waiting for transfers between devices  108 us (36%)
  starting transfers between devices  68.8 us (23%)
  Pallas kernels  49.6 us (17%)
  other arithmetic  33.8 us (11%)
  local copies, waits for them, and re-layouts  32.1 us (11%)
  matrix products  3.67 us (1%)
    ppermute x33, waiting for transfers between devices, exchange(): return lax.ppermute(value, ('ctx', 'head'), pairs)  92.9 us
    ppermute x33, starting transfers between devices, exchange(): return lax.ppermute(value, ('ctx', 'head'), pairs)  48 us
    pallas_call x2, Pallas kernels, query_part(): pl.pallas_call(functools.partial(query_body, late=late), grid_spec=pltpu....  21.7 us
    all_to_all x5, starting transfers between devices, spread(): lax.all_to_all(value, 'ctx', split, concat, axis_index_groups=groups, til...  20.8 us
    pallas_call x2, Pallas kernels, keys_values(): pl.pallas_call(functools.partial(keys_values_body, heads=heads, head_dim=...  19 us
    all_to_all x5, waiting for transfers between devices, spread(): lax.all_to_all(value, 'ctx', split, concat, axis_index_groups=groups, til...  14.6 us
    another operation x4, other arithmetic, per_device(): stack = lambda pieces: jnp.stack(pieces)  9.28 us
    pallas_call x1, Pallas kernels, mix(): pl.pallas_call(functools.partial(mix_body, heads=heads, head_dim=head_dim...  8.95 us
  transfers between devices with their start and end apart: 38, of which 14 were waited for; matrix products, arithmetic and copies ran while one was open for 21% of the time, Pallas kernels for 17%

commit v1 on v0

v1 whole, which is shorter than its diff:
```python
import functools
import math

import jax
import jax.numpy as jnp
from jax import lax
from jax.experimental import pallas as pl
from jax.experimental.pallas import tpu as pltpu
from jax.sharding import PartitionSpec as P


F32 = jnp.float32
BF16 = jnp.bfloat16


def silu(x):
    return x / (1.0 + jnp.exp(-x))


def block_state(k, v, cum_t, heads, head_dim):
    rows = k.shape[0]
    out = []
    for i in range(heads):
        cols = slice(i * head_dim, (i + 1) * head_dim)
        cum = cum_t[:, i : i + 1]
        last = cum_t[rows - 1 : rows, i : i + 1]
        decayed = (k[:, cols].astype(F32) * jnp.exp(last - cum)).astype(BF16)
        out.append(
            lax.dot_general(
                decayed, v[:, cols], (((0,), (0,)), ((), ())), preferred_element_type=F32
            )
        )
    return out


def state_body(where, k_ref, v_ref, cum_t_ref, out_ref, *, heads, head_dim):
    for i, s in enumerate(block_state(k_ref[0], v_ref[0], cum_t_ref[0], heads, head_dim)):
        out_ref[0, i] = s


def block_states(block_at, k, v, cum_t, heads, head_dim):
    count, rows, width = k.shape
    here = lambda i, w: (i, 0, 0)
    return pl.pallas_call(
        functools.partial(state_body, heads=heads, head_dim=head_dim),
        grid_spec=pltpu.PrefetchScalarGridSpec(
            num_scalar_prefetch=1,
            grid=(count,),
            in_specs=[
                pl.BlockSpec((1, rows, width), here),
                pl.BlockSpec((1, rows, width), here),
                pl.BlockSpec((1, rows, heads), lambda i, w: (w[i], 0, 0)),
            ],
            out_specs=pl.BlockSpec(
                (1, heads, head_dim, head_dim), lambda i, w: (i, 0, 0, 0)
            ),
        ),
        out_shape=jax.ShapeDtypeStruct((count, heads, head_dim, head_dim), F32),
        name="block_states",
    )(block_at, k, v, cum_t)


OWN = ((0, 0, 0), (0, 1, 1), (1, 0, 2), (1, 1, 3))
OTHER = ((0, 0, 0), (0, 1, 2), (1, 0, 1), (1, 1, 3))


def wide(ref):
    return ref[...].reshape(-1, ref.shape[-1])


def stand_up(cum_ref, cum_t_ref):
    count, _, heads = cum_t_ref.shape
    turned = cum_ref[...].T
    for i in range(count):
        cum_t_ref[i] = turned[:, i * heads : (i + 1) * heads]


def keys_values_body(table, *refs, heads, head_dim):
    tokens, weights = refs[:8], refs[8:16]
    cum_ref, after_ref, k_ref, v_ref, state_ref, total_ref, w_ref, cum_t_ref = refs[16:]
    stand_up(cum_ref, cum_t_ref)
    rows, width = k_ref.shape[1:]
    cut = weights[0].shape[0]
    mine, swap = table[8], table[9]
    for side in range(2):
        for i in range(2):
            for r in range(4):

                @pl.when(2 * (mine ^ side) + (swap ^ i) == r)
                def _():
                    for j in range(2):
                        w_ref[side, i * cut : (i + 1) * cut, j * width : (j + 1) * width] = (
                            weights[4 * j + r][...]
                        )

    totals = [0.0] * heads
    for family in range(2):
        out = [
            jnp.dot(wide(x), w_ref[i // 2], preferred_element_type=F32)
            for i, x in enumerate(tokens[4 * family : 4 * family + 4])
        ]
        block = lambda x, at: x[at[0]][at[1] * rows : (at[1] + 1) * rows]
        for spot in range(4):
            mate = [at for at in OTHER if at[2] == spot][0]
            raw = block(out[:2], OWN[spot]) + block(out[2:], mate)
            k = silu(raw[:, :width]).astype(BF16)
            v = raw[:, width:].astype(BF16)
            at = 4 * family + spot
            k_ref[at] = k
            v_ref[at] = v
            b = table[at]
            for i, s in enumerate(block_state(k, v, cum_t_ref[b], heads, head_dim)):
                state_ref[at, i] = s
                totals[i] += jnp.exp(after_ref[b, :, i : i + 1]) * s
    for i in range(heads):
        total_ref[i] = totals[i]


def on_chip(count):
    return [pl.BlockSpec(memory_space=pltpu.VMEM) for _ in range(count)]


def keys_values(table, near, far, wk, wv, cum, after, heads, head_dim):
    _, rows, _ = near[0].shape
    cut, width = wk[0].shape
    return pl.pallas_call(
        functools.partial(keys_values_body, heads=heads, head_dim=head_dim),
        in_specs=[pl.BlockSpec(memory_space=pltpu.SMEM)] + on_chip(18),
        out_specs=on_chip(4),
        out_shape=[
            jax.ShapeDtypeStruct((8, rows, width), BF16),
            jax.ShapeDtypeStruct((8, rows, width), BF16),
            jax.ShapeDtypeStruct((8, heads, head_dim, head_dim), F32),
            jax.ShapeDtypeStruct((heads, head_dim, head_dim), F32),
        ],
        scratch_shapes=[
            pltpu.VMEM((2, 2 * cut, 2 * width), BF16),
            pltpu.VMEM((8, rows, heads), F32),
        ],
        name="keys_values",
    )(table, *near, *far, *wk, *wv, cum, after)


def query_body(table, *refs, late):
    tokens, (first, second, *rest, out_ref, w_ref) = refs[:8], refs[8:]
    rows = out_ref.shape[1]
    cut = first.shape[0]
    mine, swap = table[0], table[1]
    for i, (low, high) in enumerate(((first, second), (second, first))):

        @pl.when(swap == i)
        def _():
            w_ref[:cut] = low[...]
            w_ref[cut:] = high[...]

    for side, spots in ((0, OWN), (1, OTHER)):

        @pl.when((mine ^ side) == (1 if late else 0))
        def _():
            for family in range(2):
                runs = tokens[4 * family + 2 * side : 4 * family + 2 * side + 2]
                out = [jnp.dot(wide(x), w_ref[...], preferred_element_type=F32) for x in runs]
                for run, index, spot in spots:
                    part = out[run][index * rows : (index + 1) * rows]
                    at = 4 * family + spot
                    if late:
                        out_ref[at] = silu(rest[0][at] + part).astype(BF16)
                    else:
                        out_ref[at] = part


def query_part(table, near, far, weights, early):
    _, rows, _ = near[0].shape
    cut, width = weights[0].shape
    late = early is not None
    args = [*near, *far, *weights] + ([early] if late else [])
    return pl.pallas_call(
        functools.partial(query_body, late=late),
        in_specs=[pl.BlockSpec(memory_space=pltpu.SMEM)] + on_chip(len(args)),
        out_specs=on_chip(1)[0],
        out_shape=jax.ShapeDtypeStruct((8, rows, width), BF16 if late else F32),
        scratch_shapes=[pltpu.VMEM((2 * cut, width), BF16)],
    )(table, *args)


def mix_body(
    table, q_ref, k_ref, v_ref, cum_ref, state_ref, group_ref, gain_ref, out_ref, cum_t_ref,
    *, heads, head_dim,
):
    count, rows = q_ref.shape[:2]
    causal = lax.broadcasted_iota(jnp.int32, (rows, rows), 0) >= lax.broadcasted_iota(
        jnp.int32, (rows, rows), 1
    )
    stand_up(cum_ref, cum_t_ref)
    carry = [group_ref[i] for i in range(heads)]
    for b in range(count):
        at, to, order = table[b], table[count + b], table[2 * count + b]
        for i in range(heads):
            cols = slice(i * head_dim, (i + 1) * head_dim)
            q, k, v = q_ref[at, :, cols], k_ref[at, :, cols], v_ref[at, :, cols]
            cum = cum_t_ref[order, :, i : i + 1]
            last = cum_t_ref[order, rows - 1 : rows, i : i + 1]
            diff = cum - cum_ref[pl.ds(order * heads + i, 1), :]
            decay = jnp.where(causal, jnp.exp(jnp.where(causal, diff, 0.0)), 0.0)
            scores = lax.dot_general(q, k, (((1,), (1,)), ((), ())), preferred_element_type=F32)
            weights = (scores * decay).astype(BF16)
            intra = jnp.dot(weights, v, preferred_element_type=F32)
            state = carry[i]
            carry[i] = jnp.exp(last) * state + state_ref[at, i]
            high = state.astype(BF16)
            low = (state - high.astype(F32)).astype(BF16)
            inter = jnp.dot(q, high, preferred_element_type=F32) + jnp.dot(
                q, low, preferred_element_type=F32
            )
            mixed = intra + jnp.exp(cum) * inter
            scale = lax.rsqrt(jnp.mean(mixed * mixed, axis=-1, keepdims=True) + 1e-06)
            out_ref[to, :, cols] = (mixed * scale * gain_ref[:, cols]).astype(BF16)


def mix(table, q, k, v, cum, states, group, gain, heads, head_dim):
    return pl.pallas_call(
        functools.partial(mix_body, heads=heads, head_dim=head_dim),
        in_specs=[pl.BlockSpec(memory_space=pltpu.SMEM)] + on_chip(7),
        out_specs=on_chip(1)[0],
        out_shape=jax.ShapeDtypeStruct(k.shape, BF16),
        scratch_shapes=[pltpu.VMEM((k.shape[0], k.shape[1], heads), F32)],
        name="mix",
    )(table, q, k, v, cum, states, group, gain)


def per_device(tokens, w_query, w_key, w_value, log_decay, norm_gain, w_out, *, n, nh):
    rows, model = tokens.shape
    heads_here = log_decay.shape[0]
    head_dim = w_query.shape[1] // heads_here
    g = math.gcd(heads_here, max(n // 2, 1))
    ng = n // g
    heads = heads_here // g
    width = heads * head_dim
    c = lax.axis_index("ctx")
    h = lax.axis_index("head")
    member = c % g
    group = c // g
    bits = [1 << i for i in range(g.bit_length() - 1)][::-1]
    cube = len(bits) == 3 and ng == 2 and nh == 2
    orders = (bits[:1] + bits[1:][::-1], bits)
    plane = g // 2 if cube else g
    part = (member % plane) * (g // plane) + member // plane

    def exchange(value, where):
        pairs = []
        for a in range(n):
            for b in range(nh):
                to = where(a, b)
                if to is not None:
                    pairs.append((a * nh + b, to[0] * nh + to[1]))
        return lax.ppermute(value, ("ctx", "head"), pairs)

    def spread(value, split, concat, size):
        groups = [[a * size + b for b in range(size)] for a in range(n // size)]
        return lax.all_to_all(
            value, "ctx", split, concat, axis_index_groups=groups, tiled=True
        )

    def over_groups(piece):
        pieces = [piece]
        step = 1
        while step < ng:
            pieces += [exchange(p, lambda a, b: (a ^ (step * g), b)) for p in pieces]
            step *= 2
        return pieces

    def over_planes(piece):
        odd = (c // plane) % 2 == 1
        same = jnp.where(odd, piece[1], piece[0])
        cross = jnp.where(odd, piece[0], piece[1])
        move = lambda x, r: exchange(x, lambda a, b: (a ^ (r * plane), b))
        return [same, move(cross, 1), move(same, 2), move(cross, 3)]

    def true_order(pieces, index):
        if len(pieces) == 1:
            return pieces
        half = len(pieces) // 2
        low, high = true_order(pieces[:half], index), true_order(pieces[half:], index)
        upper = (index & half) != 0
        return [jnp.where(upper, b, a) for a, b in zip(low, high)] + [
            jnp.where(upper, a, b) for a, b in zip(low, high)
        ]

    levels = g // plane
    spots = jnp.arange(rows)
    upto = (spots[:, None] <= spots[None, :]).astype(F32)
    cumul = jnp.dot(
        log_decay, upto, precision=lax.Precision.HIGHEST, preferred_element_type=F32
    ).reshape(plane, levels, heads * rows)
    if cube:
        odd = (c // plane) % 2 == 1
        keep = jnp.where(odd, cumul[:, 1], cumul[:, 0])
        give = jnp.where(odd, cumul[:, 0], cumul[:, 1])
        got = exchange(give, lambda a, b: (a ^ plane, b))
        both = jnp.concatenate(
            [keep.reshape(plane, heads, rows), got.reshape(plane, heads, rows)], axis=1
        ).reshape(g * heads, rows)
        cumul = spread(both, 0, 0, plane)
    else:
        cumul = cumul.transpose(1, 0, 2).reshape(g * heads, rows)
        cumul = spread(cumul, 0, 0, g)
    last = cumul[:, -1].reshape(g, heads)

    def entry(a, b):
        received = [bits[0]] + orders[b & 1][1:][::-1] if cube else orders[0][::-1]
        regular = bits if cube else received
        mask = lambda order, spot: sum(
            bit for i, bit in enumerate(order[::-1]) if spot >> i & 1
        )
        at = [mask(received, spot) ^ (a % g) for spot in range(g)]
        to = [mask(regular, spot) ^ (a % g) for spot in range(g)]
        where = [at.index(k) for k in range(g)] + [to.index(k) for k in range(g)]
        shift = (a // plane) % 2 if cube else 0
        decays = [(k % plane) * levels + (k // plane ^ shift) for k in range(g)]
        side = [b ^ (a // g), (a // plane) % 2]
        return [decays[k] for k in at] + where + decays + [decays.index(k) for k in range(g)] + side

    entries = jnp.array([entry(a, b) for a in range(n) for b in range(nh)], jnp.int32)
    table = lax.dynamic_index_in_dim(entries, c * nh + h, 0, False)
    decays_at, pos, turn = table[:g], table[g : 4 * g], table[5 * g :]
    ends = table[4 * g : 5 * g]
    after = jnp.sum(
        jnp.where((ends[:, None] < ends[None, :])[:, :, None], last[None], 0.0), axis=1
    )[:, None, :]
    tables = [jnp.concatenate([decays_at, turn]), turn, pos]
    gain = lax.dynamic_slice_in_dim(norm_gain, part * width, width)[None]

    share = model // nh
    own = lax.dynamic_slice_in_dim(tokens, h * share, share, axis=1)[None]
    step_to = lambda stage: (lambda a, b: (a ^ orders[b & 1][stage], b))
    if cube:
        axes = bits
        families = []
        for name, one in (("near", own), ("far", exchange(own, step_to(0)))):
            two = exchange(one, step_to(1))
            if name == "far":
                two, tables, gain = lax.optimization_barrier((two, tables, gain))
            pair = jnp.concatenate([one, two])
            families.append([pair, exchange(pair, step_to(2))])
        families = [f + [exchange(x, lambda a, b: (a, b ^ 1)) for x in f] for f in families]

        def rows_of(weight):
            moved = spread(weight, 1, 0, plane)
            return over_planes([moved[:, :width], moved[:, width:]])

        wk, wv, wq = rows_of(w_key), rows_of(w_value), rows_of(w_query)
        keys, values, states, total = keys_values(
            tables[0], *families, wk, wv, cumul, after, heads, head_dim
        )
        early = query_part(tables[1], *families, wq[:2], None)
        queries = query_part(tables[1], *families, wq[2:], early)
    else:
        axes = orders[0][::-1]
        for stage in range(len(bits)):
            got = exchange(own, lambda a, b: (a ^ orders[0][stage], b))
            own = jnp.concatenate([own, got], axis=0)
        shares = [own]
        step = 1
        while step < nh:
            shares += [exchange(s, lambda a, b: (a, b ^ step)) for s in shares]
            step *= 2
        full = jnp.concatenate(true_order(shares, h), axis=-1).reshape(g * rows, model)

        def project(weight, act):
            pieces = over_groups(spread(weight, 1, 0, g))
            whole = jnp.concatenate(true_order(pieces, group), axis=0)
            out = act(jnp.dot(full, whole, preferred_element_type=F32)).astype(BF16)
            return out.reshape(g, rows, width)

        keys, values = project(w_key, silu), project(w_value, lambda raw: raw)
        queries = project(w_query, silu)
        cum_t = cumul.reshape(g, heads, rows).transpose(0, 2, 1)
        states = block_states(decays_at, keys, values, cum_t, heads, head_dim)
        total = jnp.sum(jnp.exp(after[:, 0])[decays_at][:, :, None, None] * states, axis=0)

    keep = jnp.exp(jnp.sum(last, axis=0))
    later = lambda by: (lambda a, b: (a + by * g, b) if a + by * g < n else None)
    entering = exchange(total, later(1))
    step = 1
    if ng > 2:
        keep = exchange(keep, later(1))
    while step < ng - 1:
        entering = entering + keep[:, None, None] * exchange(entering, later(step))
        keep = keep * exchange(keep, later(step))
        step *= 2

    normed = mix(
        tables[2], queries, keys, values, cumul, states, entering, gain, heads, head_dim
    ).reshape(g * rows, width)
    sides = [normed] + [exchange(normed, lambda a, b: (a, b ^ p)) for p in range(1, nh)]

    out_cols = model // nh
    parts = 2 if cube else 1
    if cube:
        by_plane = spread(w_out, 0, 0, plane)
        by_plane = lax.optimization_barrier((by_plane, total))[0]
        by_plane = by_plane.reshape(plane, levels, width, -1)
        local = by_plane.transpose(1, 2, 0, 3).reshape(levels, width, -1)
        cut = local.shape[-1] // parts
        cuts = lax.optimization_barrier(
            [local[:, :, i * cut : (i + 1) * cut] for i in range(parts)]
        )
        swap = (c // plane) % 2 == 1
        mine = []
        for x in cuts:
            pieces = over_planes(x)
            mine.append([])
            for p in range(nh):
                side = h ^ p ^ group
                first = jnp.where(side == 0, pieces[0], pieces[2])
                second = jnp.where(side == 0, pieces[1], pieces[3])
                ordered = [jnp.where(swap, second, first), jnp.where(swap, first, second)]
                mine[-1].append(jnp.concatenate(ordered, axis=1))
    else:
        local = spread(w_out.reshape(g, width, -1), 0, 0, g)
        local = local.transpose(1, 0, 2).reshape(width, -1)
        whole = jnp.concatenate(true_order(over_groups(local), group), axis=1)
        whole = whole.reshape(width, nh, out_cols).transpose(1, 0, 2)
        mine = [[lax.dynamic_index_in_dim(whole, h ^ p, 0, False) for p in range(nh)]]

    done = []
    for columns in mine:
        right = columns[:1] + [
            exchange(m, lambda a, b: (a, b ^ (p + 1)))
            for p, m in enumerate(columns[1:])
        ]
        partial = sum(
            jnp.dot(t, w, preferred_element_type=F32) for t, w in zip(sides, right)
        ).astype(BF16)
        chunks = max(len(bits), 1)
        span = partial.shape[1] // chunks
        summed = []
        for j in range(chunks):
            piece = partial[:, j * span : (j + 1) * span].reshape((2,) * len(bits) + (rows, -1))
            left = list(axes)
            for stage, bit in enumerate(bits[j:] + bits[:j]):
                axis = left.index(bit)
                left.pop(axis)
                kept = lax.index_in_dim(piece, 0, axis, False)
                sent = lax.index_in_dim(piece, 1, axis, False)
                got = exchange(sent, lambda a, b: (a ^ bit, b))
                piece = (kept.astype(F32) + got.astype(F32)).astype(BF16)
            summed.append(piece)
        done.append(jnp.concatenate(summed, axis=1))
    if cube:
        done = [d[:, i * cut : (i + 1) * cut] for i in range(2) for d in done]
    return jnp.concatenate(done, axis=1)


def solution(mesh):
    placed = (
        P("ctx", None),
        P("ctx", "head"),
        P("ctx", "head"),
        P("ctx", "head"),
        P("head", "ctx"),
        P("head"),
        P("head", "ctx"),
    )
    body = functools.partial(per_device, n=mesh.shape["ctx"], nh=mesh.shape["head"])

    return jax.shard_map(
        body, mesh=mesh, in_specs=placed, out_specs=P("ctx", "head"), check_vma=False
    )
```

time: 298 us -> 330 us (1.11)
  waiting for transfers between devices: 108 us -> 150 us
  starting transfers between devices: 68.8 us -> 100 us
  other arithmetic: 33.8 us -> 11.8 us
  local copies, waits for them, and re-layouts: 32.1 us -> 22 us
  Pallas kernels: 49.6 us -> 39.6 us
    ppermute x33 -> x47, starting transfers between devices: 48 us -> 76.3 us  [exchange(): return lax.ppermute(value, ('ctx', 'head'), pairs)]
    ppermute x33 -> x47, waiting for transfers between devices: 92.9 us -> 120 us  [exchange(): return lax.ppermute(value, ('ctx', 'head'), pairs)]
    all_to_all x5, waiting for transfers between devices: 14.6 us -> 30.7 us  [spread(): lax.all_to_all(value, 'ctx', split, concat, axis_index_groups=groups, til...]
    another operation x9 -> x0, other arithmetic: 11.9 us -> none  [the longest x4 9.28 us: per_device(): stack = lambda pieces: jnp.stack(pieces)]
    select_n x4 -> x2, other arithmetic: 6.95 us -> 0.06 us  [over_planes(): same = jnp.where(odd, piece[1], piece[0])]
    reshape x5 -> x3, local copies, waits for them, and re-layouts: 7.91 us -> 2.01 us  [the longest x1 0.73 us: per_device(): cumul = jnp.dot(log_decay, upto, precision=lax.Precision.HIGHEST, preferr...]
    pallas_call x2, Pallas kernels: 21.7 us -> 16.7 us  [query_part(): pl.pallas_call(functools.partial(query_body, late=late), in_specs=[pl.Blo...]
    pallas_call x2 -> x1, Pallas kernels: 19 us -> 14.7 us  [keys_values(): pl.pallas_call(functools.partial(keys_values_body, heads=heads, head_dim=...]
  transfers between devices with their start and end apart: 38 -> 52, of which waited for: 14 -> 21; matrix products, arithmetic and copies ran while one was open for 21% -> 10% of each run, Pallas kernels for 17% -> 10%
where the time goes in v1:
time: 330 us; the launch traced here: 329 us
  waiting for transfers between devices  150 us (45%)
  starting transfers between devices  100 us (30%)
  Pallas kernels  39.6 us (12%)
  local copies, waits for them, and re-layouts  22 us (7%)
  other arithmetic  11.8 us (4%)
  matrix products  4.84 us (1%)
    ppermute x47, waiting for transfers between devices, exchange(): return lax.ppermute(value, ('ctx', 'head'), pairs)  120 us
    ppermute x47, starting transfers between devices, exchange(): return lax.ppermute(value, ('ctx', 'head'), pairs)  76.3 us
    all_to_all x5, waiting for transfers between devices, spread(): lax.all_to_all(value, 'ctx', split, concat, axis_index_groups=groups, til...  30.7 us
    all_to_all x5, starting transfers between devices, spread(): lax.all_to_all(value, 'ctx', split, concat, axis_index_groups=groups, til...  23.7 us
    pallas_call x2, Pallas kernels, query_part(): pl.pallas_call(functools.partial(query_body, late=late), in_specs=[pl.Blo...  16.7 us
    pallas_call x1, Pallas kernels, keys_values(): pl.pallas_call(functools.partial(keys_values_body, heads=heads, head_dim=...  14.7 us
    all_to_all x6, local copies, waits for them, and re-layouts, spread(): lax.all_to_all(value, 'ctx', split, concat, axis_index_groups=groups, til...  9.19 us
    pallas_call x1, Pallas kernels, mix(): pl.pallas_call(functools.partial(mix_body, heads=heads, head_dim=head_dim...  8.18 us
  transfers between devices with their start and end apart: 52, of which 21 were waited for; matrix products, arithmetic and copies ran while one was open for 10% of the time, Pallas kernels for 10%

profile of v1, /device:TPU:0, one launch (start us, length us, event | category | flops | bytes accessed | tf_op | source)
XLA Modules:
  0.0 329.1 jit_solution(9276657509720658250)
XLA Ops:
  0.0 1.4 copy-done
  1.5 3.1 collective-permute-start
  4.6 1.5 collective-permute-start.2
  7.5 14.8 %collective-permute-done = bf16[1,256,1536]{2,1,0:T(8,128)(2,1)} collective-permute-done((bf16[1,256,1536]{2,1,0:T(8,128)(2,1)S(1)}, bf16[1,256,1536]{2,1,0:T(8,128)(2,1)}, u32[]{:S(2)}, u32[]{:S(2)}) %collective-permute-start) | collective-permute-done | bytes 786464 | tf_op jit(solution)/shard_map/ppermute | solution.py:256
  22.2 1.7 collective-permute-start.1
  24.5 1.3 dynamic_slice.12
  26.5 1.6 collective-permute-start.3
  28.1 1.2 constant_dynamic-update-slice_fusion.1
  29.3 11.8 %collective-permute-done.1 = bf16[1,256,1536]{2,1,0:T(8,128)(2,1)} collective-permute-done((bf16[1,256,1536]{2,1,0:T(8,128)(2,1)}, bf16[1,256,1536]{2,1,0:T(8,128)(2,1)}, u32[]{:S(2)}, u32[]{:S(2)}) %collective-permute-start.1) | collective-permute-done | bytes 786464 | tf_op jit(solution)/shard_map/ppermute | solution.py:256
  41.1 1.2 constant_dynamic-update-slice_fusion.refs_4_
  42.3 2.8 collective-permute-start.6
  46.0 4.2 %all-to-all-start.1 = ((bf16[192,4,512]{2,0,1:T(8,128)(2,1)}), bf16[192,4,512]{2,0,1:T(8,128)(2,1)}, u32[]{:S(2)}, u32[]{:S(2)}) async-start(bf16[192,4,512]{2,0,1:T(8,128)(2,1)} %bitcast.207), calls=%async_computation.1 | async-start | bytes 1572864 | tf_op jit(solution)/shard_map/all_to_all | solution.py:260
  50.3 2.1 copy.118
  52.4 21.6 %all-to-all-done.1 = bf16[192,4,512]{2,0,1:T(8,128)(2,1)} async-done(((bf16[192,4,512]{2,0,1:T(8,128)(2,1)}), bf16[192,4,512]{2,0,1:T(8,128)(2,1)}, u32[]{:S(2)}, u32[]{:S(2)}) %all-to-all-start.1) | async-done | bytes 786464 | tf_op jit(solution)/shard_map/all_to_all | solution.py:260
  73.9 4.3 %all-to-all-start.2 = ((bf16[192,4,512]{2,0,1:T(8,128)(2,1)}), bf16[192,4,512]{2,0,1:T(8,128)(2,1)}, u32[]{:S(2)}, u32[]{:S(2)}) async-start(bf16[192,4,512]{2,0,1:T(8,128)(2,1)} %bitcast.206), calls=%async_computation.2 | async-start | bytes 1572864 | tf_op jit(solution)/shard_map/all_to_all | solution.py:260
  78.3 1.9 broadcast_select_fusion.2
  81.3 2.6 collective-permute-start.13
  86.5 12.7 %collective-permute-done.18 = f32[4,512]{1,0:T(4,128)S(1)} collective-permute-done((f32[4,512]{1,0:T(4,128)S(1)}, f32[4,512]{1,0:T(4,128)S(1)}, u32[]{:S(2)}, u32[]{:S(2)}) %collective-permute-start.18) | collective-permute-done | bytes 8224 | tf_op jit(solution)/shard_map/ppermute | solution.py:256
  99.1 2.4 collective-permute-start.14
  103.1 2.1 broadcast_select_fusion
  105.1 7.6 %collective-permute-done.14.refs_11_ = bf16[768,256]{1,0:T(8,128)(2,1)} collective-permute-done((bf16[768,256]{1,0:T(8,128)(2,1)}, bf16[768,256]{1,0:T(8,128)(2,1)}, u32[]{:S(2)}, u32[]{:S(2)}) %collective-permute-start.14) | collective-permute-done | bytes 393248 | tf_op jit(solution)/shard_map/ppermute | solution.py:256
  112.8 6.6 %collective-permute-start.15 = (bf16[768,256]{1,0:T(8,128)(2,1)}, bf16[768,256]{1,0:T(8,128)(2,1)}, u32[]{:S(2)}, u32[]{:S(2)}) collective-permute-start(bf16[768,256]{1,0:T(8,128)(2,1)} %get-tuple-element.51), channel_id=1, source_target_pairs={{0,8},{1,9},{2,10},{3,11},{4,12},{5,13},{6,14},{7,15},{8,0},{9,1},... | collective-permute-start | bytes 1179656 | tf_op jit(solution)/shard_map/ppermute | solution.py:256
  120.7 6.5 %all-to-all-start.3 = ((f32[4,4,256]{2,1,0:T(4,128)}), f32[4,4,256]{2,1,0:T(4,128)S(1)}, u32[]{:S(2)}, u32[]{:S(2)}) async-start(f32[4,4,256]{2,1,0:T(4,128)} %pad_maximum_fusion.3), calls=%async_computation.3 | async-start | bytes 32768 | tf_op jit(solution)/shard_map/all_to_all | solution.py:260
  127.2 2.1 copy.120
  129.3 2.6 all-to-all-done.3
  131.9 4.3 %all-to-all-start = ((bf16[192,4,512]{2,0,1:T(8,128)(2,1)}), bf16[192,4,512]{2,0,1:T(8,128)(2,1)}, u32[]{:S(2)}, u32[]{:S(2)}) async-start(bf16[192,4,512]{2,0,1:T(8,128)(2,1)} %bitcast.209), calls=%async_computation | async-start | bytes 1572864 | tf_op jit(solution)/shard_map/all_to_all | solution.py:260
  137.4 2.1 copy.117
  139.5 6.5 %all-to-all-done = bf16[192,4,512]{2,0,1:T(8,128)(2,1)} async-done(((bf16[192,4,512]{2,0,1:T(8,128)(2,1)}), bf16[192,4,512]{2,0,1:T(8,128)(2,1)}, u32[]{:S(2)}, u32[]{:S(2)}) %all-to-all-start) | async-done | bytes 786464 | tf_op jit(solution)/shard_map/all_to_all | solution.py:260
  145.9 4.3 %all-to-all-start.4 = ((bf16[4,512,192]{1,2,0:T(8,128)(2,1)}), bf16[4,512,192]{1,2,0:T(8,128)(2,1)}, u32[]{:S(2)}, u32[]{:S(2)}) async-start(bf16[4,512,192]{1,2,0:T(8,128)(2,1)} %bitcast.205), calls=%async_computation.4 | async-start | bytes 1572864 | tf_op jit(solution)/shard_map/all_to_all | solution.py:260
  150.3 4.7 %collective-permute-done.16.refs_14_ = bf16[768,256]{1,0:T(8,128)(2,1)} collective-permute-done((bf16[768,256]{1,0:T(8,128)(2,1)S(1)}, bf16[768,256]{1,0:T(8,128)(2,1)}, u32[]{:S(2)}, u32[]{:S(2)}) %collective-permute-start.16) | collective-permute-done | bytes 393248 | tf_op jit(solution)/shard_map/ppermute | solution.py:256
  155.0 2.4 collective-permute-start.17
  158.7 1.9 broadcast_select_fusion.4
  160.6 7.6 %collective-permute-done.17.refs_15_ = bf16[768,256]{1,0:T(8,128)(2,1)} collective-permute-done((bf16[768,256]{1,0:T(8,128)(2,1)}, bf16[768,256]{1,0:T(8,128)(2,1)}, u32[]{:S(2)}, u32[]{:S(2)}) %collective-permute-start.17) | collective-permute-done | bytes 393248 | tf_op jit(solution)/shard_map/ppermute | solution.py:256
  168.2 2.4 collective-permute-start.10
  170.6 12.6 %collective-permute-start.11 = (bf16[768,256]{1,0:T(8,128)(2,1)}, bf16[768,256]{1,0:T(8,128)(2,1)}, u32[]{:S(2)}, u32[]{:S(2)}) collective-permute-start(bf16[768,256]{1,0:T(8,128)(2,1)} %get-tuple-element.55), channel_id=1, source_target_pairs={{0,8},{1,9},{2,10},{3,11},{4,12},{5,13},{6,14},{7,15},{8,0},{9,1},... | collective-permute-start | bytes 1179656 | tf_op jit(solution)/shard_map/ppermute | solution.py:256
  185.9 1.2 copy.103
  187.2 14.7 %keys_values.1 = (bf16[8,256,256]{2,1,0:T(8,128)(2,1)}, bf16[8,256,256]{2,1,0:T(8,128)(2,1)}, f32[8,2,128,128]{3,2,1,0:T(8,128)}, f32[2,128,128]{2,1,0:T(8,128)}) custom-call(s32[10]{0:T(128)} %pad_add_fusion.table, bf16[2,256,1536]{2,1,0:T(8,128)(2,1)} %copy-done.2, bf16[2,256,1536]{2,1,0:T(8,128)(2,1)} %collective-permute-done.3.refs_1_, ...), custom_call_target="tpu_custom_call" | custom-call | tf_op jit(solution)/shard_map/keys_values/pallas_call | solution.py:126
  201.9 3.9 %collective-permute-start.19 = (f32[2,128,128]{2,1,0:T(8,128)}, f32[2,128,128]{2,1,0:T(8,128)S(1)}, u32[]{:S(2)}, u32[]{:S(2)}) collective-permute-start(f32[2,128,128]{2,1,0:T(8,128)} %get-tuple-element.24), channel_id=1, source_target_pairs={{0,16},{1,17},{2,18},{3,19},{4,20},{5,21},{6,22},{7,23},{8,24},{9,... | collective-permute-start | bytes 393224 | tf_op jit(solution)/shard_map/ppermute | solution.py:256
  206.6 8.1 %shard_map.82.refs_10_ = f32[8,256,256]{2,1,0:T(8,128)} custom-call(s32[2]{0:T(128)} %copy-done.16, bf16[2,256,1536]{2,1,0:T(8,128)(2,1)} %copy-done.2, bf16[2,256,1536]{2,1,0:T(8,128)(2,1)} %collective-permute-done.3.refs_1_, bf16[2,256,1536]{2,1,0:T(8,128)(2,1)} %collective-permute-done.4.refs_2_, bf16[2,256,1536]{2,1,0:T(8,128)(2,1)} %collective-permute-done.5.refs_3_, ...), custom_call_target="tpu_custom_call" | custom-call | tf_op jit(solution)/shard_map/pallas_call | solution.py:177
  215.5 8.6 %shard_map.83.q_ref = bf16[8,256,256]{2,1,0:T(8,128)(2,1)} custom-call(s32[2]{0:T(128)} %copy-done.16, bf16[2,256,1536]{2,1,0:T(8,128)(2,1)} %copy-done.2, bf16[2,256,1536]{2,1,0:T(8,128)(2,1)} %collective-permute-done.3.refs_1_, bf16[2,256,1536]{2,1,0:T(8,128)(2,1)} %collective-permute-done.4.refs_2_, bf16[2,256,1536]{2,1,0:T(8,128)(2,1)} %collective-permute-done.5.refs_3_, ...), custom_call_target="tpu_custom_call" | custom-call | tf_op jit(solution)/shard_map/pallas_call | solution.py:177
  224.8 8.2 %mix.1 = bf16[8,256,256]{2,1,0:T(8,128)(2,1)} custom-call(s32[24]{0:T(128)} %slice_bitcast_fusion.29.table, bf16[8,256,256]{2,1,0:T(8,128)(2,1)} %shard_map.83.q_ref, bf16[8,256,256]{2,1,0:T(8,128)(2,1)} %get-tuple-element.21.k_ref, bf16[8,256,256]{2,1,0:T(8,128)(2,1)} %get-tuple-element.22.v_ref, f32[16,256]{1,0:T(8,128)} %copy-done.10, ...), custom_call_target="tpu_custom_call" | custom-call | tf_op jit(solution)/shard_map/mix/pallas_call | solution.py:221
  233.9 2.6 collective-permute-start.33
  237.6 7.4 %collective-permute-done.31 = bf16[256,384]{0,1:T(8,128)(2,1)S(1)} collective-permute-done((bf16[256,384]{0,1:T(8,128)(2,1)S(1)}, bf16[256,384]{0,1:T(8,128)(2,1)S(1)}, u32[]{:S(2)}, u32[]{:S(2)}) %collective-permute-start.31) | collective-permute-done | bytes 196640 | tf_op jit(solution)/shard_map/ppermute | solution.py:256
  245.0 5.7 %collective-permute-start.22 = (bf16[256,384]{0,1:T(8,128)(2,1)S(1)}, bf16[256,384]{0,1:T(8,128)(2,1)S(1)}, u32[]{:S(2)}, u32[]{:S(2)}) collective-permute-start(bf16[256,384]{0,1:T(8,128)(2,1)S(1)} %get-tuple-element.57), channel_id=1, source_target_pairs={{0,16},{1,17},{2,18},{3,19},{4,20},{5,21},{6,22},{7,23},{8,24},{9,... | collective-permute-start | bytes 589832 | tf_op jit(solution)/shard_map/ppermute | solution.py:256
  250.7 12.6 %collective-permute-done.33 = bf16[256,384]{0,1:T(8,128)(2,1)S(1)} collective-permute-done((bf16[256,384]{0,1:T(8,128)(2,1)S(1)}, bf16[256,384]{0,1:T(8,128)(2,1)S(1)}, u32[]{:S(2)}, u32[]{:S(2)}) %collective-permute-start.33) | collective-permute-done | bytes 196640 | tf_op jit(solution)/shard_map/ppermute | solution.py:256
  263.5 7.5 %collective-permute-done.22 = bf16[256,384]{0,1:T(8,128)(2,1)S(1)} collective-permute-done((bf16[256,384]{0,1:T(8,128)(2,1)S(1)}, bf16[256,384]{0,1:T(8,128)(2,1)S(1)}, u32[]{:S(2)}, u32[]{:S(2)}) %collective-permute-start.22) | collective-permute-done | bytes 196640 | tf_op jit(solution)/shard_map/ppermute | solution.py:256
  273.6 1.7 collective-permute-start.44
  275.4 1.5 collective-permute-start.38
  280.5 7.9 %collective-permute-done.44 = bf16[2,2,256,256]{3,2,1,0:T(8,128)(2,1)S(1)} collective-permute-done((bf16[2,2,256,256]{3,2,1,0:T(8,128)(2,1)S(1)}, bf16[2,2,256,256]{3,2,1,0:T(8,128)(2,1)S(1)}, u32[]{:S(2)}, u32[]{:S(2)}) %collective-permute-start.44) | collective-permute-done | bytes 524320 | tf_op jit(solution)/shard_map/ppermute | solution.py:256
  288.6 1.6 collective-permute-done.38
  290.8 8.2 %collective-permute-done.41 = bf16[2,2,256,256]{3,2,1,0:T(8,128)(2,1)S(1)} collective-permute-done((bf16[2,2,256,256]{3,2,1,0:T(8,128)(2,1)S(1)}, bf16[2,2,256,256]{3,2,1,0:T(8,128)(2,1)S(1)}, u32[]{:S(2)}, u32[]{:S(2)}) %collective-permute-start.41) | collective-permute-done | bytes 524320 | tf_op jit(solution)/shard_map/ppermute | solution.py:256
  299.1 1.6 collective-permute-start.39
  301.8 4.8 %collective-permute-done.25 = bf16[2,2,256,256]{3,2,1,0:T(8,128)(2,1)S(1)} collective-permute-done((bf16[2,2,256,256]{3,2,1,0:T(8,128)(2,1)S(1)}, bf16[2,2,256,256]{3,2,1,0:T(8,128)(2,1)S(1)}, u32[]{:S(2)}, u32[]{:S(2)}) %collective-permute-start.25) | collective-permute-done | bytes 524320 | tf_op jit(solution)/shard_map/ppermute | solution.py:256
  306.5 1.6 collective-permute-start.36
  308.3 3.9 %collective-permute-done.45 = bf16[2,256,256]{2,1,0:T(8,128)(2,1)S(1)} collective-permute-done((bf16[2,256,256]{2,1,0:T(8,128)(2,1)S(1)}, bf16[2,256,256]{2,1,0:T(8,128)(2,1)S(1)}, u32[]{:S(2)}, u32[]{:S(2)}) %collective-permute-start.45) | collective-permute-done | bytes 262176 | tf_op jit(solution)/shard_map/ppermute | solution.py:256
  312.2 1.6 collective-permute-start.26
  314.4 1.6 collective-permute-done.42
  316.5 1.7 collective-permute-start.43
  318.2 1.8 collective-permute-start.30
  320.1 1.2 collective-permute-done.26
  321.3 1.6 collective-permute-start.37
  323.0 1.3 collective-permute-start.27
  324.6 1.7 collective-permute-done.37
  326.3 1.7 collective-permute-done.27
  (166 shorter events, 30.3 us)
Async XLA Ops:
  1.5 20.8 %collective-permute-start = (bf16[1,256,1536]{2,1,0:T(8,128)(2,1)S(1)}, bf16[1,256,1536]{2,1,0:T(8,128)(2,1)}, u32[]{:S(2)}, u32[]{:S(2)}) collective-permute-start(bf16[1,256,1536]{2,1,0:T(8,128)(2,1)S(1)} %dynamic-slice_bitcast_fusion), channel_id=1, source_target_pairs={{0,8},{1,9},{2,10},{3,11},{4,12},{5,13},{6,14},{7,15},{8,0},{9,1},... | collective-permute-start | bytes 2359304 | tf_op jit(solution)/shard_map/ppermute | solution.py:256
  4.6 21.8 %collective-permute-start.2 = (bf16[1,256,1536]{2,1,0:T(8,128)(2,1)S(1)}, bf16[1,256,1536]{2,1,0:T(8,128)(2,1)S(1)}, u32[]{:S(2)}, u32[]{:S(2)}) collective-permute-start(bf16[1,256,1536]{2,1,0:T(8,128)(2,1)S(1)} %dynamic-slice_bitcast_fusion), channel_id=1, source_target_pairs={{0,2},{1,5},{2,0},{3,7},{4,6},{5,1},{6,4},{7,3},{8,10},{9,13},{10,... | collective-permute-start | bytes 2359304 | tf_op jit(solution)/shard_map/ppermute | solution.py:256
  6.8 19.5 %copy-start.16 = (s32[2]{0:T(128)}, s32[2]{0:T(128)S(1)}, u32[]{:S(2)}) copy-start(s32[2]{0:T(128)S(1)} %slice_bitcast_fusion.30.table) | copy-start | bytes 28
  22.2 18.8 %collective-permute-start.1 = (bf16[1,256,1536]{2,1,0:T(8,128)(2,1)}, bf16[1,256,1536]{2,1,0:T(8,128)(2,1)}, u32[]{:S(2)}, u32[]{:S(2)}) collective-permute-start(bf16[1,256,1536]{2,1,0:T(8,128)(2,1)} %collective-permute-done), channel_id=1, source_target_pairs={{0,2},{1,5},{2,0},{3,7},{4,6},{5,1},{6,4},{7,3},{8,10},{9,13},{10,... | collective-permute-start | bytes 2359304 | tf_op jit(solution)/shard_map/ppermute | solution.py:256
  26.5 75.1 %copy-start.2 = (bf16[2,256,1536]{2,1,0:T(8,128)(2,1)}, bf16[2,256,1536]{2,1,0:T(8,128)(2,1)S(1)}, u32[]{:S(2)}) copy-start(bf16[2,256,1536]{2,1,0:T(8,128)(2,1)S(1)} %pad_maximum_fusion.refs_0_) | copy-start | bytes 4718596
  26.5 18.6 %copy-start.8 = (bf16[192,2048]{1,0:T(8,128)(2,1)S(1)}, bf16[192,2048]{1,0:T(8,128)(2,1)}, u32[]{:S(2)}) copy-start(bf16[192,2048]{1,0:T(8,128)(2,1)} %param.10) | copy-start | bytes 2359300
  26.5 76.0 %collective-permute-start.3 = (bf16[2,256,1536]{2,1,0:T(8,128)(2,1)S(1)}, bf16[2,256,1536]{2,1,0:T(8,128)(2,1)}, u32[]{:S(2)}, u32[]{:S(2)}) collective-permute-start(bf16[2,256,1536]{2,1,0:T(8,128)(2,1)S(1)} %pad_maximum_fusion.refs_0_), channel_id=1, source_target_pairs={{0,4},{1,3},{2,6},{3,1},{4,0},{5,7},{6,2},{7,5},{8,12},{9,11},{10,... | collective-permute-start | bytes 4718600 | tf_op jit(solution)/shard_map/ppermute | solution.py:256
  42.2 60.1 %copy-start.3 = (bf16[2,256,1536]{2,1,0:T(8,128)(2,1)}, bf16[2,256,1536]{2,1,0:T(8,128)(2,1)S(1)}, u32[]{:S(2)}) copy-start(bf16[2,256,1536]{2,1,0:T(8,128)(2,1)S(1)} %constant_dynamic-update-slice_fusion.refs_4_) | copy-start | bytes 4718596
  42.3 60.6 %collective-permute-start.6 = (bf16[2,256,1536]{2,1,0:T(8,128)(2,1)S(1)}, bf16[2,256,1536]{2,1,0:T(8,128)(2,1)}, u32[]{:S(2)}, u32[]{:S(2)}) collective-permute-start(bf16[2,256,1536]{2,1,0:T(8,128)(2,1)S(1)} %constant_dynamic-update-slice_fusion.refs_4_), channel_id=1, source_target_pairs={{0,4},{1,3},{2,6},{3,1},{4,0},{5,7},{6,2},{7,5},{8,12},{9,11},{10,... | collective-permute-start | bytes 4718600 | tf_op jit(solution)/shard_map/ppermute | solution.py:256
  46.0 27.9 %all-to-all-start.1 = ((bf16[192,4,512]{2,0,1:T(8,128)(2,1)}), bf16[192,4,512]{2,0,1:T(8,128)(2,1)}, u32[]{:S(2)}, u32[]{:S(2)}) async-start(bf16[192,4,512]{2,0,1:T(8,128)(2,1)} %bitcast.207), calls=%async_computation.1 | async-start | bytes 1572864 | tf_op jit(solution)/shard_map/all_to_all | solution.py:260
  73.9 9.9 %copy-start.17 = (f32[16,256]{1,0:T(8,128)S(1)}, f32[16,256]{1,0:T(8,128)}, u32[]{:S(2)}) copy-start(f32[16,256]{1,0:T(8,128)} %param.12) | copy-start | bytes 49156
  73.9 29.2 %all-to-all-start.2 = ((bf16[192,4,512]{2,0,1:T(8,128)(2,1)}), bf16[192,4,512]{2,0,1:T(8,128)(2,1)}, u32[]{:S(2)}, u32[]{:S(2)}) async-start(bf16[192,4,512]{2,0,1:T(8,128)(2,1)} %bitcast.206), calls=%async_computation.2 | async-start | bytes 1572864 | tf_op jit(solution)/shard_map/all_to_all | solution.py:260
  80.2 49.1 %copy-start.5 = (bf16[768,256]{1,0:T(8,128)(2,1)}, bf16[768,256]{1,0:T(8,128)(2,1)S(1)}, u32[]{:S(2)}) copy-start(bf16[768,256]{1,0:T(8,128)(2,1)S(1)} %get-tuple-element.54.refs_8_) | copy-start | bytes 1179652
  80.2 21.4 %collective-permute-start.12 = (bf16[768,256]{1,0:T(8,128)(2,1)}, bf16[768,256]{1,0:T(8,128)(2,1)}, u32[]{:S(2)}, u32[]{:S(2)}) collective-permute-start(bf16[768,256]{1,0:T(8,128)(2,1)} %get-tuple-element.53), channel_id=1, source_target_pairs={{0,8},{1,9},{2,10},{3,11},{4,12},{5,13},{6,14},{7,15},{8,0},{9,1},... | collective-permute-start | bytes 1179656 | tf_op jit(solution)/shard_map/ppermute | solution.py:256
  81.3 21.1 %collective-permute-start.13 = (bf16[768,256]{1,0:T(8,128)(2,1)S(1)}, bf16[768,256]{1,0:T(8,128)(2,1)}, u32[]{:S(2)}, u32[]{:S(2)}) collective-permute-start(bf16[768,256]{1,0:T(8,128)(2,1)S(1)} %get-tuple-element.54.refs_8_), channel_id=1, source_target_pairs={{0,16},{1,17},{2,18},{3,19},{4,20},{5,21},{6,22},{7,23},{8,24},{9,... | collective-permute-start | bytes 1179656 | tf_op jit(solution)/shard_map/ppermute | solution.py:256
  86.0 33.3 %copy-start.13 = (f32[4,512]{1,0:T(4,128)S(1)}, f32[4,512]{1,0:T(4,128)}, u32[]{:S(2)}) copy-start(f32[4,512]{1,0:T(4,128)} %get-tuple-element.61) | copy-start | bytes 24580
  86.0 13.1 %collective-permute-start.18 = (f32[4,512]{1,0:T(4,128)S(1)}, f32[4,512]{1,0:T(4,128)S(1)}, u32[]{:S(2)}, u32[]{:S(2)}) collective-permute-start(f32[4,512]{1,0:T(4,128)S(1)} %bitcast.222), channel_id=1, source_target_pairs={{0,8},{1,9},{2,10},{3,11},{4,12},{5,13},{6,14},{7,15},{8,0},{9,1},... | collective-permute-start | bytes 24584 | tf_op jit(solution)/shard_map/ppermute | solution.py:256
  99.1 13.6 %collective-permute-start.14 = (bf16[768,256]{1,0:T(8,128)(2,1)}, bf16[768,256]{1,0:T(8,128)(2,1)}, u32[]{:S(2)}, u32[]{:S(2)}) collective-permute-start(bf16[768,256]{1,0:T(8,128)(2,1)} %get-tuple-element.53), channel_id=1, source_target_pairs={{0,24},{1,25},{2,26},{3,27},{4,28},{5,29},{6,30},{7,31},{8,16},{9,... | collective-permute-start | bytes 1179656 | tf_op jit(solution)/shard_map/ppermute | solution.py:256
  101.6 69.0 %collective-permute-start.4 = (bf16[2,256,1536]{2,1,0:T(8,128)(2,1)S(1)}, bf16[2,256,1536]{2,1,0:T(8,128)(2,1)}, u32[]{:S(2)}, u32[]{:S(2)}) collective-permute-start(bf16[2,256,1536]{2,1,0:T(8,128)(2,1)S(1)} %pad_maximum_fusion.refs_0_), channel_id=1, source_target_pairs={{0,1},{1,0},{2,3},{3,2},{4,5},{5,4},{6,7},{7,6},{8,9},{9,8},{10,11... | collective-permute-start | bytes 4718600 | tf_op jit(solution)/shard_map/ppermute | solution.py:256
  102.4 80.8 %collective-permute-start.7 = (bf16[2,256,1536]{2,1,0:T(8,128)(2,1)S(1)}, bf16[2,256,1536]{2,1,0:T(8,128)(2,1)}, u32[]{:S(2)}, u32[]{:S(2)}) collective-permute-start(bf16[2,256,1536]{2,1,0:T(8,128)(2,1)S(1)} %constant_dynamic-update-slice_fusion.refs_4_), channel_id=1, source_target_pairs={{0,1},{1,0},{2,3},{3,2},{4,5},{5,4},{6,7},{7,6},{8,9},{9,8},{10,11... | collective-permute-start | bytes 4718600 | tf_op jit(solution)/shard_map/ppermute | solution.py:256
  102.6 84.6 %collective-permute-start.5 = (bf16[2,256,1536]{2,1,0:T(8,128)(2,1)}, bf16[2,256,1536]{2,1,0:T(8,128)(2,1)}, u32[]{:S(2)}, u32[]{:S(2)}) collective-permute-start(bf16[2,256,1536]{2,1,0:T(8,128)(2,1)} %collective-permute-done.3.refs_1_), channel_id=1, source_target_pairs={{0,1},{1,0},{2,3},{3,2},{4,5},{5,4},{6,7},{7,6},{8,9},{9,8},{10,11... | collective-permute-start | bytes 4718600 | tf_op jit(solution)/shard_map/ppermute | solution.py:256
  102.9 84.3 %collective-permute-start.8 = (bf16[2,256,1536]{2,1,0:T(8,128)(2,1)}, bf16[2,256,1536]{2,1,0:T(8,128)(2,1)}, u32[]{:S(2)}, u32[]{:S(2)}) collective-permute-start(bf16[2,256,1536]{2,1,0:T(8,128)(2,1)} %collective-permute-done.6.refs_5_), channel_id=1, source_target_pairs={{0,1},{1,0},{2,3},{3,2},{4,5},{5,4},{6,7},{7,6},{8,9},{9,8},{10,11... | collective-permute-start | bytes 4718600 | tf_op jit(solution)/shard_map/ppermute | solution.py:256
  112.8 23.4 %collective-permute-start.15 = (bf16[768,256]{1,0:T(8,128)(2,1)}, bf16[768,256]{1,0:T(8,128)(2,1)}, u32[]{:S(2)}, u32[]{:S(2)}) collective-permute-start(bf16[768,256]{1,0:T(8,128)(2,1)} %get-tuple-element.51), channel_id=1, source_target_pairs={{0,8},{1,9},{2,10},{3,11},{4,12},{5,13},{6,14},{7,15},{8,0},{9,1},... | collective-permute-start | bytes 1179656 | tf_op jit(solution)/shard_map/ppermute | solution.py:256
  120.7 11.2 %all-to-all-start.3 = ((f32[4,4,256]{2,1,0:T(4,128)}), f32[4,4,256]{2,1,0:T(4,128)S(1)}, u32[]{:S(2)}, u32[]{:S(2)}) async-start(f32[4,4,256]{2,1,0:T(4,128)} %pad_maximum_fusion.3), calls=%async_computation.3 | async-start | bytes 32768 | tf_op jit(solution)/shard_map/all_to_all | solution.py:260
  131.9 7.6 %copy-start.12 = (f32[4,4,256]{2,1,0:T(4,128)}, f32[4,4,256]{2,1,0:T(4,128)S(1)}, u32[]{:S(2)}) copy-start(f32[4,4,256]{2,1,0:T(4,128)S(1)} %all-to-all-done.3) | copy-start | bytes 49156
  131.9 14.1 %all-to-all-start = ((bf16[192,4,512]{2,0,1:T(8,128)(2,1)}), bf16[192,4,512]{2,0,1:T(8,128)(2,1)}, u32[]{:S(2)}, u32[]{:S(2)}) async-start(bf16[192,4,512]{2,0,1:T(8,128)(2,1)} %bitcast.209), calls=%async_computation | async-start | bytes 1572864 | tf_op jit(solution)/shard_map/all_to_all | solution.py:260
  136.2 18.8 %collective-permute-start.16 = (bf16[768,256]{1,0:T(8,128)(2,1)S(1)}, bf16[768,256]{1,0:T(8,128)(2,1)}, u32[]{:S(2)}, u32[]{:S(2)}) collective-permute-start(bf16[768,256]{1,0:T(8,128)(2,1)S(1)} %copy-done.6), channel_id=1, source_target_pairs={{0,16},{1,17},{2,18},{3,19},{4,20},{5,21},{6,22},{7,23},{8,24},{9,... | collective-permute-start | bytes 1179656 | tf_op jit(solution)/shard_map/ppermute | solution.py:256
  145.9 11.4 %copy-start.15 = (s32[8]{0:T(128)S(1)}, s32[8]{0:T(128)}, u32[]{:S(2)}) copy-start(s32[8]{0:T(128)} %get-tuple-element.63) | copy-start | bytes 100
  145.9 40.0 %all-to-all-start.4 = ((bf16[4,512,192]{1,2,0:T(8,128)(2,1)}), bf16[4,512,192]{1,2,0:T(8,128)(2,1)}, u32[]{:S(2)}, u32[]{:S(2)}) async-start(bf16[4,512,192]{1,2,0:T(8,128)(2,1)} %bitcast.205), calls=%async_computation.4 | async-start | bytes 1572864 | tf_op jit(solution)/shard_map/all_to_all | solution.py:260
  155.0 13.2 %collective-permute-start.17 = (bf16[768,256]{1,0:T(8,128)(2,1)}, bf16[768,256]{1,0:T(8,128)(2,1)}, u32[]{:S(2)}, u32[]{:S(2)}) collective-permute-start(bf16[768,256]{1,0:T(8,128)(2,1)} %get-tuple-element.51), channel_id=1, source_target_pairs={{0,24},{1,25},{2,26},{3,27},{4,28},{5,29},{6,30},{7,31},{8,16},{9,... | collective-permute-start | bytes 1179656 | tf_op jit(solution)/shard_map/ppermute | solution.py:256
  158.7 28.5 %copy-start.10 = (f32[16,256]{1,0:T(8,128)}, f32[16,256]{1,0:T(8,128)S(1)}, u32[]{:S(2)}) copy-start(f32[16,256]{1,0:T(8,128)S(1)} %all_to_all.68.refs_16_.cum_ref) | copy-start | bytes 49156
  160.6 41.3 %copy-start.7 = (bf16[768,256]{1,0:T(8,128)(2,1)}, bf16[768,256]{1,0:T(8,128)(2,1)S(1)}, u32[]{:S(2)}) copy-start(bf16[768,256]{1,0:T(8,128)(2,1)S(1)} %get-tuple-element.56.refs_8_) | copy-start | bytes 1179652
  168.2 46.5 %collective-permute-start.10 = (bf16[768,256]{1,0:T(8,128)(2,1)}, bf16[768,256]{1,0:T(8,128)(2,1)}, u32[]{:S(2)}, u32[]{:S(2)}) collective-permute-start(bf16[768,256]{1,0:T(8,128)(2,1)} %get-tuple-element.55), channel_id=1, source_target_pairs={{0,24},{1,25},{2,26},{3,27},{4,28},{5,29},{6,30},{7,31},{8,16},{9,... | collective-permute-start | bytes 1179656 | tf_op jit(solution)/shard_map/ppermute | solution.py:256
  170.6 36.0 %collective-permute-start.11 = (bf16[768,256]{1,0:T(8,128)(2,1)}, bf16[768,256]{1,0:T(8,128)(2,1)}, u32[]{:S(2)}, u32[]{:S(2)}) collective-permute-start(bf16[768,256]{1,0:T(8,128)(2,1)} %get-tuple-element.55), channel_id=1, source_target_pairs={{0,8},{1,9},{2,10},{3,11},{4,12},{5,13},{6,14},{7,15},{8,0},{9,1},... | collective-permute-start | bytes 1179656 | tf_op jit(solution)/shard_map/ppermute | solution.py:256
  183.2 31.6 %collective-permute-start.9 = (bf16[768,256]{1,0:T(8,128)(2,1)S(1)}, bf16[768,256]{1,0:T(8,128)(2,1)S(1)}, u32[]{:S(2)}, u32[]{:S(2)}) collective-permute-start(bf16[768,256]{1,0:T(8,128)(2,1)S(1)} %get-tuple-element.56.refs_8_), channel_id=1, source_target_pairs={{0,16},{1,17},{2,18},{3,19},{4,20},{5,21},{6,22},{7,23},{8,24},{9,... | collective-permute-start | bytes 1179656 | tf_op jit(solution)/shard_map/ppermute | solution.py:256
  201.9 22.2 %collective-permute-start.19 = (f32[2,128,128]{2,1,0:T(8,128)}, f32[2,128,128]{2,1,0:T(8,128)S(1)}, u32[]{:S(2)}, u32[]{:S(2)}) collective-permute-start(f32[2,128,128]{2,1,0:T(8,128)} %get-tuple-element.24), channel_id=1, source_target_pairs={{0,16},{1,17},{2,18},{3,19},{4,20},{5,21},{6,22},{7,23},{8,24},{9,... | collective-permute-start | bytes 393224 | tf_op jit(solution)/shard_map/ppermute | solution.py:256
  232.9 38.3 %collective-permute-start.23 = (bf16[2048,256]{1,0:T(8,128)(2,1)}, bf16[2048,256]{1,0:T(8,128)(2,1)S(1)}, u32[]{:S(2)}, u32[]{:S(2)}) collective-permute-start(bf16[2048,256]{1,0:T(8,128)(2,1)} %bitcast.196), channel_id=1, source_target_pairs={{0,1},{1,0},{2,3},{3,2},{4,5},{5,4},{6,7},{7,6},{8,9},{9,8},{10,11... | collective-permute-start | bytes 3145736 | tf_op jit(solution)/shard_map/ppermute | solution.py:256
  233.0 12.1 %collective-permute-start.31 = (bf16[256,384]{0,1:T(8,128)(2,1)S(1)}, bf16[256,384]{0,1:T(8,128)(2,1)S(1)}, u32[]{:S(2)}, u32[]{:S(2)}) collective-permute-start(bf16[256,384]{0,1:T(8,128)(2,1)S(1)} %get-tuple-element.60), channel_id=1, source_target_pairs={{0,8},{1,9},{2,10},{3,11},{4,12},{5,13},{6,14},{7,15},{8,0},{9,1},... | collective-permute-start | bytes 589832 | tf_op jit(solution)/shard_map/ppermute | solution.py:256
  233.1 11.9 %collective-permute-start.32 = (bf16[256,384]{0,1:T(8,128)(2,1)S(1)}, bf16[256,384]{0,1:T(8,128)(2,1)S(1)}, u32[]{:S(2)}, u32[]{:S(2)}) collective-permute-start(bf16[256,384]{0,1:T(8,128)(2,1)S(1)} %get-tuple-element.60), channel_id=1, source_target_pairs={{0,24},{1,25},{2,26},{3,27},{4,28},{5,29},{6,30},{7,31},{8,16},{9,... | collective-permute-start | bytes 589832 | tf_op jit(solution)/shard_map/ppermute | solution.py:256
  233.9 29.5 %collective-permute-start.33 = (bf16[256,384]{0,1:T(8,128)(2,1)S(1)}, bf16[256,384]{0,1:T(8,128)(2,1)S(1)}, u32[]{:S(2)}, u32[]{:S(2)}) collective-permute-start(bf16[256,384]{0,1:T(8,128)(2,1)S(1)} %get-tuple-element.59), channel_id=1, source_target_pairs={{0,16},{1,17},{2,18},{3,19},{4,20},{5,21},{6,22},{7,23},{8,24},{9,... | collective-permute-start | bytes 589832 | tf_op jit(solution)/shard_map/ppermute | solution.py:256
  236.6 27.0 %collective-permute-start.20 = (bf16[256,384]{0,1:T(8,128)(2,1)S(1)}, bf16[256,384]{0,1:T(8,128)(2,1)S(1)}, u32[]{:S(2)}, u32[]{:S(2)}) collective-permute-start(bf16[256,384]{0,1:T(8,128)(2,1)S(1)} %get-tuple-element.58), channel_id=1, source_target_pairs={{0,8},{1,9},{2,10},{3,11},{4,12},{5,13},{6,14},{7,15},{8,0},{9,1},... | collective-permute-start | bytes 589832 | tf_op jit(solution)/shard_map/ppermute | solution.py:256
  245.0 18.5 %collective-permute-start.21 = (bf16[256,384]{0,1:T(8,128)(2,1)S(1)}, bf16[256,384]{0,1:T(8,128)(2,1)S(1)}, u32[]{:S(2)}, u32[]{:S(2)}) collective-permute-start(bf16[256,384]{0,1:T(8,128)(2,1)S(1)} %get-tuple-element.58), channel_id=1, source_target_pairs={{0,24},{1,25},{2,26},{3,27},{4,28},{5,29},{6,30},{7,31},{8,16},{9,... | collective-permute-start | bytes 589832 | tf_op jit(solution)/shard_map/ppermute | solution.py:256
  245.0 26.0 %collective-permute-start.22 = (bf16[256,384]{0,1:T(8,128)(2,1)S(1)}, bf16[256,384]{0,1:T(8,128)(2,1)S(1)}, u32[]{:S(2)}, u32[]{:S(2)}) collective-permute-start(bf16[256,384]{0,1:T(8,128)(2,1)S(1)} %get-tuple-element.57), channel_id=1, source_target_pairs={{0,16},{1,17},{2,18},{3,19},{4,20},{5,21},{6,22},{7,23},{8,24},{9,... | collective-permute-start | bytes 589832 | tf_op jit(solution)/shard_map/ppermute | solution.py:256
  263.4 7.8 %collective-permute-start.34 = (bf16[256,768]{0,1:T(8,128)(2,1)S(1)}, bf16[256,768]{0,1:T(8,128)(2,1)S(1)}, u32[]{:S(2)}, u32[]{:S(2)}) collective-permute-start(bf16[256,768]{0,1:T(8,128)(2,1)S(1)} %pad_maximum_fusion.2), channel_id=1, source_target_pairs={{0,1},{1,0},{2,3},{3,2},{4,5},{5,4},{6,7},{7,6},{8,9},{9,8},{10,11... | collective-permute-start | bytes 1179656 | tf_op jit(solution)/shard_map/ppermute | solution.py:256
  271.1 5.8 %collective-permute-start.24 = (bf16[256,768]{0,1:T(8,128)(2,1)S(1)}, bf16[256,768]{0,1:T(8,128)(2,1)S(1)}, u32[]{:S(2)}, u32[]{:S(2)}) collective-permute-start(bf16[256,768]{0,1:T(8,128)(2,1)S(1)} %pad_maximum_fusion.1), channel_id=1, source_target_pairs={{0,1},{1,0},{2,3},{3,2},{4,5},{5,4},{6,7},{7,6},{8,9},{9,8},{10,11... | collective-permute-start | bytes 1179656 | tf_op jit(solution)/shard_map/ppermute | solution.py:256
  273.6 14.9 %collective-permute-start.44 = (bf16[2,2,256,256]{3,2,1,0:T(8,128)(2,1)S(1)}, bf16[2,2,256,256]{3,2,1,0:T(8,128)(2,1)S(1)}, u32[]{:S(2)}, u32[]{:S(2)}) collective-permute-start(bf16[2,2,256,256]{3,2,1,0:T(8,128)(2,1)S(1)} %slice_bitcast_fusion), channel_id=1, source_target_pairs={{0,2},{1,3},{2,0},{3,1},{4,6},{5,7},{6,4},{7,5},{8,10},{9,11},{10,... | collective-permute-start | bytes 1572872 | tf_op jit(solution)/shard_map/ppermute | solution.py:256
  275.4 14.9 %collective-permute-start.38 = (bf16[2,2,256,256]{3,2,0,1:T(8,128)(2,1)S(1)}, bf16[2,2,256,256]{3,2,0,1:T(8,128)(2,1)S(1)}, u32[]{:S(2)}, u32[]{:S(2)}) collective-permute-start(bf16[2,2,256,256]{3,2,0,1:T(8,128)(2,1)S(1)} %bitcast.218), channel_id=1, source_target_pairs={{0,4},{1,5},{2,6},{3,7},{4,0},{5,1},{6,2},{7,3},{8,12},{9,13},{10,... | collective-permute-start | bytes 1572872 | tf_op jit(solution)/shard_map/ppermute | solution.py:256
  279.2 19.9 %collective-permute-start.41 = (bf16[2,2,256,256]{3,2,1,0:T(8,128)(2,1)S(1)}, bf16[2,2,256,256]{3,2,1,0:T(8,128)(2,1)S(1)}, u32[]{:S(2)}, u32[]{:S(2)}) collective-permute-start(bf16[2,2,256,256]{3,2,1,0:T(8,128)(2,1)S(1)} %slice_bitcast_fusion.2), channel_id=1, source_target_pairs={{0,2},{1,3},{2,0},{3,1},{4,6},{5,7},{6,4},{7,5},{8,10},{9,11},{10,... | collective-permute-start | bytes 1572872 | tf_op jit(solution)/shard_map/ppermute | solution.py:256
  280.0 20.8 %collective-permute-start.28 = (bf16[2,2,256,256]{3,2,0,1:T(8,128)(2,1)S(1)}, bf16[2,2,256,256]{3,2,0,1:T(8,128)(2,1)S(1)}, u32[]{:S(2)}, u32[]{:S(2)}) collective-permute-start(bf16[2,2,256,256]{3,2,0,1:T(8,128)(2,1)S(1)} %bitcast.219), channel_id=1, source_target_pairs={{0,4},{1,5},{2,6},{3,7},{4,0},{5,1},{6,2},{7,3},{8,12},{9,13},{10,... | collective-permute-start | bytes 1572872 | tf_op jit(solution)/shard_map/ppermute | solution.py:256
  280.5 20.6 %collective-permute-start.35 = (bf16[2,2,256,256]{3,2,1,0:T(8,128)(2,1)S(1)}, bf16[2,2,256,256]{3,2,1,0:T(8,128)(2,1)S(1)}, u32[]{:S(2)}, u32[]{:S(2)}) collective-permute-start(bf16[2,2,256,256]{3,2,1,0:T(8,128)(2,1)S(1)} %bitcast.220), channel_id=1, source_target_pairs={{0,8},{1,9},{2,10},{3,11},{4,12},{5,13},{6,14},{7,15},{8,0},{9,1},... | collective-permute-start | bytes 1572872 | tf_op jit(solution)/shard_map/ppermute | solution.py:256
  288.4 18.1 %collective-permute-start.25 = (bf16[2,2,256,256]{3,2,1,0:T(8,128)(2,1)S(1)}, bf16[2,2,256,256]{3,2,1,0:T(8,128)(2,1)S(1)}, u32[]{:S(2)}, u32[]{:S(2)}) collective-permute-start(bf16[2,2,256,256]{3,2,1,0:T(8,128)(2,1)S(1)} %bitcast.221), channel_id=1, source_target_pairs={{0,8},{1,9},{2,10},{3,11},{4,12},{5,13},{6,14},{7,15},{8,0},{9,1},... | collective-permute-start | bytes 1572872 | tf_op jit(solution)/shard_map/ppermute | solution.py:256
  290.2 21.9 %collective-permute-start.45 = (bf16[2,256,256]{2,1,0:T(8,128)(2,1)S(1)}, bf16[2,256,256]{2,1,0:T(8,128)(2,1)S(1)}, u32[]{:S(2)}, u32[]{:S(2)}) collective-permute-start(bf16[2,256,256]{2,1,0:T(8,128)(2,1)S(1)} %slice_bitcast_fusion.4), channel_id=1, source_target_pairs={{0,8},{1,9},{2,10},{3,11},{4,12},{5,13},{6,14},{7,15},{8,0},{9,1},... | collective-permute-start | bytes 786440 | tf_op jit(solution)/shard_map/ppermute | solution.py:256
  299.1 14.8 %collective-permute-start.39 = (bf16[2,256,256]{2,1,0:T(8,128)(2,1)S(1)}, bf16[2,256,256]{2,1,0:T(8,128)(2,1)S(1)}, u32[]{:S(2)}, u32[]{:S(2)}) collective-permute-start(bf16[2,256,256]{2,1,0:T(8,128)(2,1)S(1)} %slice_bitcast_fusion.8), channel_id=1, source_target_pairs={{0,2},{1,3},{2,0},{3,1},{4,6},{5,7},{6,4},{7,5},{8,10},{9,11},{10,... | collective-permute-start | bytes 786440 | tf_op jit(solution)/shard_map/ppermute | solution.py:256
  300.9 15.2 %collective-permute-start.42 = (bf16[2,256,256]{2,1,0:T(8,128)(2,1)S(1)}, bf16[2,256,256]{2,1,0:T(8,128)(2,1)S(1)}, u32[]{:S(2)}, u32[]{:S(2)}) collective-permute-start(bf16[2,256,256]{2,1,0:T(8,128)(2,1)S(1)} %slice_bitcast_fusion.6), channel_id=1, source_target_pairs={{0,8},{1,9},{2,10},{3,11},{4,12},{5,13},{6,14},{7,15},{8,0},{9,1},... | collective-permute-start | bytes 786440 | tf_op jit(solution)/shard_map/ppermute | solution.py:256
  301.1 15.3 %collective-permute-start.29 = (bf16[2,256,256]{2,1,0:T(8,128)(2,1)S(1)}, bf16[2,256,256]{2,1,0:T(8,128)(2,1)S(1)}, u32[]{:S(2)}, u32[]{:S(2)}) collective-permute-start(bf16[2,256,256]{2,1,0:T(8,128)(2,1)S(1)} %slice_bitcast_fusion.12), channel_id=1, source_target_pairs={{0,2},{1,3},{2,0},{3,1},{4,6},{5,7},{6,4},{7,5},{8,10},{9,11},{10,... | collective-permute-start | bytes 786440 | tf_op jit(solution)/shard_map/ppermute | solution.py:256
  306.5 11.7 %collective-permute-start.36 = (bf16[2,256,256]{2,1,0:T(8,128)(2,1)S(1)}, bf16[2,256,256]{2,1,0:T(8,128)(2,1)S(1)}, u32[]{:S(2)}, u32[]{:S(2)}) collective-permute-start(bf16[2,256,256]{2,1,0:T(8,128)(2,1)S(1)} %slice_bitcast_fusion.10), channel_id=1, source_target_pairs={{0,4},{1,5},{2,6},{3,7},{4,0},{5,1},{6,2},{7,3},{8,12},{9,13},{10,... | collective-permute-start | bytes 786440 | tf_op jit(solution)/shard_map/ppermute | solution.py:256
  312.2 9.2 %collective-permute-start.26 = (bf16[2,256,256]{2,1,0:T(8,128)(2,1)S(1)}, bf16[2,256,256]{2,1,0:T(8,128)(2,1)S(1)}, u32[]{:S(2)}, u32[]{:S(2)}) collective-permute-start(bf16[2,256,256]{2,1,0:T(8,128)(2,1)S(1)} %slice_bitcast_fusion.14), channel_id=1, source_target_pairs={{0,4},{1,5},{2,6},{3,7},{4,0},{5,1},{6,2},{7,3},{8,12},{9,13},{10,... | collective-permute-start | bytes 786440 | tf_op jit(solution)/shard_map/ppermute | solution.py:256
  313.9 9.2 %collective-permute-start.46 = (bf16[256,256]{1,0:T(8,128)(2,1)S(1)}, bf16[256,256]{1,0:T(8,128)(2,1)S(1)}, u32[]{:S(2)}, u32[]{:S(2)}) collective-permute-start(bf16[256,256]{1,0:T(8,128)(2,1)S(1)} %slice_bitcast_fusion.16), channel_id=1, source_target_pairs={{0,4},{1,5},{2,6},{3,7},{4,0},{5,1},{6,2},{7,3},{8,12},{9,13},{10,... | collective-permute-start | bytes 393224 | tf_op jit(solution)/shard_map/ppermute | solution.py:256
  316.1 8.3 %collective-permute-start.40 = (bf16[256,256]{1,0:T(8,128)(2,1)S(1)}, bf16[256,256]{1,0:T(8,128)(2,1)S(1)}, u32[]{:S(2)}, u32[]{:S(2)}) collective-permute-start(bf16[256,256]{1,0:T(8,128)(2,1)S(1)} %slice_bitcast_fusion.20), channel_id=1, source_target_pairs={{0,8},{1,9},{2,10},{3,11},{4,12},{5,13},{6,14},{7,15},{8,0},{9,1},... | collective-permute-start | bytes 393224 | tf_op jit(solution)/shard_map/ppermute | solution.py:256
  316.5 8.0 %collective-permute-start.43 = (bf16[256,256]{1,0:T(8,128)(2,1)S(1)}, bf16[256,256]{1,0:T(8,128)(2,1)S(1)}, u32[]{:S(2)}, u32[]{:S(2)}) collective-permute-start(bf16[256,256]{1,0:T(8,128)(2,1)S(1)} %slice_bitcast_fusion.18), channel_id=1, source_target_pairs={{0,4},{1,5},{2,6},{3,7},{4,0},{5,1},{6,2},{7,3},{8,12},{9,13},{10,... | collective-permute-start | bytes 393224 | tf_op jit(solution)/shard_map/ppermute | solution.py:256
  318.2 6.3 %collective-permute-start.30 = (bf16[256,256]{1,0:T(8,128)(2,1)S(1)}, bf16[256,256]{1,0:T(8,128)(2,1)S(1)}, u32[]{:S(2)}, u32[]{:S(2)}) collective-permute-start(bf16[256,256]{1,0:T(8,128)(2,1)S(1)} %slice_bitcast_fusion.24), channel_id=1, source_target_pairs={{0,8},{1,9},{2,10},{3,11},{4,12},{5,13},{6,14},{7,15},{8,0},{9,1},... | collective-permute-start | bytes 393224 | tf_op jit(solution)/shard_map/ppermute | solution.py:256
  321.3 5.0 %collective-permute-start.37 = (bf16[256,256]{1,0:T(8,128)(2,1)S(1)}, bf16[256,256]{1,0:T(8,128)(2,1)S(1)}, u32[]{:S(2)}, u32[]{:S(2)}) collective-permute-start(bf16[256,256]{1,0:T(8,128)(2,1)S(1)} %slice_bitcast_fusion.22), channel_id=1, source_target_pairs={{0,2},{1,3},{2,0},{3,1},{4,6},{5,7},{6,4},{7,5},{8,10},{9,11},{10,... | collective-permute-start | bytes 393224 | tf_op jit(solution)/shard_map/ppermute | solution.py:256
  323.0 5.0 %collective-permute-start.27 = (bf16[256,256]{1,0:T(8,128)(2,1)S(1)}, bf16[256,256]{1,0:T(8,128)(2,1)S(1)}, u32[]{:S(2)}, u32[]{:S(2)}) collective-permute-start(bf16[256,256]{1,0:T(8,128)(2,1)S(1)} %slice_bitcast_fusion.26), channel_id=1, source_target_pairs={{0,2},{1,3},{2,0},{3,1},{4,6},{5,7},{6,4},{7,5},{8,10},{9,11},{10,... | collective-permute-start | bytes 393224 | tf_op jit(solution)/shard_map/ppermute | solution.py:256
  324.4 4.7 %copy-start.1 = (bf16[256,3072]{1,0:T(8,128)(2,1)S(1)}, bf16[256,3072]{1,0:T(8,128)(2,1)}, u32[]{:S(2)}) copy-start(bf16[256,3072]{1,0:T(8,128)(2,1)} %param.8) | copy-start | bytes 4718596
  (6 other events, 12.2 us)

commit v2 on v1

--- a/solution.py
+++ b/solution.py
@@ -76,24 +76,25 @@
 
 
 def keys_values_body(table, *refs, heads, head_dim):
-    tokens, weights = refs[:8], refs[8:16]
-    cum_ref, after_ref, k_ref, v_ref, state_ref, total_ref, w_ref, cum_t_ref = refs[16:]
+    tokens, weights, (first, second) = refs[:8], refs[8:16], refs[16:18]
+    cum_ref, k_ref, v_ref, state_ref, total_ref, early_ref, w_ref, cum_t_ref = refs[18:]
     stand_up(cum_ref, cum_t_ref)
-    rows, width = k_ref.shape[1:]
+    count, rows, width = k_ref.shape
     cut = weights[0].shape[0]
     mine, swap = table[8], table[9]
     for side in range(2):
         for i in range(2):
+            span = slice(i * cut, (i + 1) * cut)
             for r in range(4):
 
                 @pl.when(2 * (mine ^ side) + (swap ^ i) == r)
                 def _():
                     for j in range(2):
-                        w_ref[side, i * cut : (i + 1) * cut, j * width : (j + 1) * width] = (
-                            weights[4 * j + r][...]
-                        )
-
-    totals = [0.0] * heads
+                        w_ref[side, span, j * width : (j + 1) * width] = weights[4 * j + r][...]
+                    w_ref[side, span, 2 * width :] = (
+                        (first, second)[r][...] if r < 2 else jnp.zeros((cut, width), BF16)
+                    )
+
     for family in range(2):
         out = [
             jnp.dot(wide(x), w_ref[i // 2], preferred_element_type=F32)
@@ -104,45 +105,51 @@
             mate = [at for at in OTHER if at[2] == spot][0]
             raw = block(out[:2], OWN[spot]) + block(out[2:], mate)
             k = silu(raw[:, :width]).astype(BF16)
-            v = raw[:, width:].astype(BF16)
+            v = raw[:, width : 2 * width].astype(BF16)
             at = 4 * family + spot
             k_ref[at] = k
             v_ref[at] = v
+            early_ref[at] = raw[:, 2 * width :]
             b = table[at]
             for i, s in enumerate(block_state(k, v, cum_t_ref[b], heads, head_dim)):
                 state_ref[at, i] = s
-                totals[i] += jnp.exp(after_ref[b, :, i : i + 1]) * s
     for i in range(heads):
-        total_ref[i] = totals[i]
+        total = jnp.zeros(total_ref.shape[1:], F32)
+        for b in range(count):
+            at, order = table[10 + b], table[10 + 2 * count + b]
+            last = cum_t_ref[order, rows - 1 : rows, i : i + 1]
+            total = jnp.exp(last) * total + state_ref[at, i]
+        total_ref[i] = total
 
 
 def on_chip(count):
     return [pl.BlockSpec(memory_space=pltpu.VMEM) for _ in range(count)]
 
 
-def keys_values(table, near, far, wk, wv, cum, after, heads, head_dim):
+def keys_values(table, near, far, wk, wv, wq, cum, heads, head_dim):
     _, rows, _ = near[0].shape
     cut, width = wk[0].shape
     return pl.pallas_call(
         functools.partial(keys_values_body, heads=heads, head_dim=head_dim),
-        in_specs=[pl.BlockSpec(memory_space=pltpu.SMEM)] + on_chip(18),
-        out_specs=on_chip(4),
+        in_specs=[pl.BlockSpec(memory_space=pltpu.SMEM)] + on_chip(19),
+        out_specs=on_chip(5),
         out_shape=[
             jax.ShapeDtypeStruct((8, rows, width), BF16),
             jax.ShapeDtypeStruct((8, rows, width), BF16),
             jax.ShapeDtypeStruct((8, heads, head_dim, head_dim), F32),
             jax.ShapeDtypeStruct((heads, head_dim, head_dim), F32),
+            jax.ShapeDtypeStruct((8, rows, width), F32),
         ],
         scratch_shapes=[
-            pltpu.VMEM((2, 2 * cut, 2 * width), BF16),
+            pltpu.VMEM((2, 2 * cut, 3 * width), BF16),
             pltpu.VMEM((8, rows, heads), F32),
         ],
         name="keys_values",
-    )(table, *near, *far, *wk, *wv, cum, after)
-
-
-def query_body(table, *refs, late):
-    tokens, (first, second, *rest, out_ref, w_ref) = refs[:8], refs[8:]
+    )(table, *near, *far, *wk, *wv, *wq, cum)
+
+
+def query_body(table, *refs):
+    tokens, (first, second, early_ref, out_ref, w_ref) = refs[:8], refs[8:]
     rows = out_ref.shape[1]
     cut = first.shape[0]
     mine, swap = table[0], table[1]
@@ -155,7 +162,7 @@
 
     for side, spots in ((0, OWN), (1, OTHER)):
 
-        @pl.when((mine ^ side) == (1 if late else 0))
+        @pl.when((mine ^ side) == 1)
         def _():
             for family in range(2):
                 runs = tokens[4 * family + 2 * side : 4 * family + 2 * side + 2]
@@ -163,24 +170,20 @@
                 for run, index, spot in spots:
                     part = out[run][index * rows : (index + 1) * rows]
                     at = 4 * family + spot
-                    if late:
-                        out_ref[at] = silu(rest[0][at] + part).astype(BF16)
-                    else:
-                        out_ref[at] = part
-
-
-def query_part(table, near, far, weights, early):
+                    out_ref[at] = silu(early_ref[at] + part).astype(BF16)
+
+
+def late_queries(table, near, far, weights, early):
     _, rows, _ = near[0].shape
     cut, width = weights[0].shape
-    late = early is not None
-    args = [*near, *far, *weights] + ([early] if late else [])
     return pl.pallas_call(
-        functools.partial(query_body, late=late),
-        in_specs=[pl.BlockSpec(memory_space=pltpu.SMEM)] + on_chip(len(args)),
+        query_body,
+        in_specs=[pl.BlockSpec(memory_space=pltpu.SMEM)] + on_chip(11),
         out_specs=on_chip(1)[0],
-        out_shape=jax.ShapeDtypeStruct((8, rows, width), BF16 if late else F32),
+        out_shape=jax.ShapeDtypeStruct((8, rows, width), BF16),
         scratch_shapes=[pltpu.VMEM((2 * cut, width), BF16)],
-    )(table, *args)
+        name="late_q",
+    )(table, *near, *far, *weights, early)
 
 
 def mix_body(
@@ -192,7 +195,7 @@
         jnp.int32, (rows, rows), 1
     )
     stand_up(cum_ref, cum_t_ref)
-    carry = [group_ref[i] for i in range(heads)]
+    carry = [jnp.where(table[3 * count] > 0, group_ref[i], 0.0) for i in range(heads)]
     for b in range(count):
         at, to, order = table[b], table[count + b], table[2 * count + b]
         for i in range(heads):
@@ -323,11 +326,8 @@
     entries = jnp.array([entry(a, b) for a in range(n) for b in range(nh)], jnp.int32)
     table = lax.dynamic_index_in_dim(entries, c * nh + h, 0, False)
     decays_at, pos, turn = table[:g], table[g : 4 * g], table[5 * g :]
-    ends = table[4 * g : 5 * g]
-    after = jnp.sum(
-        jnp.where((ends[:, None] < ends[None, :])[:, :, None], last[None], 0.0), axis=1
-    )[:, None, :]
-    tables = [jnp.concatenate([decays_at, turn]), turn, pos]
+    tables = [jnp.concatenate([decays_at, turn, pos]), turn]
+    tables.append(jnp.concatenate([pos, jnp.stack([group]).astype(jnp.int32)]))
     gain = lax.dynamic_slice_in_dim(norm_gain, part * width, width)[None]
 
     share = model // nh
@@ -349,11 +349,10 @@
             return over_planes([moved[:, :width], moved[:, width:]])
 
         wk, wv, wq = rows_of(w_key), rows_of(w_value), rows_of(w_query)
-        keys, values, states, total = keys_values(
-            tables[0], *families, wk, wv, cumul, after, heads, head_dim
-        )
-        early = query_part(tables[1], *families, wq[:2], None)
-        queries = query_part(tables[1], *families, wq[2:], early)
+        keys, values, states, total, early = keys_values(
+            tables[0], *families, wk, wv, wq[:2], cumul, heads, head_dim
+        )
+        queries = late_queries(tables[1], *families, wq[2:], early)
     else:
         axes = orders[0][::-1]
         for stage in range(len(bits)):
@@ -376,11 +375,18 @@
         queries = project(w_query, silu)
         cum_t = cumul.reshape(g, heads, rows).transpose(0, 2, 1)
         states = block_states(decays_at, keys, values, cum_t, heads, head_dim)
-        total = jnp.sum(jnp.exp(after[:, 0])[decays_at][:, :, None, None] * states, axis=0)
+        ends = table[4 * g : 5 * g]
+        after = jnp.sum(
+            jnp.where((ends[:, None] < ends[None, :])[:, :, None], last[None], 0.0), axis=1
+        )
+        total = jnp.sum(jnp.exp(after)[decays_at][:, :, None, None] * states, axis=0)
 
     keep = jnp.exp(jnp.sum(last, axis=0))
     later = lambda by: (lambda a, b: (a + by * g, b) if a + by * g < n else None)
-    entering = exchange(total, later(1))
+    if ng == 2:
+        entering = exchange(total, lambda a, b: (a ^ g, b))
+    else:
+        entering = exchange(total, later(1))
     step = 1
     if ng > 2:
         keep = exchange(keep, later(1))

time: 330 us -> 298 us (0.903)
  waiting for transfers between devices: 150 us -> 126 us
  local copies, waits for them, and re-layouts: 22 us -> 18.6 us
    all_to_all x5, waiting for transfers between devices: 30.7 us -> 6.7 us  [spread(): lax.all_to_all(value, 'ctx', split, concat, axis_index_groups=groups, til...]
    pallas_call x2 -> x1, Pallas kernels: 16.7 us -> 8.81 us  [late_queries(): pl.pallas_call(query_body, in_specs=[pl.BlockSpec(memory_space=pltpu.SMEM...]
    pallas_call x1, Pallas kernels: 14.7 us -> 21.3 us  [keys_values(): pl.pallas_call(functools.partial(keys_values_body, heads=heads, head_dim=...]
  transfers between devices with their start and end apart: 52 -> 52, of which waited for: 21 -> 21; matrix products, arithmetic and copies ran while one was open for 10% -> 9% of each run, Pallas kernels for 10% -> 10%
where the time goes in v2:
time: 298 us; the launch traced here: 297 us
  waiting for transfers between devices  126 us (42%)
  starting transfers between devices  97.7 us (33%)
  Pallas kernels  38.3 us (13%)
  local copies, waits for them, and re-layouts  18.6 us (6%)
  other arithmetic  12.2 us (4%)
  matrix products  4.2 us (1%)
    ppermute x47, waiting for transfers between devices, exchange(): return lax.ppermute(value, ('ctx', 'head'), pairs)  119 us
    ppermute x47, starting transfers between devices, exchange(): return lax.ppermute(value, ('ctx', 'head'), pairs)  76.9 us
    pallas_call x1, Pallas kernels, keys_values(): pl.pallas_call(functools.partial(keys_values_body, heads=heads, head_dim=...  21.3 us
    all_to_all x5, starting transfers between devices, spread(): lax.all_to_all(value, 'ctx', split, concat, axis_index_groups=groups, til...  20.8 us
    pallas_call x1, Pallas kernels, late_queries(): pl.pallas_call(query_body, in_specs=[pl.BlockSpec(memory_space=pltpu.SMEM...  8.81 us
    pallas_call x1, Pallas kernels, mix(): pl.pallas_call(functools.partial(mix_body, heads=heads, head_dim=head_dim...  8.19 us
    all_to_all x6, local copies, waits for them, and re-layouts, spread(): lax.all_to_all(value, 'ctx', split, concat, axis_index_groups=groups, til...  7.9 us
    all_to_all x5, waiting for transfers between devices, spread(): lax.all_to_all(value, 'ctx', split, concat, axis_index_groups=groups, til...  6.7 us
  transfers between devices with their start and end apart: 52, of which 21 were waited for; matrix products, arithmetic and copies ran while one was open for 9% of the time, Pallas kernels for 10%

profile of v2, /device:TPU:0, one launch (start us, length us, event | category | flops | bytes accessed | tf_op | source)
XLA Modules:
  0.0 297.3 jit_solution(11477583734286577598)
XLA Ops:
  0.0 1.4 copy-done
  1.5 3.1 %collective-permute-start = (bf16[1,256,1536]{2,1,0:T(8,128)(2,1)S(1)}, bf16[1,256,1536]{2,1,0:T(8,128)(2,1)}, u32[]{:S(2)}, u32[]{:S(2)}) collective-permute-start(bf16[1,256,1536]{2,1,0:T(8,128)(2,1)S(1)} %dynamic-slice_bitcast_fusion), channel_id=1, source_target_pairs={{0,8},{1,9},{2,10},{3,11},{4,12},{5,13},{6,14},{7,15},{8,0},{9,1},... | collective-permute-start | bytes 2359304 | tf_op jit(solution)/shard_map/ppermute | solution.py:259
  4.6 1.5 collective-permute-start.2
  7.0 4.2 %all-to-all-start.1 = ((bf16[192,4,512]{2,0,1:T(8,128)(2,1)}), bf16[192,4,512]{2,0,1:T(8,128)(2,1)}, u32[]{:S(2)}, u32[]{:S(2)}) async-start(bf16[192,4,512]{2,0,1:T(8,128)(2,1)} %bitcast.189), calls=%async_computation.1 | async-start | bytes 1572864 | tf_op jit(solution)/shard_map/all_to_all | solution.py:263
  12.1 10.1 %collective-permute-done = bf16[1,256,1536]{2,1,0:T(8,128)(2,1)} collective-permute-done((bf16[1,256,1536]{2,1,0:T(8,128)(2,1)S(1)}, bf16[1,256,1536]{2,1,0:T(8,128)(2,1)}, u32[]{:S(2)}, u32[]{:S(2)}) %collective-permute-start) | collective-permute-done | bytes 786464 | tf_op jit(solution)/shard_map/ppermute | solution.py:259
  22.2 1.7 collective-permute-start.1
  23.9 1.3 dynamic_slice.12
  26.4 1.3 pad_maximum_fusion.refs_0_
  27.7 1.6 collective-permute-start.3
  29.3 1.2 constant_dynamic-update-slice_fusion.1
  30.5 9.5 %collective-permute-done.1 = bf16[1,256,1536]{2,1,0:T(8,128)(2,1)} collective-permute-done((bf16[1,256,1536]{2,1,0:T(8,128)(2,1)}, bf16[1,256,1536]{2,1,0:T(8,128)(2,1)}, u32[]{:S(2)}, u32[]{:S(2)}) %collective-permute-start.1) | collective-permute-done | bytes 786464 | tf_op jit(solution)/shard_map/ppermute | solution.py:259
  39.9 1.2 constant_dynamic-update-slice_fusion.refs_4_
  41.1 2.8 collective-permute-start.6
  44.9 4.2 %all-to-all-start.2 = ((bf16[192,4,512]{2,0,1:T(8,128)(2,1)}), bf16[192,4,512]{2,0,1:T(8,128)(2,1)}, u32[]{:S(2)}, u32[]{:S(2)}) async-start(bf16[192,4,512]{2,0,1:T(8,128)(2,1)} %bitcast.203), calls=%async_computation.2 | async-start | bytes 1572864 | tf_op jit(solution)/shard_map/all_to_all | solution.py:263
  49.3 1.9 broadcast_select_fusion.2
  51.2 1.7 collective-permute-start.11
  52.9 2.6 collective-permute-start.12
  56.6 11.9 %collective-permute-done.18 = f32[4,512]{1,0:T(4,128)} collective-permute-done((f32[4,512]{1,0:T(4,128)S(1)}, f32[4,512]{1,0:T(4,128)}, u32[]{:S(2)}, u32[]{:S(2)}) %collective-permute-start.18) | collective-permute-done | bytes 8224 | tf_op jit(solution)/shard_map/ppermute | solution.py:259
  68.5 1.3 collective-permute-start.13
  69.9 4.1 %all-to-all-done.2 = bf16[192,4,512]{2,0,1:T(8,128)(2,1)} async-done(((bf16[192,4,512]{2,0,1:T(8,128)(2,1)}), bf16[192,4,512]{2,0,1:T(8,128)(2,1)}, u32[]{:S(2)}, u32[]{:S(2)}) %all-to-all-start.2) | async-done | bytes 786464 | tf_op jit(solution)/shard_map/all_to_all | solution.py:263
  73.9 2.1 broadcast_select_fusion
  76.4 3.7 %collective-permute-start.4 = (bf16[2,256,1536]{2,1,0:T(8,128)(2,1)S(1)}, bf16[2,256,1536]{2,1,0:T(8,128)(2,1)}, u32[]{:S(2)}, u32[]{:S(2)}) collective-permute-start(bf16[2,256,1536]{2,1,0:T(8,128)(2,1)S(1)} %pad_maximum_fusion.refs_0_), channel_id=1, source_target_pairs={{0,1},{1,0},{2,3},{3,2},{4,5},{5,4},{6,7},{7,6},{8,9},{9,8},{10,11... | collective-permute-start | bytes 4718600 | tf_op jit(solution)/shard_map/ppermute | solution.py:259
  83.1 3.8 %all-to-all-start.3 = ((f32[4,4,256]{2,1,0:T(4,128)}), f32[4,4,256]{2,1,0:T(4,128)S(1)}, u32[]{:S(2)}, u32[]{:S(2)}) async-start(f32[4,4,256]{2,1,0:T(4,128)} %pad_maximum_fusion.3), calls=%async_computation.3 | async-start | bytes 32768 | tf_op jit(solution)/shard_map/all_to_all | solution.py:263
  87.0 2.1 copy.99
  89.1 2.6 all-to-all-done.3
  91.7 4.3 %all-to-all-start = ((bf16[192,4,512]{2,0,1:T(8,128)(2,1)}), bf16[192,4,512]{2,0,1:T(8,128)(2,1)}, u32[]{:S(2)}, u32[]{:S(2)}) async-start(bf16[192,4,512]{2,0,1:T(8,128)(2,1)} %bitcast.206), calls=%async_computation | async-start | bytes 1572864 | tf_op jit(solution)/shard_map/all_to_all | solution.py:263
  96.0 7.6 %collective-permute-start.15 = (bf16[768,256]{1,0:T(8,128)(2,1)S(1)}, bf16[768,256]{1,0:T(8,128)(2,1)S(1)}, u32[]{:S(2)}, u32[]{:S(2)}) collective-permute-start(bf16[768,256]{1,0:T(8,128)(2,1)S(1)} %copy-done.7), channel_id=1, source_target_pairs={{0,16},{1,17},{2,18},{3,19},{4,20},{5,21},{6,22},{7,23},{8,24},{9,... | collective-permute-start | bytes 1179656 | tf_op jit(solution)/shard_map/ppermute | solution.py:259
  103.6 16.7 %collective-permute-done.15.refs_14_ = bf16[768,256]{1,0:T(8,128)(2,1)S(1)} collective-permute-done((bf16[768,256]{1,0:T(8,128)(2,1)S(1)}, bf16[768,256]{1,0:T(8,128)(2,1)S(1)}, u32[]{:S(2)}, u32[]{:S(2)}) %collective-permute-start.15) | collective-permute-done | bytes 393248 | tf_op jit(solution)/shard_map/ppermute | solution.py:259
  121.1 1.4 collective-permute-start.16
  122.5 2.1 copy.96
  124.6 4.2 %all-to-all-start.4 = ((bf16[4,512,192]{1,2,0:T(8,128)(2,1)}), bf16[4,512,192]{1,2,0:T(8,128)(2,1)}, u32[]{:S(2)}, u32[]{:S(2)}) async-start(bf16[4,512,192]{1,2,0:T(8,128)(2,1)} %bitcast.204), calls=%async_computation.4 | async-start | bytes 1572864 | tf_op jit(solution)/shard_map/all_to_all | solution.py:263
  128.8 1.9 broadcast_select_fusion.4
  130.8 2.5 collective-permute-done.16.refs_15_
  133.2 4.9 %collective-permute-start.17 = (bf16[768,256]{1,0:T(8,128)(2,1)}, bf16[768,256]{1,0:T(8,128)(2,1)S(1)}, u32[]{:S(2)}, u32[]{:S(2)}) collective-permute-start(bf16[768,256]{1,0:T(8,128)(2,1)} %get-tuple-element.57), channel_id=1, source_target_pairs={{0,8},{1,9},{2,10},{3,11},{4,12},{5,13},{6,14},{7,15},{8,0},{9,1},... | collective-permute-start | bytes 1179656 | tf_op jit(solution)/shard_map/ppermute | solution.py:259
  138.1 7.3 %collective-permute-done.17.refs_17_ = bf16[768,256]{1,0:T(8,128)(2,1)S(1)} collective-permute-done((bf16[768,256]{1,0:T(8,128)(2,1)}, bf16[768,256]{1,0:T(8,128)(2,1)S(1)}, u32[]{:S(2)}, u32[]{:S(2)}) %collective-permute-start.17) | collective-permute-done | bytes 393248 | tf_op jit(solution)/shard_map/ppermute | solution.py:259
  145.4 3.0 %collective-permute-start.10 = (bf16[768,256]{1,0:T(8,128)(2,1)}, bf16[768,256]{1,0:T(8,128)(2,1)}, u32[]{:S(2)}, u32[]{:S(2)}) collective-permute-start(bf16[768,256]{1,0:T(8,128)(2,1)} %get-tuple-element.57), channel_id=1, source_target_pairs={{0,24},{1,25},{2,26},{3,27},{4,28},{5,29},{6,30},{7,31},{8,16},{9,... | collective-permute-start | bytes 1179656 | tf_op jit(solution)/shard_map/ppermute | solution.py:259
  148.4 1.6 collective-permute-start.9
  150.7 1.2 copy.82
  152.0 21.3 %keys_values.1 = (bf16[8,256,256]{2,1,0:T(8,128)(2,1)}, bf16[8,256,256]{2,1,0:T(8,128)(2,1)}, f32[8,2,128,128]{3,2,1,0:T(8,128)}, f32[2,128,128]{2,1,0:T(8,128)}, f32[8,256,256]{2,1,0:T(8,128)}) custom-call(s32[34]{0:T(128)} %pad_add_fusion.table, bf16[2,256,1536]{2,1,0:T(8,128)(2,1)} %copy-done.2, bf16[2,256,1536]{2,1,0:T(8,128)(2,1)} %collective-permute-done.3.refs_1_, ...), custom_call_target="tpu_custom_call" | custom-call | tf_op jit(solution)/shard_map/keys_values/pallas_call | solution.py:132
  173.3 1.3 collective-permute-start.19
  175.4 9.2 %collective-permute-done.9.refs_8_ = bf16[768,256]{1,0:T(8,128)(2,1)S(1)} collective-permute-done((bf16[768,256]{1,0:T(8,128)(2,1)S(1)}, bf16[768,256]{1,0:T(8,128)(2,1)S(1)}, u32[]{:S(2)}, u32[]{:S(2)}) %collective-permute-start.9) | collective-permute-done | bytes 393248 | tf_op jit(solution)/shard_map/ppermute | solution.py:259
  185.4 8.8 %late_q.1.q_ref = bf16[8,256,256]{2,1,0:T(8,128)(2,1)} custom-call(s32[2]{0:T(128)} %copy-done.16, bf16[2,256,1536]{2,1,0:T(8,128)(2,1)} %copy-done.2, bf16[2,256,1536]{2,1,0:T(8,128)(2,1)} %collective-permute-done.3.refs_1_, bf16[2,256,1536]{2,1,0:T(8,128)(2,1)} %collective-permute-done.4.refs_2_, bf16[2,256,1536]{2,1,0:T(8,128)(2,1)} %collective-permute-done.5.refs_3_, ...), custom_call_target="tpu_custom_call" | custom-call | tf_op jit(solution)/shard_map/late_q/pallas_call | solution.py:179
  194.8 8.2 %mix.1 = bf16[8,256,256]{2,1,0:T(8,128)(2,1)} custom-call(s32[25]{0:T(128)} %pad_add_fusion.1.table, bf16[8,256,256]{2,1,0:T(8,128)(2,1)} %late_q.1.q_ref, bf16[8,256,256]{2,1,0:T(8,128)(2,1)} %get-tuple-element.23.k_ref, bf16[8,256,256]{2,1,0:T(8,128)(2,1)} %get-tuple-element.24.v_ref, f32[16,256]{1,0:T(8,128)} %all_to_all.68.refs_18_.cum_ref, ...), custom_call_target="tpu_custom_call" | custom-call | tf_op jit(solution)/shard_map/mix/pallas_call | solution.py:224
  203.1 2.4 collective-permute-start.21
  207.7 3.2 %collective-permute-done.20 = bf16[256,384]{0,1:T(8,128)(2,1)S(1)} collective-permute-done((bf16[256,384]{0,1:T(8,128)(2,1)S(1)}, bf16[256,384]{0,1:T(8,128)(2,1)S(1)}, u32[]{:S(2)}, u32[]{:S(2)}) %collective-permute-start.20) | collective-permute-done | bytes 196640 | tf_op jit(solution)/shard_map/ppermute | solution.py:259
  210.9 6.5 %collective-permute-start.32 = (bf16[256,384]{0,1:T(8,128)(2,1)S(1)}, bf16[256,384]{0,1:T(8,128)(2,1)S(1)}, u32[]{:S(2)}, u32[]{:S(2)}) collective-permute-start(bf16[256,384]{0,1:T(8,128)(2,1)S(1)} %get-tuple-element.62), channel_id=1, source_target_pairs={{0,24},{1,25},{2,26},{3,27},{4,28},{5,29},{6,30},{7,31},{8,16},{9,... | collective-permute-start | bytes 589832 | tf_op jit(solution)/shard_map/ppermute | solution.py:259
  217.4 4.8 %collective-permute-start.33 = (bf16[256,384]{0,1:T(8,128)(2,1)S(1)}, bf16[256,384]{0,1:T(8,128)(2,1)S(1)}, u32[]{:S(2)}, u32[]{:S(2)}) collective-permute-start(bf16[256,384]{0,1:T(8,128)(2,1)S(1)} %get-tuple-element.61), channel_id=1, source_target_pairs={{0,16},{1,17},{2,18},{3,19},{4,20},{5,21},{6,22},{7,23},{8,24},{9,... | collective-permute-start | bytes 589832 | tf_op jit(solution)/shard_map/ppermute | solution.py:259
  222.2 11.2 %collective-permute-done.22 = bf16[256,384]{0,1:T(8,128)(2,1)S(1)} collective-permute-done((bf16[256,384]{0,1:T(8,128)(2,1)S(1)}, bf16[256,384]{0,1:T(8,128)(2,1)S(1)}, u32[]{:S(2)}, u32[]{:S(2)}) %collective-permute-start.22) | collective-permute-done | bytes 196640 | tf_op jit(solution)/shard_map/ppermute | solution.py:259
  233.6 7.5 %collective-permute-done.33 = bf16[256,384]{0,1:T(8,128)(2,1)S(1)} collective-permute-done((bf16[256,384]{0,1:T(8,128)(2,1)S(1)}, bf16[256,384]{0,1:T(8,128)(2,1)S(1)}, u32[]{:S(2)}, u32[]{:S(2)}) %collective-permute-start.33) | collective-permute-done | bytes 196640 | tf_op jit(solution)/shard_map/ppermute | solution.py:259
  246.0 2.0 collective-permute-start.35
  248.2 1.7 collective-permute-start.28
  249.9 1.5 collective-permute-start.41
  252.2 8.6 %collective-permute-done.25 = bf16[2,2,256,256]{3,2,1,0:T(8,128)(2,1)S(1)} collective-permute-done((bf16[2,2,256,256]{3,2,1,0:T(8,128)(2,1)S(1)}, bf16[2,2,256,256]{3,2,1,0:T(8,128)(2,1)S(1)}, u32[]{:S(2)}, u32[]{:S(2)}) %collective-permute-start.25) | collective-permute-done | bytes 524320 | tf_op jit(solution)/shard_map/ppermute | solution.py:259
  260.8 1.6 collective-permute-start.44
  262.6 8.9 %collective-permute-done.35 = bf16[2,2,256,256]{3,2,1,0:T(8,128)(2,1)S(1)} collective-permute-done((bf16[2,2,256,256]{3,2,1,0:T(8,128)(2,1)S(1)}, bf16[2,2,256,256]{3,2,1,0:T(8,128)(2,1)S(1)}, u32[]{:S(2)}, u32[]{:S(2)}) %collective-permute-start.35) | collective-permute-done | bytes 524320 | tf_op jit(solution)/shard_map/ppermute | solution.py:259
  271.5 1.6 collective-permute-start.26
  273.9 1.7 collective-permute-start.29
  276.9 3.7 %collective-permute-done.26 = bf16[2,256,256]{2,1,0:T(8,128)(2,1)S(1)} collective-permute-done((bf16[2,256,256]{2,1,0:T(8,128)(2,1)S(1)}, bf16[2,256,256]{2,1,0:T(8,128)(2,1)S(1)}, u32[]{:S(2)}, u32[]{:S(2)}) %collective-permute-start.26) | collective-permute-done | bytes 262176 | tf_op jit(solution)/shard_map/ppermute | solution.py:259
  281.0 3.8 %collective-permute-done.36 = bf16[2,256,256]{2,1,0:T(8,128)(2,1)S(1)} collective-permute-done((bf16[2,256,256]{2,1,0:T(8,128)(2,1)S(1)}, bf16[2,256,256]{2,1,0:T(8,128)(2,1)S(1)}, u32[]{:S(2)}, u32[]{:S(2)}) %collective-permute-start.36) | collective-permute-done | bytes 262176 | tf_op jit(solution)/shard_map/ppermute | solution.py:259
  284.9 1.6 collective-permute-start.27
  287.9 1.7 collective-permute-start.43
  289.6 1.5 collective-permute-start.40
  291.3 1.4 collective-permute-start.46
  294.7 1.6 collective-permute-done.46
  (160 shorter events, 27.6 us)
Async XLA Ops:
  0.0 6.1 %copy-start.9 = (bf16[192,2048]{1,0:T(8,128)(2,1)S(1)}, bf16[192,2048]{1,0:T(8,128)(2,1)}, u32[]{:S(2)}) copy-start(bf16[192,2048]{1,0:T(8,128)(2,1)} %param.10) | copy-start | bytes 2359300
  1.5 5.6 %copy-start.5 = (bf16[1,256,1536]{2,1,0:T(8,128)(2,1)}, bf16[1,256,1536]{2,1,0:T(8,128)(2,1)S(1)}, u32[]{:S(2)}) copy-start(bf16[1,256,1536]{2,1,0:T(8,128)(2,1)S(1)} %dynamic-slice_bitcast_fusion) | copy-start | bytes 2359300
  1.5 20.8 %collective-permute-start = (bf16[1,256,1536]{2,1,0:T(8,128)(2,1)S(1)}, bf16[1,256,1536]{2,1,0:T(8,128)(2,1)}, u32[]{:S(2)}, u32[]{:S(2)}) collective-permute-start(bf16[1,256,1536]{2,1,0:T(8,128)(2,1)S(1)} %dynamic-slice_bitcast_fusion), channel_id=1, source_target_pairs={{0,8},{1,9},{2,10},{3,11},{4,12},{5,13},{6,14},{7,15},{8,0},{9,1},... | collective-permute-start | bytes 2359304 | tf_op jit(solution)/shard_map/ppermute | solution.py:259
  4.6 21.8 %collective-permute-start.2 = (bf16[1,256,1536]{2,1,0:T(8,128)(2,1)S(1)}, bf16[1,256,1536]{2,1,0:T(8,128)(2,1)S(1)}, u32[]{:S(2)}, u32[]{:S(2)}) collective-permute-start(bf16[1,256,1536]{2,1,0:T(8,128)(2,1)S(1)} %dynamic-slice_bitcast_fusion), channel_id=1, source_target_pairs={{0,2},{1,5},{2,0},{3,7},{4,6},{5,1},{6,4},{7,3},{8,10},{9,13},{10,... | collective-permute-start | bytes 2359304 | tf_op jit(solution)/shard_map/ppermute | solution.py:259
  7.0 37.8 %all-to-all-start.1 = ((bf16[192,4,512]{2,0,1:T(8,128)(2,1)}), bf16[192,4,512]{2,0,1:T(8,128)(2,1)}, u32[]{:S(2)}, u32[]{:S(2)}) async-start(bf16[192,4,512]{2,0,1:T(8,128)(2,1)} %bitcast.189), calls=%async_computation.1 | async-start | bytes 1572864 | tf_op jit(solution)/shard_map/all_to_all | solution.py:263
  12.1 15.5 %copy-start.16 = (s32[2]{0:T(128)}, s32[2]{0:T(128)S(1)}, u32[]{:S(2)}) copy-start(s32[2]{0:T(128)S(1)} %slice_bitcast_fusion.29.table) | copy-start | bytes 28
  22.2 17.7 %collective-permute-start.1 = (bf16[1,256,1536]{2,1,0:T(8,128)(2,1)}, bf16[1,256,1536]{2,1,0:T(8,128)(2,1)}, u32[]{:S(2)}, u32[]{:S(2)}) collective-permute-start(bf16[1,256,1536]{2,1,0:T(8,128)(2,1)} %collective-permute-done), channel_id=1, source_target_pairs={{0,2},{1,5},{2,0},{3,7},{4,6},{5,1},{6,4},{7,3},{8,10},{9,13},{10,... | collective-permute-start | bytes 2359304 | tf_op jit(solution)/shard_map/ppermute | solution.py:259
  27.7 48.8 %copy-start.2 = (bf16[2,256,1536]{2,1,0:T(8,128)(2,1)}, bf16[2,256,1536]{2,1,0:T(8,128)(2,1)S(1)}, u32[]{:S(2)}) copy-start(bf16[2,256,1536]{2,1,0:T(8,128)(2,1)S(1)} %pad_maximum_fusion.refs_0_) | copy-start | bytes 4718596
  27.7 16.3 %copy-start.10 = (bf16[192,2048]{1,0:T(8,128)(2,1)S(1)}, bf16[192,2048]{1,0:T(8,128)(2,1)}, u32[]{:S(2)}) copy-start(bf16[192,2048]{1,0:T(8,128)(2,1)} %param.11) | copy-start | bytes 2359300
  27.7 53.5 %collective-permute-start.3 = (bf16[2,256,1536]{2,1,0:T(8,128)(2,1)S(1)}, bf16[2,256,1536]{2,1,0:T(8,128)(2,1)}, u32[]{:S(2)}, u32[]{:S(2)}) collective-permute-start(bf16[2,256,1536]{2,1,0:T(8,128)(2,1)S(1)} %pad_maximum_fusion.refs_0_), channel_id=1, source_target_pairs={{0,4},{1,3},{2,6},{3,1},{4,0},{5,7},{6,2},{7,5},{8,12},{9,11},{10,... | collective-permute-start | bytes 4718600 | tf_op jit(solution)/shard_map/ppermute | solution.py:259
  41.1 40.1 %copy-start.3 = (bf16[2,256,1536]{2,1,0:T(8,128)(2,1)}, bf16[2,256,1536]{2,1,0:T(8,128)(2,1)S(1)}, u32[]{:S(2)}) copy-start(bf16[2,256,1536]{2,1,0:T(8,128)(2,1)S(1)} %constant_dynamic-update-slice_fusion.refs_4_) | copy-start | bytes 4718596
  41.1 40.6 %collective-permute-start.6 = (bf16[2,256,1536]{2,1,0:T(8,128)(2,1)S(1)}, bf16[2,256,1536]{2,1,0:T(8,128)(2,1)}, u32[]{:S(2)}, u32[]{:S(2)}) collective-permute-start(bf16[2,256,1536]{2,1,0:T(8,128)(2,1)S(1)} %constant_dynamic-update-slice_fusion.refs_4_), channel_id=1, source_target_pairs={{0,4},{1,3},{2,6},{3,1},{4,0},{5,7},{6,2},{7,5},{8,12},{9,11},{10,... | collective-permute-start | bytes 4718600 | tf_op jit(solution)/shard_map/ppermute | solution.py:259
  43.9 5.2 %copy-start.17 = (f32[16,256]{1,0:T(8,128)S(1)}, f32[16,256]{1,0:T(8,128)}, u32[]{:S(2)}) copy-start(f32[16,256]{1,0:T(8,128)} %param.12) | copy-start | bytes 49156
  44.9 29.0 %all-to-all-start.2 = ((bf16[192,4,512]{2,0,1:T(8,128)(2,1)}), bf16[192,4,512]{2,0,1:T(8,128)(2,1)}, u32[]{:S(2)}, u32[]{:S(2)}) async-start(bf16[192,4,512]{2,0,1:T(8,128)(2,1)} %bitcast.203), calls=%async_computation.2 | async-start | bytes 1572864 | tf_op jit(solution)/shard_map/all_to_all | solution.py:263
  51.2 37.8 %copy-start.6 = (bf16[768,256]{1,0:T(8,128)(2,1)}, bf16[768,256]{1,0:T(8,128)(2,1)S(1)}, u32[]{:S(2)}) copy-start(bf16[768,256]{1,0:T(8,128)(2,1)S(1)} %get-tuple-element.56.refs_8_) | copy-start | bytes 1179652
  51.2 24.8 %collective-permute-start.11 = (bf16[768,256]{1,0:T(8,128)(2,1)}, bf16[768,256]{1,0:T(8,128)(2,1)}, u32[]{:S(2)}, u32[]{:S(2)}) collective-permute-start(bf16[768,256]{1,0:T(8,128)(2,1)} %get-tuple-element.55), channel_id=1, source_target_pairs={{0,8},{1,9},{2,10},{3,11},{4,12},{5,13},{6,14},{7,15},{8,0},{9,1},... | collective-permute-start | bytes 1179656 | tf_op jit(solution)/shard_map/ppermute | solution.py:259
  52.9 23.5 %collective-permute-start.12 = (bf16[768,256]{1,0:T(8,128)(2,1)S(1)}, bf16[768,256]{1,0:T(8,128)(2,1)}, u32[]{:S(2)}, u32[]{:S(2)}) collective-permute-start(bf16[768,256]{1,0:T(8,128)(2,1)S(1)} %get-tuple-element.56.refs_8_), channel_id=1, source_target_pairs={{0,16},{1,17},{2,18},{3,19},{4,20},{5,21},{6,22},{7,23},{8,24},{9,... | collective-permute-start | bytes 1179656 | tf_op jit(solution)/shard_map/ppermute | solution.py:259
  56.2 25.6 %copy-start.15 = (f32[4,512]{1,0:T(4,128)S(1)}, f32[4,512]{1,0:T(4,128)}, u32[]{:S(2)}) copy-start(f32[4,512]{1,0:T(4,128)} %get-tuple-element.63) | copy-start | bytes 24580
  56.2 12.4 %collective-permute-start.18 = (f32[4,512]{1,0:T(4,128)S(1)}, f32[4,512]{1,0:T(4,128)}, u32[]{:S(2)}, u32[]{:S(2)}) collective-permute-start(f32[4,512]{1,0:T(4,128)S(1)} %bitcast.219), channel_id=1, source_target_pairs={{0,8},{1,9},{2,10},{3,11},{4,12},{5,13},{6,14},{7,15},{8,0},{9,1},... | collective-permute-start | bytes 24584 | tf_op jit(solution)/shard_map/ppermute | solution.py:259
  68.5 12.7 %collective-permute-start.13 = (bf16[768,256]{1,0:T(8,128)(2,1)}, bf16[768,256]{1,0:T(8,128)(2,1)}, u32[]{:S(2)}, u32[]{:S(2)}) collective-permute-start(bf16[768,256]{1,0:T(8,128)(2,1)} %get-tuple-element.55), channel_id=1, source_target_pairs={{0,24},{1,25},{2,26},{3,27},{4,28},{5,29},{6,30},{7,31},{8,16},{9,... | collective-permute-start | bytes 1179656 | tf_op jit(solution)/shard_map/ppermute | solution.py:259
  76.0 20.0 %collective-permute-start.14 = (bf16[768,256]{1,0:T(8,128)(2,1)}, bf16[768,256]{1,0:T(8,128)(2,1)}, u32[]{:S(2)}, u32[]{:S(2)}) collective-permute-start(bf16[768,256]{1,0:T(8,128)(2,1)} %get-tuple-element.53), channel_id=1, source_target_pairs={{0,8},{1,9},{2,10},{3,11},{4,12},{5,13},{6,14},{7,15},{8,0},{9,1},... | collective-permute-start | bytes 1179656 | tf_op jit(solution)/shard_map/ppermute | solution.py:259
  76.4 72.0 %collective-permute-start.4 = (bf16[2,256,1536]{2,1,0:T(8,128)(2,1)S(1)}, bf16[2,256,1536]{2,1,0:T(8,128)(2,1)}, u32[]{:S(2)}, u32[]{:S(2)}) collective-permute-start(bf16[2,256,1536]{2,1,0:T(8,128)(2,1)S(1)} %pad_maximum_fusion.refs_0_), channel_id=1, source_target_pairs={{0,1},{1,0},{2,3},{3,2},{4,5},{5,4},{6,7},{7,6},{8,9},{9,8},{10,11... | collective-permute-start | bytes 4718600 | tf_op jit(solution)/shard_map/ppermute | solution.py:259
  81.2 70.7 %collective-permute-start.7 = (bf16[2,256,1536]{2,1,0:T(8,128)(2,1)S(1)}, bf16[2,256,1536]{2,1,0:T(8,128)(2,1)}, u32[]{:S(2)}, u32[]{:S(2)}) collective-permute-start(bf16[2,256,1536]{2,1,0:T(8,128)(2,1)S(1)} %constant_dynamic-update-slice_fusion.refs_4_), channel_id=1, source_target_pairs={{0,1},{1,0},{2,3},{3,2},{4,5},{5,4},{6,7},{7,6},{8,9},{9,8},{10,11... | collective-permute-start | bytes 4718600 | tf_op jit(solution)/shard_map/ppermute | solution.py:259
  81.2 70.7 %collective-permute-start.5 = (bf16[2,256,1536]{2,1,0:T(8,128)(2,1)}, bf16[2,256,1536]{2,1,0:T(8,128)(2,1)}, u32[]{:S(2)}, u32[]{:S(2)}) collective-permute-start(bf16[2,256,1536]{2,1,0:T(8,128)(2,1)} %collective-permute-done.3.refs_1_), channel_id=1, source_target_pairs={{0,1},{1,0},{2,3},{3,2},{4,5},{5,4},{6,7},{7,6},{8,9},{9,8},{10,11... | collective-permute-start | bytes 4718600 | tf_op jit(solution)/shard_map/ppermute | solution.py:259
  81.7 70.2 %collective-permute-start.8 = (bf16[2,256,1536]{2,1,0:T(8,128)(2,1)}, bf16[2,256,1536]{2,1,0:T(8,128)(2,1)}, u32[]{:S(2)}, u32[]{:S(2)}) collective-permute-start(bf16[2,256,1536]{2,1,0:T(8,128)(2,1)} %collective-permute-done.6.refs_5_), channel_id=1, source_target_pairs={{0,1},{1,0},{2,3},{3,2},{4,5},{5,4},{6,7},{7,6},{8,9},{9,8},{10,11... | collective-permute-start | bytes 4718600 | tf_op jit(solution)/shard_map/ppermute | solution.py:259
  83.1 8.6 %all-to-all-start.3 = ((f32[4,4,256]{2,1,0:T(4,128)}), f32[4,4,256]{2,1,0:T(4,128)S(1)}, u32[]{:S(2)}, u32[]{:S(2)}) async-start(f32[4,4,256]{2,1,0:T(4,128)} %pad_maximum_fusion.3), calls=%async_computation.3 | async-start | bytes 32768 | tf_op jit(solution)/shard_map/all_to_all | solution.py:263
  91.7 4.3 %copy-start.7 = (bf16[768,256]{1,0:T(8,128)(2,1)S(1)}, bf16[768,256]{1,0:T(8,128)(2,1)}, u32[]{:S(2)}) copy-start(bf16[768,256]{1,0:T(8,128)(2,1)} %get-tuple-element.54.refs_12_) | copy-start | bytes 1179652
  91.7 32.9 %all-to-all-start = ((bf16[192,4,512]{2,0,1:T(8,128)(2,1)}), bf16[192,4,512]{2,0,1:T(8,128)(2,1)}, u32[]{:S(2)}, u32[]{:S(2)}) async-start(bf16[192,4,512]{2,0,1:T(8,128)(2,1)} %bitcast.206), calls=%async_computation | async-start | bytes 1572864 | tf_op jit(solution)/shard_map/all_to_all | solution.py:263
  96.0 24.3 %collective-permute-start.15 = (bf16[768,256]{1,0:T(8,128)(2,1)S(1)}, bf16[768,256]{1,0:T(8,128)(2,1)S(1)}, u32[]{:S(2)}, u32[]{:S(2)}) collective-permute-start(bf16[768,256]{1,0:T(8,128)(2,1)S(1)} %copy-done.7), channel_id=1, source_target_pairs={{0,16},{1,17},{2,18},{3,19},{4,20},{5,21},{6,22},{7,23},{8,24},{9,... | collective-permute-start | bytes 1179656 | tf_op jit(solution)/shard_map/ppermute | solution.py:259
  121.1 12.1 %collective-permute-start.16 = (bf16[768,256]{1,0:T(8,128)(2,1)}, bf16[768,256]{1,0:T(8,128)(2,1)}, u32[]{:S(2)}, u32[]{:S(2)}) collective-permute-start(bf16[768,256]{1,0:T(8,128)(2,1)} %get-tuple-element.53), channel_id=1, source_target_pairs={{0,24},{1,25},{2,26},{3,27},{4,28},{5,29},{6,30},{7,31},{8,16},{9,... | collective-permute-start | bytes 1179656 | tf_op jit(solution)/shard_map/ppermute | solution.py:259
  124.6 26.1 %all-to-all-start.4 = ((bf16[4,512,192]{1,2,0:T(8,128)(2,1)}), bf16[4,512,192]{1,2,0:T(8,128)(2,1)}, u32[]{:S(2)}, u32[]{:S(2)}) async-start(bf16[4,512,192]{1,2,0:T(8,128)(2,1)} %bitcast.204), calls=%async_computation.4 | async-start | bytes 1572864 | tf_op jit(solution)/shard_map/all_to_all | solution.py:263
  130.8 21.2 %copy-start.8 = (bf16[768,256]{1,0:T(8,128)(2,1)}, bf16[768,256]{1,0:T(8,128)(2,1)S(1)}, u32[]{:S(2)}) copy-start(bf16[768,256]{1,0:T(8,128)(2,1)S(1)} %get-tuple-element.58.refs_16_) | copy-start | bytes 1179652
  133.2 12.2 %collective-permute-start.17 = (bf16[768,256]{1,0:T(8,128)(2,1)}, bf16[768,256]{1,0:T(8,128)(2,1)S(1)}, u32[]{:S(2)}, u32[]{:S(2)}) collective-permute-start(bf16[768,256]{1,0:T(8,128)(2,1)} %get-tuple-element.57), channel_id=1, source_target_pairs={{0,8},{1,9},{2,10},{3,11},{4,12},{5,13},{6,14},{7,15},{8,0},{9,1},... | collective-permute-start | bytes 1179656 | tf_op jit(solution)/shard_map/ppermute | solution.py:259
  145.4 30.0 %collective-permute-start.10 = (bf16[768,256]{1,0:T(8,128)(2,1)}, bf16[768,256]{1,0:T(8,128)(2,1)}, u32[]{:S(2)}, u32[]{:S(2)}) collective-permute-start(bf16[768,256]{1,0:T(8,128)(2,1)} %get-tuple-element.57), channel_id=1, source_target_pairs={{0,24},{1,25},{2,26},{3,27},{4,28},{5,29},{6,30},{7,31},{8,16},{9,... | collective-permute-start | bytes 1179656 | tf_op jit(solution)/shard_map/ppermute | solution.py:259
  148.4 36.2 %collective-permute-start.9 = (bf16[768,256]{1,0:T(8,128)(2,1)S(1)}, bf16[768,256]{1,0:T(8,128)(2,1)S(1)}, u32[]{:S(2)}, u32[]{:S(2)}) collective-permute-start(bf16[768,256]{1,0:T(8,128)(2,1)S(1)} %get-tuple-element.58.refs_16_), channel_id=1, source_target_pairs={{0,16},{1,17},{2,18},{3,19},{4,20},{5,21},{6,22},{7,23},{8,24},{9,... | collective-permute-start | bytes 1179656 | tf_op jit(solution)/shard_map/ppermute | solution.py:259
  173.3 20.9 %collective-permute-start.19 = (f32[2,128,128]{2,1,0:T(8,128)}, f32[2,128,128]{2,1,0:T(8,128)S(1)}, u32[]{:S(2)}, u32[]{:S(2)}) collective-permute-start(f32[2,128,128]{2,1,0:T(8,128)} %get-tuple-element.26), channel_id=1, source_target_pairs={{0,16},{1,17},{2,18},{3,19},{4,20},{5,21},{6,22},{7,23},{8,24},{9,... | collective-permute-start | bytes 393224 | tf_op jit(solution)/shard_map/ppermute | solution.py:259
  203.0 38.3 %collective-permute-start.23 = (bf16[2048,256]{1,0:T(8,128)(2,1)}, bf16[2048,256]{1,0:T(8,128)(2,1)S(1)}, u32[]{:S(2)}, u32[]{:S(2)}) collective-permute-start(bf16[2048,256]{1,0:T(8,128)(2,1)} %bitcast.194), channel_id=1, source_target_pairs={{0,1},{1,0},{2,3},{3,2},{4,5},{5,4},{6,7},{7,6},{8,9},{9,8},{10,11... | collective-permute-start | bytes 3145736 | tf_op jit(solution)/shard_map/ppermute | solution.py:259
  203.1 7.9 %collective-permute-start.20 = (bf16[256,384]{0,1:T(8,128)(2,1)S(1)}, bf16[256,384]{0,1:T(8,128)(2,1)S(1)}, u32[]{:S(2)}, u32[]{:S(2)}) collective-permute-start(bf16[256,384]{0,1:T(8,128)(2,1)S(1)} %get-tuple-element.60), channel_id=1, source_target_pairs={{0,8},{1,9},{2,10},{3,11},{4,12},{5,13},{6,14},{7,15},{8,0},{9,1},... | collective-permute-start | bytes 589832 | tf_op jit(solution)/shard_map/ppermute | solution.py:259
  203.1 14.3 %collective-permute-start.21 = (bf16[256,384]{0,1:T(8,128)(2,1)S(1)}, bf16[256,384]{0,1:T(8,128)(2,1)S(1)}, u32[]{:S(2)}, u32[]{:S(2)}) collective-permute-start(bf16[256,384]{0,1:T(8,128)(2,1)S(1)} %get-tuple-element.60), channel_id=1, source_target_pairs={{0,24},{1,25},{2,26},{3,27},{4,28},{5,29},{6,30},{7,31},{8,16},{9,... | collective-permute-start | bytes 589832 | tf_op jit(solution)/shard_map/ppermute | solution.py:259
  205.5 27.9 %collective-permute-start.22 = (bf16[256,384]{0,1:T(8,128)(2,1)S(1)}, bf16[256,384]{0,1:T(8,128)(2,1)S(1)}, u32[]{:S(2)}, u32[]{:S(2)}) collective-permute-start(bf16[256,384]{0,1:T(8,128)(2,1)S(1)} %get-tuple-element.59), channel_id=1, source_target_pairs={{0,16},{1,17},{2,18},{3,19},{4,20},{5,21},{6,22},{7,23},{8,24},{9,... | collective-permute-start | bytes 589832 | tf_op jit(solution)/shard_map/ppermute | solution.py:259
  206.6 27.0 %collective-permute-start.31 = (bf16[256,384]{0,1:T(8,128)(2,1)S(1)}, bf16[256,384]{0,1:T(8,128)(2,1)S(1)}, u32[]{:S(2)}, u32[]{:S(2)}) collective-permute-start(bf16[256,384]{0,1:T(8,128)(2,1)S(1)} %get-tuple-element.62), channel_id=1, source_target_pairs={{0,8},{1,9},{2,10},{3,11},{4,12},{5,13},{6,14},{7,15},{8,0},{9,1},... | collective-permute-start | bytes 589832 | tf_op jit(solution)/shard_map/ppermute | solution.py:259
  210.9 22.7 %collective-permute-start.32 = (bf16[256,384]{0,1:T(8,128)(2,1)S(1)}, bf16[256,384]{0,1:T(8,128)(2,1)S(1)}, u32[]{:S(2)}, u32[]{:S(2)}) collective-permute-start(bf16[256,384]{0,1:T(8,128)(2,1)S(1)} %get-tuple-element.62), channel_id=1, source_target_pairs={{0,24},{1,25},{2,26},{3,27},{4,28},{5,29},{6,30},{7,31},{8,16},{9,... | collective-permute-start | bytes 589832 | tf_op jit(solution)/shard_map/ppermute | solution.py:259
  217.4 23.7 %collective-permute-start.33 = (bf16[256,384]{0,1:T(8,128)(2,1)S(1)}, bf16[256,384]{0,1:T(8,128)(2,1)S(1)}, u32[]{:S(2)}, u32[]{:S(2)}) collective-permute-start(bf16[256,384]{0,1:T(8,128)(2,1)S(1)} %get-tuple-element.61), channel_id=1, source_target_pairs={{0,16},{1,17},{2,18},{3,19},{4,20},{5,21},{6,22},{7,23},{8,24},{9,... | collective-permute-start | bytes 589832 | tf_op jit(solution)/shard_map/ppermute | solution.py:259
  233.5 7.8 %collective-permute-start.24 = (bf16[256,768]{0,1:T(8,128)(2,1)S(1)}, bf16[256,768]{0,1:T(8,128)(2,1)S(1)}, u32[]{:S(2)}, u32[]{:S(2)}) collective-permute-start(bf16[256,768]{0,1:T(8,128)(2,1)S(1)} %pad_maximum_fusion.1), channel_id=1, source_target_pairs={{0,1},{1,0},{2,3},{3,2},{4,5},{5,4},{6,7},{7,6},{8,9},{9,8},{10,11... | collective-permute-start | bytes 1179656 | tf_op jit(solution)/shard_map/ppermute | solution.py:259
  241.2 2.5 collective-permute-start.34
  246.0 14.9 %collective-permute-start.25 = (bf16[2,2,256,256]{3,2,1,0:T(8,128)(2,1)S(1)}, bf16[2,2,256,256]{3,2,1,0:T(8,128)(2,1)S(1)}, u32[]{:S(2)}, u32[]{:S(2)}) collective-permute-start(bf16[2,2,256,256]{3,2,1,0:T(8,128)(2,1)S(1)} %bitcast.217), channel_id=1, source_target_pairs={{0,8},{1,9},{2,10},{3,11},{4,12},{5,13},{6,14},{7,15},{8,0},{9,1},... | collective-permute-start | bytes 1572872 | tf_op jit(solution)/shard_map/ppermute | solution.py:259
  246.0 25.4 %collective-permute-start.35 = (bf16[2,2,256,256]{3,2,1,0:T(8,128)(2,1)S(1)}, bf16[2,2,256,256]{3,2,1,0:T(8,128)(2,1)S(1)}, u32[]{:S(2)}, u32[]{:S(2)}) collective-permute-start(bf16[2,2,256,256]{3,2,1,0:T(8,128)(2,1)S(1)} %bitcast.218), channel_id=1, source_target_pairs={{0,8},{1,9},{2,10},{3,11},{4,12},{5,13},{6,14},{7,15},{8,0},{9,1},... | collective-permute-start | bytes 1572872 | tf_op jit(solution)/shard_map/ppermute | solution.py:259
  248.2 25.1 %collective-permute-start.28 = (bf16[2,2,256,256]{3,2,0,1:T(8,128)(2,1)S(1)}, bf16[2,2,256,256]{3,2,0,1:T(8,128)(2,1)S(1)}, u32[]{:S(2)}, u32[]{:S(2)}) collective-permute-start(bf16[2,2,256,256]{3,2,0,1:T(8,128)(2,1)S(1)} %bitcast.216), channel_id=1, source_target_pairs={{0,4},{1,5},{2,6},{3,7},{4,0},{5,1},{6,2},{7,3},{8,12},{9,13},{10,... | collective-permute-start | bytes 1572872 | tf_op jit(solution)/shard_map/ppermute | solution.py:259
  249.9 24.0 %collective-permute-start.41 = (bf16[2,2,256,256]{3,2,1,0:T(8,128)(2,1)S(1)}, bf16[2,2,256,256]{3,2,1,0:T(8,128)(2,1)S(1)}, u32[]{:S(2)}, u32[]{:S(2)}) collective-permute-start(bf16[2,2,256,256]{3,2,1,0:T(8,128)(2,1)S(1)} %slice_bitcast_fusion.2), channel_id=1, source_target_pairs={{0,2},{1,3},{2,0},{3,1},{4,6},{5,7},{6,4},{7,5},{8,10},{9,11},{10,... | collective-permute-start | bytes 1572872 | tf_op jit(solution)/shard_map/ppermute | solution.py:259
  251.5 24.2 %collective-permute-start.38 = (bf16[2,2,256,256]{3,2,0,1:T(8,128)(2,1)S(1)}, bf16[2,2,256,256]{3,2,0,1:T(8,128)(2,1)S(1)}, u32[]{:S(2)}, u32[]{:S(2)}) collective-permute-start(bf16[2,2,256,256]{3,2,0,1:T(8,128)(2,1)S(1)} %bitcast.215), channel_id=1, source_target_pairs={{0,4},{1,5},{2,6},{3,7},{4,0},{5,1},{6,2},{7,3},{8,12},{9,13},{10,... | collective-permute-start | bytes 1572872 | tf_op jit(solution)/shard_map/ppermute | solution.py:259
  260.8 15.5 %collective-permute-start.44 = (bf16[2,2,256,256]{3,2,1,0:T(8,128)(2,1)S(1)}, bf16[2,2,256,256]{3,2,1,0:T(8,128)(2,1)S(1)}, u32[]{:S(2)}, u32[]{:S(2)}) collective-permute-start(bf16[2,2,256,256]{3,2,1,0:T(8,128)(2,1)S(1)} %slice_bitcast_fusion), channel_id=1, source_target_pairs={{0,2},{1,3},{2,0},{3,1},{4,6},{5,7},{6,4},{7,5},{8,10},{9,11},{10,... | collective-permute-start | bytes 1572872 | tf_op jit(solution)/shard_map/ppermute | solution.py:259
  271.5 9.2 %collective-permute-start.26 = (bf16[2,256,256]{2,1,0:T(8,128)(2,1)S(1)}, bf16[2,256,256]{2,1,0:T(8,128)(2,1)S(1)}, u32[]{:S(2)}, u32[]{:S(2)}) collective-permute-start(bf16[2,256,256]{2,1,0:T(8,128)(2,1)S(1)} %slice_bitcast_fusion.14), channel_id=1, source_target_pairs={{0,4},{1,5},{2,6},{3,7},{4,0},{5,1},{6,2},{7,3},{8,12},{9,13},{10,... | collective-permute-start | bytes 786440 | tf_op jit(solution)/shard_map/ppermute | solution.py:259
  273.3 11.6 %collective-permute-start.36 = (bf16[2,256,256]{2,1,0:T(8,128)(2,1)S(1)}, bf16[2,256,256]{2,1,0:T(8,128)(2,1)S(1)}, u32[]{:S(2)}, u32[]{:S(2)}) collective-permute-start(bf16[2,256,256]{2,1,0:T(8,128)(2,1)S(1)} %slice_bitcast_fusion.10), channel_id=1, source_target_pairs={{0,4},{1,5},{2,6},{3,7},{4,0},{5,1},{6,2},{7,3},{8,12},{9,13},{10,... | collective-permute-start | bytes 786440 | tf_op jit(solution)/shard_map/ppermute | solution.py:259
  273.9 12.6 %collective-permute-start.29 = (bf16[2,256,256]{2,1,0:T(8,128)(2,1)S(1)}, bf16[2,256,256]{2,1,0:T(8,128)(2,1)S(1)}, u32[]{:S(2)}, u32[]{:S(2)}) collective-permute-start(bf16[2,256,256]{2,1,0:T(8,128)(2,1)S(1)} %slice_bitcast_fusion.12), channel_id=1, source_target_pairs={{0,2},{1,3},{2,0},{3,1},{4,6},{5,7},{6,4},{7,5},{8,10},{9,11},{10,... | collective-permute-start | bytes 786440 | tf_op jit(solution)/shard_map/ppermute | solution.py:259
  275.8 11.4 %collective-permute-start.42 = (bf16[2,256,256]{2,1,0:T(8,128)(2,1)S(1)}, bf16[2,256,256]{2,1,0:T(8,128)(2,1)S(1)}, u32[]{:S(2)}, u32[]{:S(2)}) collective-permute-start(bf16[2,256,256]{2,1,0:T(8,128)(2,1)S(1)} %slice_bitcast_fusion.6), channel_id=1, source_target_pairs={{0,8},{1,9},{2,10},{3,11},{4,12},{5,13},{6,14},{7,15},{8,0},{9,1},... | collective-permute-start | bytes 786440 | tf_op jit(solution)/shard_map/ppermute | solution.py:259
  276.3 11.6 %collective-permute-start.39 = (bf16[2,256,256]{2,1,0:T(8,128)(2,1)S(1)}, bf16[2,256,256]{2,1,0:T(8,128)(2,1)S(1)}, u32[]{:S(2)}, u32[]{:S(2)}) collective-permute-start(bf16[2,256,256]{2,1,0:T(8,128)(2,1)S(1)} %slice_bitcast_fusion.8), channel_id=1, source_target_pairs={{0,2},{1,3},{2,0},{3,1},{4,6},{5,7},{6,4},{7,5},{8,10},{9,11},{10,... | collective-permute-start | bytes 786440 | tf_op jit(solution)/shard_map/ppermute | solution.py:259
  280.7 9.0 %collective-permute-start.45 = (bf16[2,256,256]{2,1,0:T(8,128)(2,1)S(1)}, bf16[2,256,256]{2,1,0:T(8,128)(2,1)S(1)}, u32[]{:S(2)}, u32[]{:S(2)}) collective-permute-start(bf16[2,256,256]{2,1,0:T(8,128)(2,1)S(1)} %slice_bitcast_fusion.4), channel_id=1, source_target_pairs={{0,8},{1,9},{2,10},{3,11},{4,12},{5,13},{6,14},{7,15},{8,0},{9,1},... | collective-permute-start | bytes 786440 | tf_op jit(solution)/shard_map/ppermute | solution.py:259
  284.9 6.4 %collective-permute-start.27 = (bf16[256,256]{1,0:T(8,128)(2,1)S(1)}, bf16[256,256]{1,0:T(8,128)(2,1)S(1)}, u32[]{:S(2)}, u32[]{:S(2)}) collective-permute-start(bf16[256,256]{1,0:T(8,128)(2,1)S(1)} %slice_bitcast_fusion.26), channel_id=1, source_target_pairs={{0,2},{1,3},{2,0},{3,1},{4,6},{5,7},{6,4},{7,5},{8,10},{9,11},{10,... | collective-permute-start | bytes 393224 | tf_op jit(solution)/shard_map/ppermute | solution.py:259
  286.6 6.1 %collective-permute-start.37 = (bf16[256,256]{1,0:T(8,128)(2,1)S(1)}, bf16[256,256]{1,0:T(8,128)(2,1)S(1)}, u32[]{:S(2)}, u32[]{:S(2)}) collective-permute-start(bf16[256,256]{1,0:T(8,128)(2,1)S(1)} %slice_bitcast_fusion.22), channel_id=1, source_target_pairs={{0,2},{1,3},{2,0},{3,1},{4,6},{5,7},{6,4},{7,5},{8,10},{9,11},{10,... | collective-permute-start | bytes 393224 | tf_op jit(solution)/shard_map/ppermute | solution.py:259
  287.1 5.8 %collective-permute-start.30 = (bf16[256,256]{1,0:T(8,128)(2,1)S(1)}, bf16[256,256]{1,0:T(8,128)(2,1)S(1)}, u32[]{:S(2)}, u32[]{:S(2)}) collective-permute-start(bf16[256,256]{1,0:T(8,128)(2,1)S(1)} %slice_bitcast_fusion.24), channel_id=1, source_target_pairs={{0,8},{1,9},{2,10},{3,11},{4,12},{5,13},{6,14},{7,15},{8,0},{9,1},... | collective-permute-start | bytes 393224 | tf_op jit(solution)/shard_map/ppermute | solution.py:259
  287.9 6.2 %collective-permute-start.43 = (bf16[256,256]{1,0:T(8,128)(2,1)S(1)}, bf16[256,256]{1,0:T(8,128)(2,1)S(1)}, u32[]{:S(2)}, u32[]{:S(2)}) collective-permute-start(bf16[256,256]{1,0:T(8,128)(2,1)S(1)} %slice_bitcast_fusion.18), channel_id=1, source_target_pairs={{0,4},{1,5},{2,6},{3,7},{4,0},{5,1},{6,2},{7,3},{8,12},{9,13},{10,... | collective-permute-start | bytes 393224 | tf_op jit(solution)/shard_map/ppermute | solution.py:259
  289.6 5.0 %collective-permute-start.40 = (bf16[256,256]{1,0:T(8,128)(2,1)S(1)}, bf16[256,256]{1,0:T(8,128)(2,1)S(1)}, u32[]{:S(2)}, u32[]{:S(2)}) collective-permute-start(bf16[256,256]{1,0:T(8,128)(2,1)S(1)} %slice_bitcast_fusion.20), channel_id=1, source_target_pairs={{0,8},{1,9},{2,10},{3,11},{4,12},{5,13},{6,14},{7,15},{8,0},{9,1},... | collective-permute-start | bytes 393224 | tf_op jit(solution)/shard_map/ppermute | solution.py:259
  291.3 5.0 %collective-permute-start.46 = (bf16[256,256]{1,0:T(8,128)(2,1)S(1)}, bf16[256,256]{1,0:T(8,128)(2,1)S(1)}, u32[]{:S(2)}, u32[]{:S(2)}) collective-permute-start(bf16[256,256]{1,0:T(8,128)(2,1)S(1)} %slice_bitcast_fusion.16), channel_id=1, source_target_pairs={{0,4},{1,5},{2,6},{3,7},{4,0},{5,1},{6,2},{7,3},{8,12},{9,13},{10,... | collective-permute-start | bytes 393224 | tf_op jit(solution)/shard_map/ppermute | solution.py:259
  292.7 4.6 %copy-start.1 = (bf16[256,3072]{1,0:T(8,128)(2,1)S(1)}, bf16[256,3072]{1,0:T(8,128)(2,1)}, u32[]{:S(2)}) copy-start(bf16[256,3072]{1,0:T(8,128)(2,1)} %param.8) | copy-start | bytes 4718596
  (6 other events, 7.8 us)
